TPU v7x, 32 devices: a whole 2x2x4 slice. The times are simulated.
32 devices in a mesh: rows: 8 (over z, y), band: 4 (over x, core).
Axes of the slice: x: 2, y: 2, z: 4, core: 2. Of those that a mesh axis runs over, the one named last changes fastest.
Arguments:
- embedding: bfloat16 [1024, 512], P('rows'), may hold values from -6 to 6
- w_left: bfloat16 [512, 32], replicated, may hold values from -0.25 to 0.25
- w_right: bfloat16 [512, 32], replicated, may hold values from -0.25 to 0.25
- w_in: bfloat16 [32, 128], replicated, may hold values from -1 to 1
- w_out: bfloat16 [128, 32], replicated, may hold values from -0.5 to 0.5
- w_head: float32 [32], replicated, may hold values from -1 to 1
- dist_bias: float32 [32, 4], replicated, may hold values from -3 to 3
- offsets: int32 [8, 4], P('rows', 'band'), may hold values from 0 to 3, each once within a row
- valid_bins: int32 [1024], P('rows'), may hold values 0 or 1
- target: bfloat16 [8, 4, 128, 128], P('rows', 'band'), may hold values from -6 to 6
Outputs:
- predicted: bfloat16 [8, 4, 128, 128], P('rows', 'band')
- grad_embedding: bfloat16 [1024, 512], P('rows', 'band')
- grad_left: float32 [512, 32], replicated
- grad_right: float32 [512, 32], replicated
- grad_in: float32 [32, 128], replicated
- grad_out: float32 [128, 32], replicated
- grad_head: float32 [32], replicated
- grad_bias: float32 [32, 4], replicated
Inputs may be any that keep to these rules, and one draw needn't show every extreme that they name: `offsets`: each row tile's 4 entries are the numbers 0 to 3 in some order.
All inputs are finite; a program needn't handle non-finite values. No bound on the sum of `valid_bins` on one device may be relied on, other than what follows from the above.
Results may differ from a plain program's by a relative error of at most 0.0058.
Values may be sent and summed in bfloat16 or wider, within the bound.
No kernel may reach another device: no remote copies, remote signals or barrier semaphores. Data moves between devices by JAX's collectives and lax.ppermute only.
A program may use at most 64 MiB of HBM per device.

v0:
```python
import jax
import jax.numpy as jnp
from jax import lax
from jax.sharding import PartitionSpec as P

TILE = 128
NOFF = 4


def from_behind(value, axis, steps):
    count = lax.axis_size(axis)
    leading, last = (max(0, -steps), min(count, count - steps))
    return lax.ppermute(value, axis, [(source, source + steps) for source in range(leading, last)])


def gelu_pair(pre_act):
    return jax.nn.gelu(pre_act, approximate=True)


def block_terms(row_proj, col_proj, bias_col, row_flags, col_flags, goal_rows, w_in, w_out, w_head):
    channels = row_proj.shape[0]
    row_count = row_proj.shape[1]
    col_count = col_proj.shape[1]
    summed = (
        row_proj.astype(jnp.float32)[:, :, None]
        + col_proj.astype(jnp.float32)[:, None, :]
        + bias_col[:, None, None]
    )
    summed = summed.reshape(channels, row_count * col_count)
    pair_in = summed.astype(jnp.bfloat16)
    pre_act = lax.dot_general(
        w_in, pair_in, (((0,), (0,)), ((), ())), preferred_element_type=jnp.float32
    )
    activation = gelu_pair(pre_act).astype(jnp.bfloat16)
    update = summed + lax.dot_general(
        w_out, activation, (((0,), (0,)), ((), ())), preferred_element_type=jnp.float32
    )
    logits = jnp.dot(w_head, update, precision=lax.Precision.HIGHEST)
    weight_mask = (row_flags[:, None] * col_flags[None, :]).reshape(-1)
    residual = weight_mask * (logits - goal_rows.astype(jnp.float32).reshape(-1)) / (NOFF * TILE)
    grad_update = w_head[:, None] * residual[None, :]
    grad_low = grad_update.astype(jnp.bfloat16)
    head_term = jnp.dot(update, residual, precision=lax.Precision.HIGHEST)
    out_term = lax.dot_general(
        activation, grad_low, (((1,), (1,)), ((), ())), preferred_element_type=jnp.float32
    )
    grad_act = lax.dot_general(
        w_out, grad_low, (((1,), (0,)), ((), ())), preferred_element_type=jnp.float32
    )
    _, backward = jax.vjp(gelu_pair, pre_act)
    grad_pre = backward(grad_act)[0].astype(jnp.bfloat16)
    in_term = lax.dot_general(
        pair_in, grad_pre, (((1,), (1,)), ((), ())), preferred_element_type=jnp.float32
    )
    grad_pair = grad_update + lax.dot_general(
        w_in, grad_pre, (((1,), (0,)), ((), ())), preferred_element_type=jnp.float32
    )
    grad_cube = grad_pair.reshape(channels, row_count, col_count)
    return (
        logits.reshape(row_count, col_count),
        head_term,
        out_term,
        in_term,
        jnp.sum(grad_pair, axis=1),
        jnp.sum(grad_cube, axis=2),
        jnp.sum(grad_cube, axis=1),
    )


def tile_terms(row_proj, col_proj, bias_col, row_flags, col_flags, goal_tile, w_in, w_out, w_head):
    half_rows = row_proj.shape[1] // 2
    first = block_terms(
        row_proj[:, :half_rows],
        col_proj,
        bias_col,
        row_flags[:half_rows],
        col_flags,
        goal_tile[:half_rows],
        w_in,
        w_out,
        w_head,
    )
    second = block_terms(
        row_proj[:, half_rows:],
        col_proj,
        bias_col,
        row_flags[half_rows:],
        col_flags,
        goal_tile[half_rows:],
        w_in,
        w_out,
        w_head,
    )
    return (
        jnp.concatenate([first[0], second[0]], axis=0),
        first[1] + second[1],
        first[2] + second[2],
        first[3] + second[3],
        first[4] + second[4],
        jnp.concatenate([first[5], second[5]], axis=1),
        first[6] + second[6],
    )


def project(embedding, weight):
    return lax.dot_general(
        weight, embedding, (((0,), (1,)), ((), ())), preferred_element_type=jnp.float32
    ).astype(jnp.bfloat16)


def fetch_ahead(right_proj, flags_low, step_count):
    return from_behind((right_proj, flags_low), "rows", -step_count)


def return_behind(col_piece, step_count):
    return from_behind(col_piece, "rows", step_count)


def on_device(
    embedding, w_left, w_right, w_in, w_out, w_head, dist_bias, offsets, valid_bins, target
):
    bin_count = embedding.shape[0]
    tile_count = bin_count // TILE
    slot_count = offsets.shape[1]
    reach_count = (NOFF + tile_count - 2) // tile_count
    channels = w_left.shape[1]
    hidden = w_in.shape[1]
    left_proj = project(embedding, w_left)
    right_proj = project(embedding, w_right)
    flags_low = valid_bins.astype(jnp.bfloat16)
    proj_parts = [right_proj]
    flag_parts = [flags_low]
    for step_count in range(1, reach_count + 1):
        moved_proj, moved_flags = fetch_ahead(right_proj, flags_low, step_count)
        proj_parts.append(moved_proj)
        flag_parts.append(moved_flags)
    right_ext = jnp.concatenate(proj_parts, axis=1)
    flags_ext = jnp.concatenate(flag_parts, axis=0).astype(jnp.float32)
    extended = bin_count * (reach_count + 1)
    initial = (
        jnp.zeros((channels, bin_count), jnp.float32),
        jnp.zeros((channels, extended), jnp.float32),
        jnp.zeros((channels, hidden), jnp.float32),
        jnp.zeros((hidden, channels), jnp.float32),
        jnp.zeros((channels,), jnp.float32),
        jnp.zeros((channels, NOFF), jnp.float32),
    )

    def advance(totals, item_index):
        tile_row = item_index // slot_count
        slot_index = item_index % slot_count
        offset = offsets[tile_row, slot_index]
        one_hot = (jnp.arange(NOFF, dtype=jnp.int32) == offset).astype(jnp.float32)
        bias_col = jnp.sum(dist_bias * one_hot[None, :], axis=1)
        row_start = tile_row * TILE
        col_start = (tile_row + offset) * TILE
        col_proj = lax.dynamic_slice_in_dim(right_ext, col_start, TILE, 1)
        row_flags = lax.dynamic_slice_in_dim(flags_ext, row_start, TILE, 0)
        col_flags = lax.dynamic_slice_in_dim(flags_ext, col_start, TILE, 0)
        goal_tile = target[tile_row, slot_index]
        logits, head_term, out_term, in_term, bias_sum, row_sums, col_sums = tile_terms(
            left_proj, col_proj, bias_col, row_flags, col_flags, goal_tile, w_in, w_out, w_head
        )
        row_acc, col_acc, in_acc, out_acc, head_acc, bias_acc = totals
        row_acc = row_acc + row_sums
        col_acc = lax.dynamic_update_slice_in_dim(
            col_acc, lax.dynamic_slice_in_dim(col_acc, col_start, TILE, 1) + col_sums, col_start, 1
        )
        bias_acc = bias_acc + bias_sum[:, None] * one_hot[None, :]
        return (
            (
                row_acc,
                col_acc,
                in_acc + in_term,
                out_acc + out_term,
                head_acc + head_term,
                bias_acc,
            ),
            logits,
        )

    totals, logits = lax.scan(
        advance, initial, jnp.arange(tile_count * slot_count, dtype=jnp.int32)
    )
    row_acc, col_acc, in_part, out_part, head_part, bias_part = totals
    predicted = logits.reshape(tile_count, slot_count, TILE, TILE).astype(jnp.bfloat16)
    col_own = col_acc[:, :bin_count]
    for step_count in range(1, reach_count + 1):
        col_piece = col_acc[:, step_count * bin_count : (step_count + 1) * bin_count]
        col_own = col_own + return_behind(col_piece, step_count)
    row_total, col_total = lax.psum((row_acc, col_own), "band")
    row_grad = row_total.astype(jnp.bfloat16)
    col_grad = col_total.astype(jnp.bfloat16)
    grad_in, grad_out, grad_head, grad_bias = lax.psum(
        (in_part, out_part, head_part, bias_part), ("rows", "band")
    )
    share = embedding.shape[1] // lax.axis_size("band")
    share_start = lax.axis_index("band") * share
    left_share = lax.dynamic_slice_in_dim(w_left, share_start, share, 0)
    right_share = lax.dynamic_slice_in_dim(w_right, share_start, share, 0)
    grad_embedding = (
        lax.dot_general(
            row_grad, left_share, (((0,), (1,)), ((), ())), preferred_element_type=jnp.float32
        )
        + lax.dot_general(
            col_grad, right_share, (((0,), (1,)), ((), ())), preferred_element_type=jnp.float32
        )
    ).astype(jnp.bfloat16)
    embed_share = lax.dynamic_slice_in_dim(embedding, share_start, share, 1)
    left_part = lax.dot_general(
        embed_share, row_grad, (((0,), (1,)), ((), ())), preferred_element_type=jnp.float32
    )
    right_part = lax.dot_general(
        embed_share, col_grad, (((0,), (1,)), ((), ())), preferred_element_type=jnp.float32
    )
    left_sum, right_sum = lax.psum((left_part, right_part), "rows")
    grad_left, grad_right = (
        lax.all_gather(left_sum, "band", axis=0, tiled=True),
        lax.all_gather(right_sum, "band", axis=0, tiled=True),
    )
    return (
        predicted,
        grad_embedding,
        grad_left,
        grad_right,
        grad_in,
        grad_out,
        grad_head,
        grad_bias,
    )


def solution(mesh):
    placed = (
        P("rows", None),
        P(),
        P(),
        P(),
        P(),
        P(),
        P(),
        P("rows", "band"),
        P("rows"),
        P("rows", "band", None, None),
    )
    return jax.shard_map(
        on_device,
        mesh=mesh,
        in_specs=placed,
        out_specs=(P("rows", "band", None, None), P("rows", "band"), P(), P(), P(), P(), P(), P()),
        check_vma=False,
    )
```

profile of v0, /device:TPU:0, one launch (start us, length us, event | category | flops | bytes accessed | tf_op | source)
XLA Modules:
  0.0 160.9 jit_solution(8311720177533387643)
XLA Ops:
  2.4 1.3 collective-permute-start
  3.7 1.3 collective-permute-start.1
  5.7 1.3 collective-permute-start.3
  7.0 1.3 collective-permute-start.4
  8.3 1.3 collective-permute-start.5
  12.8 1.3 collective-permute-start.2
  14.1 2.7 %collective-permute-done.4 = bf16[128]{0:T(256)(128)(2,1)S(1)} collective-permute-done((bf16[128]{0:T(256)(128)(2,1)S(1)}, bf16[128]{0:T(256)(128)(2,1)S(1)}, u32[]{:S(2)}, u32[]{:S(2)}) %collective-permute-start.4) | collective-permute-done | bytes 288 | tf_op jit(solution)/shard_map/ppermute | solution.py:13
  16.8 3.4 %collective-permute-done.5 = bf16[128]{0:T(256)(128)(2,1)S(1)} collective-permute-done((bf16[128]{0:T(256)(128)(2,1)S(1)}, bf16[128]{0:T(256)(128)(2,1)S(1)}, u32[]{:S(2)}, u32[]{:S(2)}) %collective-permute-start.5) | collective-permute-done | bytes 288 | tf_op jit(solution)/shard_map/ppermute | solution.py:13
  20.3 4.3 %collective-permute-done.2 = bf16[32,128]{1,0:T(8,128)(2,1)S(1)} collective-permute-done((bf16[32,128]{1,0:T(8,128)(2,1)S(1)}, bf16[32,128]{1,0:T(8,128)(2,1)S(1)}, u32[]{:S(2)}, u32[]{:S(2)}) %collective-permute-start.2) | collective-permute-done | bytes 8224 | tf_op jit(solution)/shard_map/ppermute | solution.py:13
  25.2 2.7 %multiply_convert_fusion = (bf16[128,8192]{0,1:T(8,128)(2,1)S(1)}, f32[128,8192]{0,1:T(8,128)S(1)}) fusion(bf16[32,128]{1,0:T(8,128)(2,1)} %param.13, f32[4,8,64,128]{3,2,1,0:T(8,128)S(1)} %bitcast.119, f32[32]{0:T(128)S(1)} %multiply_reduce_fusion), kind=kOutput, calls=%fused_computation.30 | convolution fusion | flops 77070336 | bytes 7348352 | tf_op jit(solution)/shard_map/while/body/eval_jaxpr/dot_general | solution.py:31
  28.0 2.0 %multiply_convert_fusion.1 = (bf16[128,8192]{0,1:T(8,128)(2,1)S(1)}, f32[128,8192]{0,1:T(8,128)S(1)}) fusion(bf16[32,128]{1,0:T(8,128)(2,1)S(1)} %copy-done.2, f32[4,8,64,128]{3,2,1,0:T(8,128)S(1)} %bitcast.122, f32[32]{0:T(128)S(1)} %multiply_reduce_fusion), kind=kOutput, calls=%fused_computation.31 | convolution fusion | flops 77070336 | bytes 7348352 | tf_op jit(solution)/shard_map/while/body/eval_jaxpr/dot_general | solution.py:31
  33.9 3.7 %fusion.10 = bf16[128,8192]{0,1:T(8,128)(2,1)S(1)} fusion(f32[128,8192]{0,1:T(8,128)S(1)} %get-tuple-element.81, bf16[128,32]{0,1:T(8,128)(2,1)S(1)} %copy-done.1, f32[8192]{0:T(1024)S(1)} %get-tuple-element.70, f32[32]{0:T(128)S(1)} %copy-done.4), kind=kOutput, calls=%fused_computation.22 | convolution fusion | flops 88604672 | bytes 6332544 | tf_op jit(solution)/shard_map/while/body/eval_jaxpr/dot_general | solution.py:47
  39.3 3.5 %fusion.17 = bf16[128,8192]{0,1:T(8,128)(2,1)S(1)} fusion(f32[128,8192]{0,1:T(8,128)S(1)} %get-tuple-element.83, bf16[128,32]{0,1:T(8,128)(2,1)S(1)} %copy-done.1, f32[8192]{0:T(1024)S(1)} %get-tuple-element.71, f32[32]{0:T(128)S(1)} %copy-done.4), kind=kOutput, calls=%fused_computation.29 | convolution fusion | flops 88604672 | bytes 6332544 | tf_op jit(solution)/shard_map/while/body/eval_jaxpr/dot_general | solution.py:47
  44.4 1.4 convolution_bitcast_fusion.8
  47.7 3.4 %collective-permute-start.6 = (f32[32,128]{1,0:T(8,128)S(1)}, f32[32,128]{1,0:T(8,128)S(1)}, u32[]{:S(2)}, u32[]{:S(2)}) collective-permute-start(f32[32,128]{1,0:T(8,128)S(1)} %get-tuple-element.50), channel_id=1, source_target_pairs={{0,4},{4,8},{8,12},{12,16},{16,20},{20,24},{24,28},{1,5},{5,9},{9,... | collective-permute-start | bytes 49160 | tf_op jit(solution)/shard_map/ppermute | solution.py:13
  51.2 4.8 %collective-permute-start.7 = (f32[32,128]{1,0:T(8,128)S(1)}, f32[32,128]{1,0:T(8,128)S(1)}, u32[]{:S(2)}, u32[]{:S(2)}) collective-permute-start(f32[32,128]{1,0:T(8,128)S(1)} %get-tuple-element.69), channel_id=1, source_target_pairs={{0,8},{4,12},{8,16},{12,20},{16,24},{20,28},{1,9},{5,13},{9,17},{1... | collective-permute-start | bytes 49160 | tf_op jit(solution)/shard_map/ppermute | solution.py:13
  55.9 2.0 %collective-permute-start.8 = (f32[32,128]{1,0:T(8,128)S(1)}, f32[32,128]{1,0:T(8,128)S(1)}, u32[]{:S(2)}, u32[]{:S(2)}) collective-permute-start(f32[32,128]{1,0:T(8,128)S(1)} %get-tuple-element.68), channel_id=1, source_target_pairs={{0,12},{4,16},{8,20},{12,24},{16,28},{1,13},{5,17},{9,21},{13,25},... | collective-permute-start | bytes 49160 | tf_op jit(solution)/shard_map/ppermute | solution.py:13
  58.6 1.6 fusion.19
  60.9 39.1 %all-reduce = (f32[32,128]{1,0:T(8,128)}, f32[128,32]{0,1:T(8,128)}, f32[32]{0:T(128)}, f32[32,4]{0,1:T(4,128)}) all-reduce(f32[32,128]{1,0:T(8,128)S(1)} %convolution_add_fusion.2, f32[128,32]{0,1:T(8,128)S(1)} %convolution_add_fusion.1, f32[32]{0:T(128)S(1)} %fusion.19, ...), channel_id=1, replica_groups=mesh['rows'=8,'band'=4] {'rows','band'}, use_global_device_ids=true, to_apply=%region_9.10 | all-reduce | flops 8352 | bytes 66816 | tf_op jit(solution)/shard_map/psum | solution.py:194
  100.1 10.3 %all-reduce.2 = (bf16[32,128]{1,0:T(8,128)(2,1)S(1)}, bf16[32,128]{1,0:T(8,128)(2,1)S(1)}) all-reduce(f32[32,128]{1,0:T(8,128)S(1)} %pad_maximum_fusion.1, f32[32,128]{1,0:T(8,128)S(1)} %fusion.40), channel_id=1, replica_groups=mesh['rows'=8,'band'=4] {'band'}, use_global_device_ids=true, to_apply=%region_3.4 | all-reduce | flops 8192 | bytes 49152 | tf_op jit(solution)/shard_map/psum | solution.py:191
  111.5 36.1 %all-reduce.1 = (f32[128,32]{0,1:T(8,128)S(1)}, f32[128,32]{0,1:T(8,128)S(1)}) all-reduce(f32[128,32]{0,1:T(8,128)S(1)} %fusion.35, f32[128,32]{0,1:T(8,128)S(1)} %fusion.37), channel_id=1, replica_groups=mesh['rows'=8,'band'=4] {'rows'}, use_global_device_ids=true, to_apply=%region_7.8 | all-reduce | flops 8192 | bytes 65536 | tf_op jit(solution)/shard_map/psum | solution.py:216
  147.7 5.2 %all_gather.6 = f32[512,32]{0,1:T(8,128)S(1)} all-gather(f32[128,32]{0,1:T(8,128)S(1)} %get-tuple-element.46), channel_id=1, replica_groups=mesh['rows'=8,'band'=4] {'band'}, dimensions={0}, use_global_device_ids=true | all-gather | bytes 81920 | tf_op jit(solution)/shard_map/all_gather | solution.py:218
  152.9 5.2 %all_gather.7 = f32[512,32]{0,1:T(8,128)S(1)} all-gather(f32[128,32]{0,1:T(8,128)S(1)} %get-tuple-element.47), channel_id=1, replica_groups=mesh['rows'=8,'band'=4] {'band'}, dimensions={0}, use_global_device_ids=true | all-gather | bytes 81920 | tf_op jit(solution)/shard_map/all_gather | solution.py:219
  158.1 1.5 fusion.18
  (56 shorter events, 18.6 us)
Async XLA Ops:
  0.6 0.9 copy-start
  2.4 17.9 %collective-permute-start = (bf16[32,128]{1,0:T(8,128)(2,1)S(1)}, bf16[32,128]{1,0:T(8,128)(2,1)S(1)}, u32[]{:S(2)}, u32[]{:S(2)}) collective-permute-start(bf16[32,128]{1,0:T(8,128)(2,1)S(1)} %convolution_convert_fusion), channel_id=1, source_target_pairs={{4,0},{8,4},{12,8},{16,12},{20,16},{24,20},{28,24},{5,1},{9,5},{13... | collective-permute-start | bytes 24584 | tf_op jit(solution)/shard_map/ppermute | solution.py:13
  3.7 16.6 %collective-permute-start.1 = (bf16[32,128]{1,0:T(8,128)(2,1)S(1)}, bf16[32,128]{1,0:T(8,128)(2,1)S(1)}, u32[]{:S(2)}, u32[]{:S(2)}) collective-permute-start(bf16[32,128]{1,0:T(8,128)(2,1)S(1)} %convolution_convert_fusion), channel_id=1, source_target_pairs={{8,0},{12,4},{16,8},{20,12},{24,16},{28,20},{9,1},{13,5},{17,9},{2... | collective-permute-start | bytes 24584 | tf_op jit(solution)/shard_map/ppermute | solution.py:13
  5.7 7.1 %collective-permute-start.3 = (bf16[128]{0:T(256)(128)(2,1)S(1)}, bf16[128]{0:T(256)(128)(2,1)S(1)}, u32[]{:S(2)}, u32[]{:S(2)}) collective-permute-start(bf16[128]{0:T(256)(128)(2,1)S(1)} %convert_element_type.109), channel_id=1, source_target_pairs={{4,0},{8,4},{12,8},{16,12},{20,16},{24,20},{28,24},{5,1},{9,5},{13... | collective-permute-start | bytes 776 | tf_op jit(solution)/shard_map/ppermute | solution.py:13
  7.0 9.8 %collective-permute-start.4 = (bf16[128]{0:T(256)(128)(2,1)S(1)}, bf16[128]{0:T(256)(128)(2,1)S(1)}, u32[]{:S(2)}, u32[]{:S(2)}) collective-permute-start(bf16[128]{0:T(256)(128)(2,1)S(1)} %convert_element_type.109), channel_id=1, source_target_pairs={{8,0},{12,4},{16,8},{20,12},{24,16},{28,20},{9,1},{13,5},{17,9},{2... | collective-permute-start | bytes 776 | tf_op jit(solution)/shard_map/ppermute | solution.py:13
  8.3 11.9 %collective-permute-start.5 = (bf16[128]{0:T(256)(128)(2,1)S(1)}, bf16[128]{0:T(256)(128)(2,1)S(1)}, u32[]{:S(2)}, u32[]{:S(2)}) collective-permute-start(bf16[128]{0:T(256)(128)(2,1)S(1)} %convert_element_type.109), channel_id=1, source_target_pairs={{12,0},{16,4},{20,8},{24,12},{28,16},{13,1},{17,5},{21,9},{25,13},... | collective-permute-start | bytes 776 | tf_op jit(solution)/shard_map/ppermute | solution.py:13
  12.8 11.8 %collective-permute-start.2 = (bf16[32,128]{1,0:T(8,128)(2,1)S(1)}, bf16[32,128]{1,0:T(8,128)(2,1)S(1)}, u32[]{:S(2)}, u32[]{:S(2)}) collective-permute-start(bf16[32,128]{1,0:T(8,128)(2,1)S(1)} %convolution_convert_fusion), channel_id=1, source_target_pairs={{12,0},{16,4},{20,8},{24,12},{28,16},{13,1},{17,5},{21,9},{25,13},... | collective-permute-start | bytes 24584 | tf_op jit(solution)/shard_map/ppermute | solution.py:13
  25.2 2.8 %copy-start.2 = (bf16[32,128]{1,0:T(8,128)(2,1)S(1)}, bf16[32,128]{1,0:T(8,128)(2,1)}, u32[]{:S(2)}) copy-start(bf16[32,128]{1,0:T(8,128)(2,1)} %param.13) | copy-start | bytes 24580
  28.0 2.0 %copy-start.1 = (bf16[128,32]{0,1:T(8,128)(2,1)S(1)}, bf16[128,32]{0,1:T(8,128)(2,1)}, u32[]{:S(2)}) copy-start(bf16[128,32]{0,1:T(8,128)(2,1)} %param.14) | copy-start | bytes 24580
  30.0 2.0 %copy-start.4 = (f32[32]{0:T(128)S(1)}, f32[32]{0:T(128)}, u32[]{:S(2)}) copy-start(f32[32]{0:T(128)} %param.15) | copy-start | bytes 388
  31.0 2.3 %copy-start.3 = (bf16[1,1,128,128]{3,2,1,0:T(8,128)(2,1)S(1)}, bf16[1,1,128,128]{3,2,1,0:T(8,128)(2,1)}, u32[]{:S(2)}) copy-start(bf16[1,1,128,128]{3,2,1,0:T(8,128)(2,1)} %param.19) | copy-start | bytes 98308
  47.7 52.3 %collective-permute-start.6 = (f32[32,128]{1,0:T(8,128)S(1)}, f32[32,128]{1,0:T(8,128)S(1)}, u32[]{:S(2)}, u32[]{:S(2)}) collective-permute-start(f32[32,128]{1,0:T(8,128)S(1)} %get-tuple-element.50), channel_id=1, source_target_pairs={{0,4},{4,8},{8,12},{12,16},{16,20},{20,24},{24,28},{1,5},{5,9},{9,... | collective-permute-start | bytes 49160 | tf_op jit(solution)/shard_map/ppermute | solution.py:13
  51.2 48.9 %collective-permute-start.7 = (f32[32,128]{1,0:T(8,128)S(1)}, f32[32,128]{1,0:T(8,128)S(1)}, u32[]{:S(2)}, u32[]{:S(2)}) collective-permute-start(f32[32,128]{1,0:T(8,128)S(1)} %get-tuple-element.69), channel_id=1, source_target_pairs={{0,8},{4,12},{8,16},{12,20},{16,24},{20,28},{1,9},{5,13},{9,17},{1... | collective-permute-start | bytes 49160 | tf_op jit(solution)/shard_map/ppermute | solution.py:13
  55.9 44.1 %collective-permute-start.8 = (f32[32,128]{1,0:T(8,128)S(1)}, f32[32,128]{1,0:T(8,128)S(1)}, u32[]{:S(2)}, u32[]{:S(2)}) collective-permute-start(f32[32,128]{1,0:T(8,128)S(1)} %get-tuple-element.68), channel_id=1, source_target_pairs={{0,12},{4,16},{8,20},{12,24},{16,28},{1,13},{5,17},{9,21},{13,25},... | collective-permute-start | bytes 49160 | tf_op jit(solution)/shard_map/ppermute | solution.py:13
where the time goes:
time: 162 us; the launch traced here: 161 us
  blocking collectives  96 us (59%)
  matrix products  27 us (17%)
  starting transfers between devices  17.9 us (11%)
  waiting for transfers between devices  11.1 us (7%)
  other arithmetic  4.46 us (3%)
  local copies, waits for them, and re-layouts  2.72 us (2%)
  between operations  1.62 us (1%)
    psum x1, blocking collectives, on_device(): lax.psum((in_part, out_part, head_part, bias_part), ('rows', 'band'))  39.1 us
    psum x1, blocking collectives, on_device(): left_sum, right_sum = lax.psum((left_part, right_part), 'rows')  36.1 us
    ppermute x9, starting transfers between devices, from_behind(): lax.ppermute(value, axis, [(source, source + steps) for source in range(l...  17.9 us
    ppermute x9, waiting for transfers between devices, from_behind(): lax.ppermute(value, axis, [(source, source + steps) for source in range(l...  11.1 us
    psum x1, blocking collectives, on_device(): row_total, col_total = lax.psum((row_acc, col_own), 'band')  10.3 us
    dot_general x2, matrix products, block_terms(): lax.dot_general(w_out, grad_low, (((1,), (0,)), ((), ())), preferred_elem...  7.13 us
    all_gather x1, blocking collectives, on_device(): lax.all_gather(left_sum, 'band', axis=0, tiled=True)  5.22 us
    all_gather x1, blocking collectives, on_device(): lax.all_gather(right_sum, 'band', axis=0, tiled=True)  5.22 us
  transfers between devices with their start and end apart: 9, of which 4 were waited for; matrix products, arithmetic and copies ran while one was open for 3% of the time, Pallas kernels for 0%

commit v1 on v0

v1 whole, which is shorter than its diff:
```python
import math

import jax
import jax.numpy as jnp
from jax import lax
from jax.experimental import pallas as pl
from jax.experimental.pallas import tpu as pltpu
from jax.sharding import PartitionSpec as P

BF = jnp.bfloat16
F32 = jnp.float32
CURVE = math.sqrt(2.0 / math.pi)
CUBIC = 0.044715 * CURVE
GROUP = 8
HALVES = 2
NT = (((1,), (1,)), ((), ()))
NN = (((1,), (0,)), ((), ()))


def mm(a, b, dims=NN):
    return lax.dot_general(a, b, dims, preferred_element_type=F32)


def split(x):
    high = x.astype(BF)
    return high, (x - high.astype(F32)).astype(BF)


def mm_wide(a, b, dims=NN):
    high, low = split(b)
    return mm(a, high, dims) + mm(a, low, dims)


def eye(count):
    return lax.broadcasted_iota(jnp.int32, (count, count), 0) == lax.broadcasted_iota(
        jnp.int32, (count, count), 1
    )


def to_col(row):
    count = row.shape[1]
    return jnp.sum(jnp.where(eye(count), jnp.broadcast_to(row, (count, count)), 0.0), axis=1, keepdims=True)


def to_row(col):
    count = col.shape[0]
    return jnp.sum(jnp.where(eye(count), jnp.broadcast_to(col, (count, count)), 0.0), axis=0, keepdims=True)


def project_kernel(emb_ref, wl_ref, wr_ref, flags_ref, left_ref, send_ref):
    channels = wl_ref.shape[1]
    emb = emb_ref[...]
    bins = emb.shape[0]
    pad = jnp.zeros((bins, bins - 2 * channels), F32)
    both = jnp.concatenate([mm(emb, wl_ref[...]), mm(emb, wr_ref[...]), pad], axis=1).T
    left_ref[...] = both[:channels].astype(BF)
    flags = jnp.broadcast_to(flags_ref[...].astype(F32), (GROUP, bins))
    piece = jnp.concatenate([both[channels : 2 * channels], flags], axis=0).astype(BF)
    for row in range(send_ref.shape[0]):
        send_ref[row] = piece


def tile_kernel(
    info_ref,
    left_ref,
    recv_ref,
    flags_ref,
    target_ref,
    w_in_ref,
    w_out_ref,
    w_head_ref,
    bias_ref,
    pred_ref,
    send_ref,
    target_wide,
    act_ref,
    slope_ref,
    logit_ref,
    res_ref,
    row_ref,
    col_ref,
    act_sum_ref,
    logit_col_ref,
    flag_col_ref,
):
    channels, hidden = w_in_ref.shape
    tile = target_ref.shape[0]
    noff = bias_ref.shape[1]
    rows = recv_ref.shape[0]
    bands = send_ref.shape[0] // rows
    part = 2 * channels // bands
    here, offset = info_ref[0], info_ref[1]
    there = here + offset
    inside = (there < rows).astype(F32)
    piece = recv_ref[jnp.minimum(there, rows - 1)].astype(F32) * inside
    right = piece[:channels]
    col_flags = piece[channels : channels + 1] * (1.0 / (noff * tile))
    left = left_ref[...].astype(F32)
    lane_off = lax.broadcasted_iota(jnp.int32, (channels, noff), 1)
    bias = jnp.sum(jnp.where(lane_off == offset, bias_ref[...], 0.0), axis=1, keepdims=True)
    head_row = w_head_ref[...]
    head = to_col(head_row)
    gain = jnp.sum(w_out_ref[...].astype(F32) * head_row, axis=1, keepdims=True) * 0.5
    gain_row = to_row(gain)
    logit_col_ref[...] = to_col(jnp.sum((left + bias) * head, axis=0, keepdims=True))
    logit_row = jnp.sum(right * head, axis=0, keepdims=True)
    flag_col_ref[...] = to_col(flags_ref[...].astype(F32))
    target_wide[...] = target_ref[...].astype(F32)
    shifted = right + bias
    w_in = w_in_ref[...]
    w_in_t = w_in.astype(F32).T.astype(BF)
    gain_a, rest = gain_row.astype(BF), gain_row - gain_row.astype(BF).astype(F32)
    gain_b = rest.astype(BF)
    gain_c = (rest - gain_b.astype(F32)).astype(BF)
    group_row = lax.broadcasted_iota(jnp.int32, (GROUP, 1), 0)
    gain_parts = [
        jnp.concatenate(
            [jnp.where(group_row == step, part_of.astype(F32), 0.0) for part_of in (gain_a, gain_b, gain_c)], axis=0
        ).astype(BF)
        for step in range(GROUP)
    ]
    col_ref[...] = jnp.zeros_like(col_ref)
    act_sum_ref[...] = jnp.zeros_like(act_sum_ref)

    def body(index, carry):
        start = pl.multiple_of(index * GROUP, GROUP)
        turned = pltpu.roll(left, (tile - start) % tile, 1)
        logits = jnp.zeros((3 * GROUP, tile), F32)
        for step in range(GROUP):
            pair_in = (turned[:, step : step + 1] + shifted).astype(BF)
            x = mm(w_in_t, pair_in)
            inner = CURVE + CUBIC * (x * x)
            bend = jnp.tanh(x * inner)
            lift = 1.0 + bend
            act = (x * lift).astype(BF)
            slope_ref[step] = lift + (1.0 - bend * bend) * (x * (3.0 * inner - 2.0 * CURVE))
            act_ref[step] = act
            logits = logits + mm(gain_parts[step], act)
        logits = logits[:GROUP] + logits[GROUP : 2 * GROUP] + logits[2 * GROUP :]
        logits = logits + logit_col_ref[pl.ds(start, GROUP), :] + logit_row
        logit_ref[pl.ds(start, GROUP), :] = logits
        mask = flag_col_ref[pl.ds(start, GROUP), :] * col_flags
        res = mask * (logits - target_wide[pl.ds(start, GROUP), :])
        res_ref[pl.ds(start, GROUP), :] = res
        high = res.astype(BF).astype(F32)
        low = res - high
        grow = jnp.zeros((2 * GROUP, hidden), F32)
        acts = jnp.zeros((2 * GROUP, hidden), F32)
        total = col_ref[...]
        for step in range(GROUP):
            slope = slope_ref[step]
            keep = group_row == step
            lhs = jnp.concatenate([jnp.where(keep, high, 0.0), jnp.where(keep, low, 0.0)], axis=0).astype(BF)
            grow = grow + mm(lhs, slope.astype(BF), NT)
            acts = acts + mm(lhs, act_ref[step], NT)
            total = total + slope * res[step : step + 1]
        col_ref[...] = total
        row_ref[pl.ds(start, GROUP), :] = grow[:GROUP] + grow[GROUP:]
        act_sum_ref[...] += acts
        return carry

    lax.fori_loop(0, tile // GROUP, body, 0)

    pred_ref[...] = logit_ref[...].astype(BF)
    res = res_ref[...]
    res_col = jnp.sum(res, axis=0, keepdims=True)
    res_row = to_row(jnp.sum(res, axis=1, keepdims=True))
    res_all = jnp.sum(res_row, axis=1, keepdims=True)
    row_part = row_ref[...] * gain_row
    col_part = col_ref[...] * gain
    act_sum = jnp.sum(act_sum_ref[...], axis=0, keepdims=True) * 0.5
    row_sums = head * res_row + mm_wide(w_in, row_part, NT)
    col_sums = head * res_col + mm_wide(w_in, col_part)
    left_low, right_low = left_ref[...], right.astype(BF)
    in_term = (
        mm_wide(left_low, row_part) + mm_wide(right_low, col_part, NT) + bias * jnp.sum(row_part, axis=0, keepdims=True)
    )
    w_out_t = w_out_ref[...].astype(F32).T
    head_term = jnp.sum(left * res_row + right * res_col + w_out_t * act_sum, axis=1, keepdims=True) + bias * res_all
    bias_sum = jnp.sum(row_sums, axis=1, keepdims=True)
    wide = jnp.zeros((channels, hidden), F32)
    lane = lax.broadcasted_iota(jnp.int32, (channels, hidden), 1)
    wide = jnp.where(lane == 1, head_term, wide)
    wide = jnp.where(lane == offset + 2, bias_sum, wide)
    flat = jnp.concatenate([wide] + [jnp.zeros_like(wide)] * (hidden // channels - 1), axis=0).T
    first = lax.broadcasted_iota(jnp.int32, (GROUP, hidden), 0) == 0
    small = jnp.concatenate([in_term, jnp.where(first, act_sum, flat[:GROUP])], axis=0)
    small_high = small.astype(BF).astype(F32)
    small_low = small - small_high
    owners = small.shape[0] // GROUP
    send_ref[...] = jnp.zeros_like(send_ref)
    for piece_index in range(3 * owners):
        source = small_low if piece_index // owners == 1 else small_high
        block = piece_index % owners
        send_ref[piece_index, part:, :] = source[block * GROUP : (block + 1) * GROUP].astype(BF)
    for quarter in range(bands // 2):
        send_ref[here * bands + quarter, :part, :] = row_sums[quarter * part : (quarter + 1) * part].astype(BF)

    @pl.when(there < rows)
    def _():
        for quarter in range(bands // 2):
            send_ref[there * bands + bands // 2 + quarter, :part, :] = col_sums[
                quarter * part : (quarter + 1) * part
            ].astype(BF)


def total_kernel(info_ref, recv_ref, send_ref):
    devices, height, width = recv_ref.shape
    total = recv_ref[0].astype(F32)
    for source in range(1, devices):
        total = total + recv_ref[source].astype(F32)
    low = total - total.astype(BF).astype(F32)
    row = lax.broadcasted_iota(jnp.int32, (height, width), 0)
    use_low = jnp.logical_and(info_ref[0] == 2, row >= height - GROUP)
    piece = jnp.where(use_low, low, total).astype(BF)
    for target in range(devices):
        send_ref[target] = piece


def finish_kernel(
    info_ref, recv_ref, emb_ref, wl_ref, wr_ref, w_head_ref, share_ref, grad_emb_ref, in_ref, out_ref, head_ref, bias_ref
):
    rows = emb_ref.shape[0]
    devices, height, width = recv_ref.shape
    bands = devices // rows
    part = height - GROUP
    channels = in_ref.shape[0]
    hidden = out_ref.shape[0]

    def grads(row):
        return jnp.concatenate([recv_ref[row * bands + band, :part, :].astype(F32) for band in range(bands)], axis=0)

    def body(row, total):
        return total + mm(grads(row).astype(BF), emb_ref[row])

    share_ref[...] = lax.fori_loop(0, rows, body, jnp.zeros(share_ref.shape, F32), unroll=rows <= 8)
    own = grads(info_ref[0]).astype(BF)
    share = pl.ds(pl.multiple_of(info_ref[1] * width, width), width)
    weights = jnp.concatenate([wl_ref[share, :].astype(F32), wr_ref[share, :].astype(F32)], axis=1).astype(BF)
    grad_emb_ref[...] = mm(weights, own).T.astype(BF)
    owners = channels // GROUP + 1
    small = [
        recv_ref[block, part:, :].astype(F32)
        + recv_ref[owners + block, part:, :].astype(F32)
        + recv_ref[2 * owners + block, part:, :].astype(F32)
        for block in range(owners)
    ]
    in_ref[...] = jnp.concatenate(small[:-1], axis=0)
    last = small[-1]
    turned = jnp.concatenate([last, jnp.zeros((hidden - GROUP, hidden), F32)], axis=0).T
    out_ref[...] = turned[:, :1] * w_head_ref[...]
    head_ref[...] = last[1:2, :channels]
    bias_ref[...] = turned[:channels, 2 : 2 + bias_ref.shape[1]]


def arrange_kernel(info_ref, own_ref, other_ref, left_ref, right_ref):
    channels = left_ref.shape[1]
    width = own_ref.shape[1]
    for ref, index in ((own_ref, info_ref[0]), (other_ref, 1 - info_ref[0])):
        turned = ref[...].T
        place = pl.ds(pl.multiple_of(index * width, width), width)
        left_ref[place, :] = turned[:, :channels]
        right_ref[place, :] = turned[:, channels:]


def vmem():
    return pl.BlockSpec(memory_space=pltpu.VMEM)


def smem():
    return pl.BlockSpec(memory_space=pltpu.SMEM)


def call(kernel, outs, ins, scratch=(), name=None):
    return pl.pallas_call(
        kernel,
        out_shape=[jax.ShapeDtypeStruct(shape, kind) for shape, kind in outs],
        in_specs=ins,
        out_specs=[vmem()] * len(outs),
        scratch_shapes=[pltpu.VMEM(shape, kind) for shape, kind in scratch],
        name=name,
    )


def exchange(value, axes):
    return lax.all_to_all(value, axes, 0, 0, tiled=True)


def on_device(embedding, w_left, w_right, w_in, w_out, w_head, dist_bias, offsets, valid_bins, target):
    rows, bands = lax.axis_size("rows"), lax.axis_size("band")
    devices = rows * bands
    bins, features = embedding.shape
    channels, hidden = w_in.shape
    tile = target.shape[-1]
    part = 2 * channels // bands
    owners = channels // GROUP + 1
    half = features // HALVES
    row_index, band_index = lax.axis_index("rows"), lax.axis_index("band")
    device_index = row_index * bands + band_index
    half_index = band_index % HALVES
    flags = valid_bins.reshape(1, bins)
    head_row = w_head.reshape(1, channels)

    left, send = call(
        project_kernel,
        [((channels, bins), BF), ((rows, channels + GROUP, bins), BF)],
        [vmem()] * 4,
        name="project",
    )(embedding, w_left, w_right, flags)
    received = exchange(send, "rows")
    embedding, received = lax.optimization_barrier((embedding, received))
    emb_half = lax.dynamic_slice_in_dim(embedding, half_index * half, half, 1)
    emb_all = exchange(jnp.broadcast_to(emb_half[None], (rows, bins, half)), "rows")

    info = jnp.stack([row_index, offsets[0, 0]]).astype(jnp.int32)
    predicted, send = call(
        tile_kernel,
        [((tile, tile), BF), ((devices, part + GROUP, tile), BF)],
        [smem()] + [vmem()] * 8,
        [
            ((tile, tile), F32),
            ((GROUP, hidden, tile), BF),
            ((GROUP, hidden, tile), F32),
            ((tile, tile), F32),
            ((tile, tile), F32),
            ((tile, hidden), F32),
            ((hidden, tile), F32),
            ((2 * GROUP, hidden), F32),
            ((tile, 1), F32),
            ((tile, 1), F32),
        ],
        name="tile",
    )(info, left, received, flags, target.reshape(tile, tile), w_in, w_out, head_row, dist_bias)
    partial = exchange(send, ("rows", "band"))
    group = (device_index // owners).astype(jnp.int32).reshape(1)
    (send,) = call(
        total_kernel, [(partial.shape, BF)], [smem(), vmem()], name="total"
    )(group, partial)
    complete = exchange(send, ("rows", "band"))
    place = jnp.stack([row_index, band_index]).astype(jnp.int32)
    share, grad_embedding, grad_in, grad_out, grad_head, grad_bias = call(
        finish_kernel,
        [
            ((2 * channels, half), F32),
            ((bins, features // bands), BF),
            ((channels, hidden), F32),
            ((hidden, channels), F32),
            ((1, channels), F32),
            (dist_bias.shape, F32),
        ],
        [smem()] + [vmem()] * 5,
        name="finish",
    )(place, complete, emb_all, w_left, w_right, head_row)
    other = lax.ppermute(share, "band", [(source, source ^ 1) for source in range(bands)])
    grad_left, grad_right = call(
        arrange_kernel,
        [(w_left.shape, F32), (w_right.shape, F32)],
        [smem(), vmem(), vmem()],
        name="arrange",
    )(half_index.astype(jnp.int32).reshape(1), share, other)
    return (
        predicted.reshape(target.shape),
        grad_embedding,
        grad_left,
        grad_right,
        grad_in,
        grad_out,
        grad_head.reshape(channels),
        grad_bias,
    )


def solution(mesh):
    placed = (
        P("rows", None),
        P(),
        P(),
        P(),
        P(),
        P(),
        P(),
        P("rows", "band"),
        P("rows"),
        P("rows", "band", None, None),
    )
    return jax.shard_map(
        on_device,
        mesh=mesh,
        in_specs=placed,
        out_specs=(P("rows", "band", None, None), P("rows", "band"), P(), P(), P(), P(), P(), P()),
        check_vma=False,
    )
```

time: 162 us -> 98.3 us (0.61)
  blocking collectives: 96 us -> 0 us
  Pallas kernels: 0 us -> 30 us
  matrix products: 27 us -> 0 us
  waiting for transfers between devices: 11.1 us -> 36.9 us
  local copies, waits for them, and re-layouts: 2.72 us -> 12 us
  other arithmetic: 4.46 us -> 1.17 us
  starting transfers between devices: 17.9 us -> 16.1 us
    psum x3 -> x0, blocking collectives: 85.6 us -> none  [the longest x1 39.1 us: on_device(): lax.psum((in_part, out_part, head_part, bias_part), ('rows', 'band'))]
    all_to_all x0 -> x4, waiting for transfers between devices: none -> 36.9 us  [exchange(): return lax.all_to_all(value, axes, 0, 0, tiled=True)]
    pallas_call x0 -> x5, Pallas kernels: none -> 30 us  [the longest x1 22.4 us: on_device(): call(tile_kernel, [((tile, tile), BF), ((devices, part + GROUP, tile), BF...]
    dot_general x22 -> x0, matrix products: 27 us -> none  [the longest x2 7.13 us: block_terms(): lax.dot_general(w_out, grad_low, (((1,), (0,)), ((), ())), preferred_elem...]
    ppermute x9 -> x1, starting transfers between devices: 17.9 us -> 0.01 us  [on_device(): lax.ppermute(share, 'band', [(source, source ^ 1) for source in range(ban...]
    all_to_all x0 -> x4, starting transfers between devices: none -> 16.1 us  [exchange(): return lax.all_to_all(value, axes, 0, 0, tiled=True)]
    ppermute x9 -> x1, waiting for transfers between devices: 11.1 us -> 0.01 us  [on_device(): lax.ppermute(share, 'band', [(source, source ^ 1) for source in range(ban...]
    all_gather x2 -> x0, blocking collectives: 10.4 us -> none  [the longest x1 5.22 us: on_device(): lax.all_gather(left_sum, 'band', axis=0, tiled=True)]
  transfers between devices with their start and end apart: 9 -> 5, of which waited for: 4 -> 4; matrix products, arithmetic and copies ran while one was open for 3% -> 5% of each run, Pallas kernels for 0% -> 0%
where the time goes in v1:
time: 98.3 us; the launch traced here: 97.6 us
  waiting for transfers between devices  36.9 us (38%)
  Pallas kernels  30 us (31%)
  starting transfers between devices  16.1 us (16%)
  local copies, waits for them, and re-layouts  12 us (12%)
  between operations  1.42 us (1%)
  other arithmetic  1.17 us (1%)
    all_to_all x4, waiting for transfers between devices, exchange(): return lax.all_to_all(value, axes, 0, 0, tiled=True)  36.9 us
    pallas_call x1, Pallas kernels, on_device(): call(tile_kernel, [((tile, tile), BF), ((devices, part + GROUP, tile), BF...  22.4 us
    all_to_all x4, starting transfers between devices, exchange(): return lax.all_to_all(value, axes, 0, 0, tiled=True)  16.1 us
    unnamed x30, local copies, waits for them, and re-layouts  11.1 us
    pallas_call x1, Pallas kernels, on_device(): call(finish_kernel, [((2 * channels, half), F32), ((bins, features // ban...  2.15 us
    pallas_call x1, Pallas kernels, on_device(): call(project_kernel, [((channels, bins), BF), ((rows, channels + GROUP, b...  2.01 us
  transfers between devices with their start and end apart: 5, of which 4 were waited for; matrix products, arithmetic and copies ran while one was open for 5% of the time, Pallas kernels for 0%

profile of v1, /device:TPU:0, one launch (start us, length us, event | category | flops | bytes accessed | tf_op | source)
XLA Modules:
  0.0 97.6 jit_solution(6386514328697913037)
XLA Ops:
  0.6 1.5 %copy.18.wl_ref = bf16[512,32]{1,0:T(8,128)(2,1)} copy(bf16[512,32]{0,1:T(8,128)(2,1)} %param.11) | data formatting | bytes 65536 | tf_op args[1]
  2.2 0.7 copy.19.wr_ref
  2.9 2.0 %project.1 = (bf16[32,128]{1,0:T(8,128)(2,1)}, bf16[8,40,128]{2,1,0:T(8,128)(2,1)}) custom-call(bf16[128,512]{1,0:T(8,128)(2,1)} %emb_ref.1, bf16[512,32]{1,0:T(8,128)(2,1)} %copy.18.wl_ref, bf16[512,32]{1,0:T(8,128)(2,1)} %copy.19.wr_ref, s32[1,128]{1,0:T(1,128)} %bitcast.12), custom_call_target="tpu_custom_call" | custom-call | tf_op jit(solution)/shard_map/project/pallas_call | solution.py:304
  4.9 7.3 %all-to-all-start = ((bf16[8,40,128]{2,1,0:T(8,128)(2,1)}), bf16[8,40,128]{2,1,0:T(8,128)(2,1)S(1)}, u32[]{:S(2)}, u32[]{:S(2)}) async-start(bf16[8,40,128]{2,1,0:T(8,128)(2,1)} %get-tuple-element.23), calls=%async_computation | async-start | bytes 163840 | tf_op jit(solution)/shard_map/all_to_all | solution.py:286
  12.9 0.7 copy.20.w_out_ref
  13.6 0.7 copy.21.bias_ref
  14.9 4.3 %all-to-all-done.recv_ref = bf16[8,40,128]{2,1,0:T(8,128)(2,1)S(1)} async-done(((bf16[8,40,128]{2,1,0:T(8,128)(2,1)}), bf16[8,40,128]{2,1,0:T(8,128)(2,1)S(1)}, u32[]{:S(2)}, u32[]{:S(2)}) %all-to-all-start) | async-done | bytes 81952 | tf_op jit(solution)/shard_map/all_to_all | solution.py:286
  19.9 22.4 %tile.1 = (bf16[128,128]{1,0:T(8,128)(2,1)}, bf16[32,24,128]{2,1,0:T(8,128)(2,1)}) custom-call(s32[2]{0:T(128)} %pad_add_fusion.info_ref, bf16[32,128]{1,0:T(8,128)(2,1)} %get-tuple-element.22.left_ref, bf16[8,40,128]{2,1,0:T(8,128)(2,1)} %copy-done.3, s32[1,128]{1,0:T(1,128)} %bitcast.13, bf16[128,128]{1,0:T(8,128)(2,1)} %bitcast.11, ...), custom_call_target="tpu_custom_call" | custom-call | tf_op jit(solution)/shard_map/tile/pallas_call | solution.py:316
  42.2 2.6 %all-to-all-start.1 = ((bf16[32,24,128]{2,1,0:T(8,128)(2,1)}), bf16[32,24,128]{2,1,0:T(8,128)(2,1)S(1)}, u32[]{:S(2)}, u32[]{:S(2)}) async-start(bf16[32,24,128]{2,1,0:T(8,128)(2,1)} %get-tuple-element.26), calls=%async_computation.1 | async-start | bytes 393216 | tf_op jit(solution)/shard_map/all_to_all | solution.py:286
  44.9 8.9 %all-to-all-done.1.recv_ref = bf16[32,24,128]{2,1,0:T(8,128)(2,1)S(1)} async-done(((bf16[32,24,128]{2,1,0:T(8,128)(2,1)}), bf16[32,24,128]{2,1,0:T(8,128)(2,1)S(1)}, u32[]{:S(2)}, u32[]{:S(2)}) %all-to-all-start.1) | async-done | bytes 196640 | tf_op jit(solution)/shard_map/all_to_all | solution.py:286
  53.8 0.7 copy-done.1
  54.4 1.6 %total.1 = bf16[32,24,128]{2,1,0:T(8,128)(2,1)} custom-call(s32[1]{0:T(128)} %bitcast.7.info_ref, bf16[32,24,128]{2,1,0:T(8,128)(2,1)} %copy-done.1), custom_call_target="tpu_custom_call" | custom-call | tf_op jit(solution)/shard_map/total/pallas_call | solution.py:336
  56.1 2.7 %all-to-all-start.2 = ((bf16[32,24,128]{2,1,0:T(8,128)(2,1)}), bf16[32,24,128]{2,1,0:T(8,128)(2,1)S(1)}, u32[]{:S(2)}, u32[]{:S(2)}) async-start(bf16[32,24,128]{2,1,0:T(8,128)(2,1)} %total.1), calls=%async_computation.2 | async-start | bytes 393216 | tf_op jit(solution)/shard_map/all_to_all | solution.py:286
  58.9 8.9 %all-to-all-done.2.recv_ref = bf16[32,24,128]{2,1,0:T(8,128)(2,1)S(1)} async-done(((bf16[32,24,128]{2,1,0:T(8,128)(2,1)}), bf16[32,24,128]{2,1,0:T(8,128)(2,1)S(1)}, u32[]{:S(2)}, u32[]{:S(2)}) %all-to-all-start.2) | async-done | bytes 196640 | tf_op jit(solution)/shard_map/all_to_all | solution.py:286
  67.8 0.9 broadcast_in_dim.2
  68.6 3.5 %all-to-all-start.3 = ((bf16[8,128,256]{2,1,0:T(8,128)(2,1)}), bf16[8,128,256]{2,1,0:T(8,128)(2,1)S(1)}, u32[]{:S(2)}, u32[]{:S(2)}) async-start(bf16[8,128,256]{2,1,0:T(8,128)(2,1)} %broadcast_in_dim.2), calls=%async_computation.3 | async-start | bytes 1048576 | tf_op jit(solution)/shard_map/all_to_all | solution.py:286
  72.7 14.8 %all-to-all-done.3.emb_ref = bf16[8,128,256]{2,1,0:T(8,128)(2,1)S(1)} async-done(((bf16[8,128,256]{2,1,0:T(8,128)(2,1)}), bf16[8,128,256]{2,1,0:T(8,128)(2,1)S(1)}, u32[]{:S(2)}, u32[]{:S(2)}) %all-to-all-start.3) | async-done | bytes 524320 | tf_op jit(solution)/shard_map/all_to_all | solution.py:286
  87.5 0.8 copy-done
  88.3 2.1 %finish.1 = (f32[64,256]{1,0:T(8,128)}, bf16[128,128]{1,0:T(8,128)(2,1)}, f32[32,128]{1,0:T(8,128)}, f32[128,32]{1,0:T(8,128)}, f32[1,32]{1,0:T(1,128)}, /*index=5*/f32[32,4]{1,0:T(8,128)}) custom-call(s32[2]{0:T(128)} %pad_add_fusion.1.info_ref, bf16[32,24,128]{2,1,0:T(8,128)(2,1)} %copy-done.2, bf16[8,128,256]{2,1,0:T(8,128)(2,1)} %copy-done, ...), custom_call_target="tpu_custom_call" | custom-call | tf_op jit(solution)/shard_map/finish/pallas_call | solution.py:341
  90.5 1.5 %copy.26 = f32[128,32]{0,1:T(8,128)} copy(f32[128,32]{1,0:T(8,128)} %get-tuple-element.41) | data formatting | bytes 32768
  92.0 0.7 copy.27
  93.3 1.8 %arrange.1 = (f32[512,32]{1,0:T(8,128)}, f32[512,32]{1,0:T(8,128)}) custom-call(s32[1]{0:T(128)} %bitcast.8.info_ref, f32[64,256]{1,0:T(8,128)} %get-tuple-element.29.own_ref, f32[64,256]{1,0:T(8,128)} %copy-done.6), custom_call_target="tpu_custom_call" | custom-call | tf_op jit(solution)/shard_map/arrange/pallas_call | solution.py:355
  95.1 1.7 %copy.24 = f32[512,32]{0,1:T(8,128)} copy(f32[512,32]{1,0:T(8,128)} %get-tuple-element.38) | data formatting | bytes 131072
  96.8 0.7 copy.25
  (25 shorter events, 2.5 us)
Async XLA Ops:
  0.6 1.5 %copy-start.7 = (bf16[512,32]{0,1:T(8,128)(2,1)S(1)}, bf16[512,32]{0,1:T(8,128)(2,1)}, u32[]{:S(2)}) copy-start(bf16[512,32]{0,1:T(8,128)(2,1)} %param.12) | copy-start | bytes 98308
  4.9 14.3 %all-to-all-start = ((bf16[8,40,128]{2,1,0:T(8,128)(2,1)}), bf16[8,40,128]{2,1,0:T(8,128)(2,1)S(1)}, u32[]{:S(2)}, u32[]{:S(2)}) async-start(bf16[8,40,128]{2,1,0:T(8,128)(2,1)} %get-tuple-element.23), calls=%async_computation | async-start | bytes 163840 | tf_op jit(solution)/shard_map/all_to_all | solution.py:286
  12.2 0.7 copy-start.9
  12.9 0.7 copy-start.10
  19.2 0.6 copy-start.3
  42.2 11.5 %all-to-all-start.1 = ((bf16[32,24,128]{2,1,0:T(8,128)(2,1)}), bf16[32,24,128]{2,1,0:T(8,128)(2,1)S(1)}, u32[]{:S(2)}, u32[]{:S(2)}) async-start(bf16[32,24,128]{2,1,0:T(8,128)(2,1)} %get-tuple-element.26), calls=%async_computation.1 | async-start | bytes 393216 | tf_op jit(solution)/shard_map/all_to_all | solution.py:286
  53.8 0.7 copy-start.1
  56.1 2.7 %copy-start.4 = (bf16[128,512]{1,0:T(8,128)(2,1)S(1)}, bf16[128,512]{1,0:T(8,128)(2,1)}, u32[]{:S(2)}) copy-start(bf16[128,512]{1,0:T(8,128)(2,1)} %emb_ref.1) | copy-start | bytes 393220
  56.1 11.7 %all-to-all-start.2 = ((bf16[32,24,128]{2,1,0:T(8,128)(2,1)}), bf16[32,24,128]{2,1,0:T(8,128)(2,1)S(1)}, u32[]{:S(2)}, u32[]{:S(2)}) async-start(bf16[32,24,128]{2,1,0:T(8,128)(2,1)} %total.1), calls=%async_computation.2 | async-start | bytes 393216 | tf_op jit(solution)/shard_map/all_to_all | solution.py:286
  67.8 0.9 copy-start.2
  68.6 18.9 %all-to-all-start.3 = ((bf16[8,128,256]{2,1,0:T(8,128)(2,1)}), bf16[8,128,256]{2,1,0:T(8,128)(2,1)S(1)}, u32[]{:S(2)}, u32[]{:S(2)}) async-start(bf16[8,128,256]{2,1,0:T(8,128)(2,1)} %broadcast_in_dim.2), calls=%async_computation.3 | async-start | bytes 1048576 | tf_op jit(solution)/shard_map/all_to_all | solution.py:286
  87.5 0.8 copy-start
  90.4 2.2 %collective-permute-start = (f32[64,256]{1,0:T(8,128)}, f32[64,256]{1,0:T(8,128)S(1)}, u32[]{:S(2)}, u32[]{:S(2)}) collective-permute-start(f32[64,256]{1,0:T(8,128)} %get-tuple-element.29.own_ref), channel_id=1, source_target_pairs={{0,1},{1,0},{2,3},{3,2},{4,5},{5,4},{6,7},{7,6},{8,9},{9,8},{10,11... | collective-permute-start | bytes 196616 | tf_op jit(solution)/shard_map/ppermute | solution.py:354
  90.5 1.5 %copy-start.8 = (f32[32,4]{1,0:T(8,128)S(1)}, f32[32,4]{1,0:T(8,128)}, u32[]{:S(2)}) copy-start(f32[32,4]{1,0:T(8,128)} %get-tuple-element.43) | copy-start | bytes 1540
  92.6 0.6 copy-start.6
  95.1 1.7 %copy-start.5 = (f32[512,32]{1,0:T(8,128)S(1)}, f32[512,32]{1,0:T(8,128)}, u32[]{:S(2)}) copy-start(f32[512,32]{1,0:T(8,128)} %get-tuple-element.39) | copy-start | bytes 196612

commit v2 on v1

--- a/solution.py
+++ b/solution.py
@@ -1,3 +1,4 @@
+import functools
 import math
 
 import jax
@@ -7,12 +8,14 @@
 from jax.experimental.pallas import tpu as pltpu
 from jax.sharding import PartitionSpec as P
 
+
 BF = jnp.bfloat16
 F32 = jnp.float32
 CURVE = math.sqrt(2.0 / math.pi)
 CUBIC = 0.044715 * CURVE
 GROUP = 8
 HALVES = 2
+SMALL = 1 << 20
 NT = (((1,), (1,)), ((), ()))
 NN = (((1,), (0,)), ((), ()))
 
@@ -47,21 +50,26 @@
     return jnp.sum(jnp.where(eye(count), jnp.broadcast_to(col, (count, count)), 0.0), axis=0, keepdims=True)
 
 
-def project_kernel(emb_ref, wl_ref, wr_ref, flags_ref, left_ref, send_ref):
-    channels = wl_ref.shape[1]
+def project_kernel(emb_ref, wl_ref, wr_ref, flags_ref, left_ref, send_ref, share_ref):
     emb = emb_ref[...]
     bins = emb.shape[0]
-    pad = jnp.zeros((bins, bins - 2 * channels), F32)
-    both = jnp.concatenate([mm(emb, wl_ref[...]), mm(emb, wr_ref[...]), pad], axis=1).T
-    left_ref[...] = both[:channels].astype(BF)
+    left_ref[...] = mm(wl_ref[...], emb, NT).astype(BF)
     flags = jnp.broadcast_to(flags_ref[...].astype(F32), (GROUP, bins))
-    piece = jnp.concatenate([both[channels : 2 * channels], flags], axis=0).astype(BF)
-    for row in range(send_ref.shape[0]):
+    piece = jnp.concatenate([mm(wr_ref[...], emb, NT), flags], axis=0).astype(BF)
+    width = share_ref.shape[2]
+    start = pl.multiple_of(lax.rem(lax.axis_index("band"), HALVES) * width, width)
+    share = emb_ref[:, pl.ds(start, width)]
+
+    def body(row, carry):
         send_ref[row] = piece
+        share_ref[row] = share
+        return carry
+
+    lax.fori_loop(0, send_ref.shape[0], body, 0, unroll=send_ref.shape[0] <= 8)
 
 
 def tile_kernel(
-    info_ref,
+    offset_ref,
     left_ref,
     recv_ref,
     flags_ref,
@@ -85,23 +93,24 @@
 ):
     channels, hidden = w_in_ref.shape
     tile = target_ref.shape[0]
-    noff = bias_ref.shape[1]
+    noff = bias_ref.shape[0]
     rows = recv_ref.shape[0]
     bands = send_ref.shape[0] // rows
     part = 2 * channels // bands
-    here, offset = info_ref[0], info_ref[1]
+    here, offset = lax.axis_index("rows"), offset_ref[0, 0]
     there = here + offset
     inside = (there < rows).astype(F32)
     piece = recv_ref[jnp.minimum(there, rows - 1)].astype(F32) * inside
     right = piece[:channels]
     col_flags = piece[channels : channels + 1] * (1.0 / (noff * tile))
     left = left_ref[...].astype(F32)
-    lane_off = lax.broadcasted_iota(jnp.int32, (channels, noff), 1)
-    bias = jnp.sum(jnp.where(lane_off == offset, bias_ref[...], 0.0), axis=1, keepdims=True)
+    off_row = lax.broadcasted_iota(jnp.int32, (noff, channels), 0)
+    bias = to_col(jnp.sum(jnp.where(off_row == offset, bias_ref[...], 0.0), axis=0, keepdims=True))
     head_row = w_head_ref[...]
     head = to_col(head_row)
-    gain = jnp.sum(w_out_ref[...].astype(F32) * head_row, axis=1, keepdims=True) * 0.5
-    gain_row = to_row(gain)
+    w_out_t = w_out_ref[...].astype(F32)
+    gain_row = jnp.sum(w_out_t * head, axis=0, keepdims=True) * 0.5
+    gain = to_col(gain_row)
     logit_col_ref[...] = to_col(jnp.sum((left + bias) * head, axis=0, keepdims=True))
     logit_row = jnp.sum(right * head, axis=0, keepdims=True)
     flag_col_ref[...] = to_col(flags_ref[...].astype(F32))
@@ -175,7 +184,6 @@
     in_term = (
         mm_wide(left_low, row_part) + mm_wide(right_low, col_part, NT) + bias * jnp.sum(row_part, axis=0, keepdims=True)
     )
-    w_out_t = w_out_ref[...].astype(F32).T
     head_term = jnp.sum(left * res_row + right * res_col + w_out_t * act_sum, axis=1, keepdims=True) + bias * res_all
     bias_sum = jnp.sum(row_sums, axis=1, keepdims=True)
     wide = jnp.zeros((channels, hidden), F32)
@@ -204,28 +212,25 @@
             ].astype(BF)
 
 
-def total_kernel(info_ref, recv_ref, send_ref):
-    devices, height, width = recv_ref.shape
-    total = recv_ref[0].astype(F32)
-    for source in range(1, devices):
-        total = total + recv_ref[source].astype(F32)
+def total_kernel(owners, recv_ref, send_ref):
+    _, height, width = recv_ref.shape
+    total = jnp.sum(recv_ref[...].astype(F32), axis=0)
+    index = lax.axis_index("rows") * lax.axis_size("band") + lax.axis_index("band")
     low = total - total.astype(BF).astype(F32)
     row = lax.broadcasted_iota(jnp.int32, (height, width), 0)
-    use_low = jnp.logical_and(info_ref[0] == 2, row >= height - GROUP)
-    piece = jnp.where(use_low, low, total).astype(BF)
-    for target in range(devices):
-        send_ref[target] = piece
+    third = jnp.logical_and(index >= 2 * owners, index < 3 * owners)
+    use_low = jnp.logical_and(third, row >= height - GROUP)
+    send_ref[...] = jnp.broadcast_to(jnp.where(use_low, low, total).astype(BF)[None], send_ref.shape)
 
 
 def finish_kernel(
-    info_ref, recv_ref, emb_ref, wl_ref, wr_ref, w_head_ref, share_ref, grad_emb_ref, in_ref, out_ref, head_ref, bias_ref
+    recv_ref, emb_ref, wl_ref, wr_ref, w_head_ref, share_ref, grad_emb_ref, in_ref, out_ref, head_ref, bias_ref
 ):
     rows = emb_ref.shape[0]
     devices, height, width = recv_ref.shape
     bands = devices // rows
     part = height - GROUP
     channels = in_ref.shape[0]
-    hidden = out_ref.shape[0]
 
     def grads(row):
         return jnp.concatenate([recv_ref[row * bands + band, :part, :].astype(F32) for band in range(bands)], axis=0)
@@ -234,10 +239,10 @@
         return total + mm(grads(row).astype(BF), emb_ref[row])
 
     share_ref[...] = lax.fori_loop(0, rows, body, jnp.zeros(share_ref.shape, F32), unroll=rows <= 8)
-    own = grads(info_ref[0]).astype(BF)
-    share = pl.ds(pl.multiple_of(info_ref[1] * width, width), width)
-    weights = jnp.concatenate([wl_ref[share, :].astype(F32), wr_ref[share, :].astype(F32)], axis=1).astype(BF)
-    grad_emb_ref[...] = mm(weights, own).T.astype(BF)
+    own = grads(lax.axis_index("rows")).T.astype(BF)
+    share = pl.ds(pl.multiple_of(lax.axis_index("band") * width, width), width)
+    weights = jnp.concatenate([wl_ref[:, share], wr_ref[:, share]], axis=0)
+    grad_emb_ref[...] = mm(own, weights).astype(BF)
     owners = channels // GROUP + 1
     small = [
         recv_ref[block, part:, :].astype(F32)
@@ -247,20 +252,19 @@
     ]
     in_ref[...] = jnp.concatenate(small[:-1], axis=0)
     last = small[-1]
-    turned = jnp.concatenate([last, jnp.zeros((hidden - GROUP, hidden), F32)], axis=0).T
-    out_ref[...] = turned[:, :1] * w_head_ref[...]
+    out_ref[...] = last[:1] * to_col(w_head_ref[...])
     head_ref[...] = last[1:2, :channels]
-    bias_ref[...] = turned[:channels, 2 : 2 + bias_ref.shape[1]]
-
-
-def arrange_kernel(info_ref, own_ref, other_ref, left_ref, right_ref):
-    channels = left_ref.shape[1]
+    bias_ref[...] = last[2 : 2 + bias_ref.shape[0], :channels]
+
+
+def arrange_kernel(own_ref, other_ref, left_ref, right_ref):
+    channels = left_ref.shape[0]
     width = own_ref.shape[1]
-    for ref, index in ((own_ref, info_ref[0]), (other_ref, 1 - info_ref[0])):
-        turned = ref[...].T
+    half = lax.rem(lax.axis_index("band"), HALVES)
+    for ref, index in ((own_ref, half), (other_ref, 1 - half)):
         place = pl.ds(pl.multiple_of(index * width, width), width)
-        left_ref[place, :] = turned[:, :channels]
-        right_ref[place, :] = turned[:, channels:]
+        left_ref[:, place] = ref[:channels]
+        right_ref[:, place] = ref[channels:]
 
 
 def vmem():
@@ -271,15 +275,24 @@
     return pl.BlockSpec(memory_space=pltpu.SMEM)
 
 
-def call(kernel, outs, ins, scratch=(), name=None):
+def fits(shape, kind):
+    return math.prod(shape) * jnp.dtype(kind).itemsize <= SMALL
+
+
+def near(value):
+    return pltpu.with_memory_space_constraint(value, pltpu.VMEM) if fits(value.shape, value.dtype) else value
+
+
+def call(kernel, outs, args, first=None, scratch=()):
     return pl.pallas_call(
         kernel,
-        out_shape=[jax.ShapeDtypeStruct(shape, kind) for shape, kind in outs],
-        in_specs=ins,
+        out_shape=[
+            pltpu.VMEM(shape, kind) if inner and fits(shape, kind) else jax.ShapeDtypeStruct(shape, kind) for shape, kind, inner in outs
+        ],
+        in_specs=[first or vmem()] + [vmem()] * (len(args) - 1),
         out_specs=[vmem()] * len(outs),
         scratch_shapes=[pltpu.VMEM(shape, kind) for shape, kind in scratch],
-        name=name,
-    )
+    )(*args)
 
 
 def exchange(value, axes):
@@ -295,28 +308,22 @@
     part = 2 * channels // bands
     owners = channels // GROUP + 1
     half = features // HALVES
-    row_index, band_index = lax.axis_index("rows"), lax.axis_index("band")
-    device_index = row_index * bands + band_index
-    half_index = band_index % HALVES
     flags = valid_bins.reshape(1, bins)
     head_row = w_head.reshape(1, channels)
 
-    left, send = call(
+    left, send, share = call(
         project_kernel,
-        [((channels, bins), BF), ((rows, channels + GROUP, bins), BF)],
-        [vmem()] * 4,
-        name="project",
-    )(embedding, w_left, w_right, flags)
+        [((channels, bins), BF, True), ((rows, channels + GROUP, bins), BF, True), ((rows, bins, half), BF, True)],
+        (embedding, w_left.T, w_right.T, flags),
+    )
     received = exchange(send, "rows")
-    embedding, received = lax.optimization_barrier((embedding, received))
-    emb_half = lax.dynamic_slice_in_dim(embedding, half_index * half, half, 1)
-    emb_all = exchange(jnp.broadcast_to(emb_half[None], (rows, bins, half)), "rows")
-
-    info = jnp.stack([row_index, offsets[0, 0]]).astype(jnp.int32)
+    share, received = lax.optimization_barrier((share, received))
+    emb_all = exchange(share, "rows")
     predicted, send = call(
         tile_kernel,
-        [((tile, tile), BF), ((devices, part + GROUP, tile), BF)],
-        [smem()] + [vmem()] * 8,
+        [((tile, tile), BF, False), ((devices, part + GROUP, tile), BF, True)],
+        (offsets, near(left), near(received), flags, target.reshape(tile, tile), w_in, w_out.T, head_row, dist_bias.T),
+        smem(),
         [
             ((tile, tile), F32),
             ((GROUP, hidden, tile), BF),
@@ -329,44 +336,34 @@
             ((tile, 1), F32),
             ((tile, 1), F32),
         ],
-        name="tile",
-    )(info, left, received, flags, target.reshape(tile, tile), w_in, w_out, head_row, dist_bias)
+    )
+    send, emb_all = lax.optimization_barrier((send, emb_all))
     partial = exchange(send, ("rows", "band"))
-    group = (device_index // owners).astype(jnp.int32).reshape(1)
-    (send,) = call(
-        total_kernel, [(partial.shape, BF)], [smem(), vmem()], name="total"
-    )(group, partial)
+    (send,) = call(functools.partial(total_kernel, owners), [(partial.shape, BF, True)], (near(partial),))
     complete = exchange(send, ("rows", "band"))
-    place = jnp.stack([row_index, band_index]).astype(jnp.int32)
-    share, grad_embedding, grad_in, grad_out, grad_head, grad_bias = call(
+    mine, grad_embedding, grad_in, grad_out, grad_head, grad_bias = call(
         finish_kernel,
         [
-            ((2 * channels, half), F32),
-            ((bins, features // bands), BF),
-            ((channels, hidden), F32),
-            ((hidden, channels), F32),
-            ((1, channels), F32),
-            (dist_bias.shape, F32),
+            ((2 * channels, half), F32, True),
+            ((bins, features // bands), BF, False),
+            ((channels, hidden), F32, False),
+            ((channels, hidden), F32, False),
+            ((1, channels), F32, False),
+            (dist_bias.shape[::-1], F32, False),
         ],
-        [smem()] + [vmem()] * 5,
-        name="finish",
-    )(place, complete, emb_all, w_left, w_right, head_row)
-    other = lax.ppermute(share, "band", [(source, source ^ 1) for source in range(bands)])
-    grad_left, grad_right = call(
-        arrange_kernel,
-        [(w_left.shape, F32), (w_right.shape, F32)],
-        [smem(), vmem(), vmem()],
-        name="arrange",
-    )(half_index.astype(jnp.int32).reshape(1), share, other)
+        (near(complete), near(emb_all), w_left.T, w_right.T, head_row),
+    )
+    other = lax.ppermute(mine, "band", [(source, source ^ 1) for source in range(bands)])
+    grad_left, grad_right = call(arrange_kernel, [((channels, features), F32, False)] * 2, (near(mine), near(other)))
     return (
         predicted.reshape(target.shape),
         grad_embedding,
-        grad_left,
-        grad_right,
+        grad_left.T,
+        grad_right.T,
         grad_in,
-        grad_out,
+        grad_out.T,
         grad_head.reshape(channels),
-        grad_bias,
+        grad_bias.T,
     )
 
 
@@ -383,6 +380,7 @@
         P("rows"),
         P("rows", "band", None, None),
     )
+
     return jax.shard_map(
         on_device,
         mesh=mesh,

time: 98.3 us -> 73.2 us (0.74)
  blocking collectives: 0 us -> 40.2 us
  waiting for transfers between devices: 36.9 us -> 0.9 us
  starting transfers between devices: 16.1 us -> 4 us
  local copies, waits for them, and re-layouts: 12 us -> 0 us
  Pallas kernels: 30 us -> 26.3 us
  other arithmetic: 1.17 us -> 0 us
    all_to_all x0 -> x3, blocking collectives: none -> 40.2 us  [exchange(): return lax.all_to_all(value, axes, 0, 0, tiled=True)]
    all_to_all x4 -> x1, waiting for transfers between devices: 36.9 us -> 0.01 us  [exchange(): return lax.all_to_all(value, axes, 0, 0, tiled=True)]
    all_to_all x4 -> x1, starting transfers between devices: 16.1 us -> 3.49 us  [exchange(): return lax.all_to_all(value, axes, 0, 0, tiled=True)]
    unnamed x30 -> x0, local copies, waits for them, and re-layouts: 11.1 us -> none
    pallas_call x5, Pallas kernels: 30 us -> 26.3 us  [call(): pl.pallas_call(kernel, out_shape=[pltpu.VMEM(shape, kind) if inner and fi...]
    another operation x2 -> x0, other arithmetic: 1.17 us -> none  [the longest x1 0.59 us: on_device(): place = jnp.stack([row_index, band_index]).astype(jnp.int32)]
  transfers between devices with their start and end apart: 5 -> 2, of which waited for: 4 -> 1; matrix products, arithmetic and copies ran while one was open for 5% -> 0% of each run, Pallas kernels for 0% -> 31%
where the time goes in v2:
time: 73.2 us; the launch traced here: 72.7 us
  blocking collectives  40.2 us (55%)
  Pallas kernels  26.3 us (36%)
  starting transfers between devices  4 us (5%)
  between operations  1.3 us (2%)
  waiting for transfers between devices  0.9 us (1%)
    all_to_all x3, blocking collectives, exchange(): return lax.all_to_all(value, axes, 0, 0, tiled=True)  40.2 us
    pallas_call x5, Pallas kernels, call(): pl.pallas_call(kernel, out_shape=[pltpu.VMEM(shape, kind) if inner and fi...  26.3 us
    all_to_all x1, starting transfers between devices, exchange(): return lax.all_to_all(value, axes, 0, 0, tiled=True)  3.49 us
  transfers between devices with their start and end apart: 2, of which 1 were waited for; matrix products, arithmetic and copies ran while one was open for 0% of the time, Pallas kernels for 31%

profile of v2, /device:TPU:0, one launch (start us, length us, event | category | flops | bytes accessed | tf_op | source)
XLA Modules:
  0.0 72.7 jit_solution(13124367204721582791)
XLA Ops:
  0.6 1.8 %shard_map.161 = (bf16[32,128]{1,0:T(8,128)(2,1)S(1)}, bf16[8,40,128]{2,1,0:T(8,128)(2,1)S(1)}, bf16[8,128,256]{2,1,0:T(8,128)(2,1)}) custom-call(bf16[128,512]{1,0:T(8,128)(2,1)} %emb_ref.1, bf16[32,512]{1,0:T(8,128)(2,1)} %bitcast.13, bf16[32,512]{1,0:T(8,128)(2,1)} %bitcast.15, s32[1,128]{1,0:T(1,128)} %bitcast.20), custom_call_target="tpu_custom_call" | custom-call | tf_op jit(solution)/shard_map/pallas_call | solution.py:287
  2.4 14.1 %all_to_all.20.recv_ref = bf16[8,40,128]{2,1,0:T(8,128)(2,1)S(1)} all-to-all(bf16[8,40,128]{2,1,0:T(8,128)(2,1)S(1)} %get-tuple-element.27), channel_id=1, replica_groups=mesh['rows'=8,'band'=4] {'rows'}, dimensions={0} | all-to-all | bytes 163840 | tf_op jit(solution)/shard_map/all_to_all | solution.py:299
  16.5 3.5 %all-to-all-start.1 = ((bf16[8,128,256]{2,1,0:T(8,128)(2,1)}), bf16[8,128,256]{2,1,0:T(8,128)(2,1)S(1)}, u32[]{:S(2)}, u32[]{:S(2)}) async-start(bf16[8,128,256]{2,1,0:T(8,128)(2,1)} %get-tuple-element.31), calls=%async_computation.1 | async-start | bytes 1048576 | tf_op jit(solution)/shard_map/all_to_all | solution.py:299
  20.7 22.2 %shard_map.162 = (bf16[128,128]{1,0:T(8,128)(2,1)}, bf16[32,24,128]{2,1,0:T(8,128)(2,1)S(1)}) custom-call(s32[1,1]{1,0:T(1,128)S(6)} %copy.18.offset_ref, bf16[32,128]{1,0:T(8,128)(2,1)S(1)} %get-tuple-element.25.left_ref, bf16[8,40,128]{2,1,0:T(8,128)(2,1)S(1)} %all_to_all.20.recv_ref, s32[1,128]{1,0:T(1,128)} %bitcast.21, bf16[128,128]{1,0:T(8,128)(2,1)} %bitcast.17, ...), custom_call_target="tpu_custom_call" | custom-call | tf_op jit(solution)/shard_map/pallas_call | solution.py:287
  42.9 0.0 all-to-all-done.1.emb_ref
  42.9 14.7 %all_to_all.21.recv_ref = bf16[32,24,128]{2,1,0:T(8,128)(2,1)S(1)} all-to-all(bf16[32,24,128]{2,1,0:T(8,128)(2,1)S(1)} %get-tuple-element.32), channel_id=1, replica_groups=mesh['rows'=8,'band'=4] {'rows','band'}, dimensions={0} | all-to-all | bytes 393216 | tf_op jit(solution)/shard_map/all_to_all | solution.py:299
  57.6 11.4 %all_to_all.22.recv_ref = bf16[32,24,128]{2,1,0:T(8,128)(2,1)S(1)} all-to-all(bf16[32,24,128]{2,1,0:T(8,128)(2,1)S(1)} %shard_map.163), channel_id=1, replica_groups=mesh['rows'=8,'band'=4] {'rows','band'}, dimensions={0} | all-to-all | bytes 393216 | tf_op jit(solution)/shard_map/all_to_all | solution.py:299
  69.0 1.6 %shard_map.164 = (f32[64,256]{1,0:T(8,128)S(1)}, bf16[128,128]{1,0:T(8,128)(2,1)}, f32[32,128]{1,0:T(8,128)}, f32[32,128]{1,0:T(8,128)}, f32[1,32]{1,0:T(1,128)}, /*index=5*/f32[4,32]{1,0:T(4,128)}) custom-call(bf16[32,24,128]{2,1,0:T(8,128)(2,1)S(1)} %all_to_all.22.recv_ref, bf16[8,128,256]{2,1,0:T(8,128)(2,1)S(1)} %all-to-all-done.1.emb_ref, ...), custom_call_target="tpu_custom_call" | custom-call | tf_op jit(solution)/shard_map/pallas_call | solution.py:287
  70.6 0.5 collective-permute-start
  71.2 0.9 %collective-permute-done.other_ref = f32[64,256]{1,0:T(8,128)S(1)} collective-permute-done((f32[64,256]{1,0:T(8,128)S(1)}, f32[64,256]{1,0:T(8,128)S(1)}, u32[]{:S(2)}, u32[]{:S(2)}) %collective-permute-start) | collective-permute-done | bytes 65568 | tf_op jit(solution)/shard_map/ppermute | solution.py:356
  72.1 0.7 shard_map.165
  (1 shorter events, 0.0 us)
Async XLA Ops:
  16.5 26.3 %all-to-all-start.1 = ((bf16[8,128,256]{2,1,0:T(8,128)(2,1)}), bf16[8,128,256]{2,1,0:T(8,128)(2,1)S(1)}, u32[]{:S(2)}, u32[]{:S(2)}) async-start(bf16[8,128,256]{2,1,0:T(8,128)(2,1)} %get-tuple-element.31), calls=%async_computation.1 | async-start | bytes 1048576 | tf_op jit(solution)/shard_map/all_to_all | solution.py:299
  70.6 1.4 %collective-permute-start = (f32[64,256]{1,0:T(8,128)S(1)}, f32[64,256]{1,0:T(8,128)S(1)}, u32[]{:S(2)}, u32[]{:S(2)}) collective-permute-start(f32[64,256]{1,0:T(8,128)S(1)} %get-tuple-element.35.own_ref), channel_id=1, source_target_pairs={{0,1},{1,0},{2,3},{3,2},{4,5},{5,4},{6,7},{7,6},{8,9},{9,8},{10,11... | collective-permute-start | bytes 196616 | tf_op jit(solution)/shard_map/ppermute | solution.py:356

commit v3 on v2

--- a/solution.py
+++ b/solution.py
@@ -12,7 +12,8 @@
 BF = jnp.bfloat16
 F32 = jnp.float32
 CURVE = math.sqrt(2.0 / math.pi)
-CUBIC = 0.044715 * CURVE
+STRETCH = (0.044715 * CURVE) ** (1.0 / 3.0)
+LINEAR = CURVE / STRETCH
 GROUP = 8
 HALVES = 2
 SMALL = 1 << 20
@@ -85,9 +86,10 @@
     slope_ref,
     logit_ref,
     res_ref,
-    row_ref,
     col_ref,
-    act_sum_ref,
+    product_ref,
+    pick_ref,
+    sums_ref,
     logit_col_ref,
     flag_col_ref,
 ):
@@ -109,80 +111,115 @@
     head_row = w_head_ref[...]
     head = to_col(head_row)
     w_out_t = w_out_ref[...].astype(F32)
-    gain_row = jnp.sum(w_out_t * head, axis=0, keepdims=True) * 0.5
-    gain = to_col(gain_row)
+    gain_row = jnp.sum(w_out_t * head, axis=0, keepdims=True)
+    gain = to_col(gain_row) * 0.5
+    gain_row = gain_row * (0.5 / STRETCH)
     logit_col_ref[...] = to_col(jnp.sum((left + bias) * head, axis=0, keepdims=True))
     logit_row = jnp.sum(right * head, axis=0, keepdims=True)
     flag_col_ref[...] = to_col(flags_ref[...].astype(F32))
     target_wide[...] = target_ref[...].astype(F32)
     shifted = right + bias
     w_in = w_in_ref[...]
-    w_in_t = w_in.astype(F32).T.astype(BF)
-    gain_a, rest = gain_row.astype(BF), gain_row - gain_row.astype(BF).astype(F32)
-    gain_b = rest.astype(BF)
-    gain_c = (rest - gain_b.astype(F32)).astype(BF)
+    w_high, w_low = split(w_in.astype(F32).T * STRETCH)
+    w_both = jnp.concatenate([w_high, w_low], axis=1)
+    gain_high = gain_row.astype(BF).astype(F32)
+    gain_low = gain_row - gain_high
     group_row = lax.broadcasted_iota(jnp.int32, (GROUP, 1), 0)
     gain_parts = [
-        jnp.concatenate(
-            [jnp.where(group_row == step, part_of.astype(F32), 0.0) for part_of in (gain_a, gain_b, gain_c)], axis=0
-        ).astype(BF)
+        jnp.concatenate([jnp.where(group_row == step, piece, 0.0) for piece in (gain_high, gain_low)], axis=0).astype(BF)
         for step in range(GROUP)
     ]
     col_ref[...] = jnp.zeros_like(col_ref)
-    act_sum_ref[...] = jnp.zeros_like(act_sum_ref)
+    chosen = lax.broadcasted_iota(jnp.int32, pick_ref.shape, 0) // tile
+    lane_of = lax.broadcasted_iota(jnp.int32, pick_ref.shape, 1)
+    pick_ref[...] = jnp.where(jnp.minimum(chosen, GROUP) == lane_of, 1.0, 0.0).astype(BF)
+    groups = tile // GROUP
+
+    def start_of(group):
+        return pl.multiple_of(group * GROUP, GROUP)
+
+    def turn(group):
+        return pltpu.roll(left, lax.rem(tile - start_of(group), tile), 1)
+
+    def forward(turned, step, slot, logits):
+        pair_in = (turned[:, step : step + 1] + shifted).astype(BF)
+        x = mm(w_both, jnp.concatenate([pair_in, pair_in], axis=0))
+        square = x * x
+        inner = square + LINEAR
+        bend = jnp.tanh(x * inner)
+        lift = 1.0 + bend
+        act = x * lift
+        slope_ref[slot, step] = lift + (act * (1.0 - bend)) * (inner + (square + square))
+        act = act.astype(BF)
+        act_ref[slot, step] = act
+        return logits + mm(gain_parts[step], act)
+
+    def settle(group, logits):
+        at = pl.ds(start_of(group), GROUP)
+        logits = logits[:GROUP] + logits[GROUP:]
+        logits = logits + logit_col_ref[at, :] + logit_row
+        logit_ref[at, :] = logits
+        res_ref[at, :] = flag_col_ref[at, :] * col_flags * (logits - target_wide[at, :])
+
+    def backward(res, res_low, step, slot, total):
+        product = slope_ref[slot, step] * res[step : step + 1]
+        product_ref[slot, :, step * tile : (step + 1) * tile] = product.astype(BF)
+        product_ref[slot, :, (GROUP + step) * tile : (GROUP + step + 1) * tile] = (
+            act_ref[slot, step] * res_low[step : step + 1]
+        )
+        return total + product
+
+    def none():
+        return jnp.zeros((2 * GROUP, tile), F32)
+
+    logits = none()
+    turned = turn(0)
+    for step in range(GROUP):
+        logits = forward(turned, step, 0, logits)
+    settle(0, logits)
 
     def body(index, carry):
-        start = pl.multiple_of(index * GROUP, GROUP)
-        turned = pltpu.roll(left, (tile - start) % tile, 1)
-        logits = jnp.zeros((3 * GROUP, tile), F32)
-        for step in range(GROUP):
-            pair_in = (turned[:, step : step + 1] + shifted).astype(BF)
-            x = mm(w_in_t, pair_in)
-            inner = CURVE + CUBIC * (x * x)
-            bend = jnp.tanh(x * inner)
-            lift = 1.0 + bend
-            act = (x * lift).astype(BF)
-            slope_ref[step] = lift + (1.0 - bend * bend) * (x * (3.0 * inner - 2.0 * CURVE))
-            act_ref[step] = act
-            logits = logits + mm(gain_parts[step], act)
-        logits = logits[:GROUP] + logits[GROUP : 2 * GROUP] + logits[2 * GROUP :]
-        logits = logits + logit_col_ref[pl.ds(start, GROUP), :] + logit_row
-        logit_ref[pl.ds(start, GROUP), :] = logits
-        mask = flag_col_ref[pl.ds(start, GROUP), :] * col_flags
-        res = mask * (logits - target_wide[pl.ds(start, GROUP), :])
-        res_ref[pl.ds(start, GROUP), :] = res
-        high = res.astype(BF).astype(F32)
-        low = res - high
-        grow = jnp.zeros((2 * GROUP, hidden), F32)
-        acts = jnp.zeros((2 * GROUP, hidden), F32)
-        total = col_ref[...]
-        for step in range(GROUP):
-            slope = slope_ref[step]
-            keep = group_row == step
-            lhs = jnp.concatenate([jnp.where(keep, high, 0.0), jnp.where(keep, low, 0.0)], axis=0).astype(BF)
-            grow = grow + mm(lhs, slope.astype(BF), NT)
-            acts = acts + mm(lhs, act_ref[step], NT)
-            total = total + slope * res[step : step + 1]
-        col_ref[...] = total
-        row_ref[pl.ds(start, GROUP), :] = grow[:GROUP] + grow[GROUP:]
-        act_sum_ref[...] += acts
+        for slot in range(2):
+            group = 2 * index + slot
+            following = lax.rem(group + 1, groups)
+            at = pl.ds(start_of(group), GROUP)
+            res = res_ref[at, :]
+            res_low = res.astype(BF)
+            total = col_ref[...]
+            turned = turn(following)
+            logits = none()
+            for step in range(GROUP):
+                logits = forward(turned, step, 1 - slot, logits)
+                total = backward(res, res_low, step, slot, total)
+            col_ref[...] = total
+            sums_ref[group] = mm(product_ref[slot], pick_ref[...])
+            settle(following, logits)
         return carry
 
-    lax.fori_loop(0, tile // GROUP, body, 0)
+    lax.fori_loop(0, groups // 2, body, 0)
 
     pred_ref[...] = logit_ref[...].astype(BF)
     res = res_ref[...]
     res_col = jnp.sum(res, axis=0, keepdims=True)
     res_row = to_row(jnp.sum(res, axis=1, keepdims=True))
     res_all = jnp.sum(res_row, axis=1, keepdims=True)
-    row_part = row_ref[...] * gain_row
+    row_sum = jnp.zeros((hidden, tile), F32)
+    act_sum = jnp.zeros((hidden, tile), F32)
+    lane = lax.broadcasted_iota(jnp.int32, (hidden, tile), 1)
+    for group in range(groups):
+        sums = sums_ref[group]
+        act_sum = act_sum + sums
+        moved = pltpu.roll(sums, group * GROUP, 1) if group else sums
+        row_sum = jnp.where(lane // GROUP == group, moved, row_sum)
+    row_part = row_sum * gain
+    act_sum = jnp.sum(jnp.where(lane == GROUP, act_sum, 0.0), axis=1, keepdims=True) * (0.5 / STRETCH)
+    act_sum = to_row(act_sum)
     col_part = col_ref[...] * gain
-    act_sum = jnp.sum(act_sum_ref[...], axis=0, keepdims=True) * 0.5
-    row_sums = head * res_row + mm_wide(w_in, row_part, NT)
+    row_sums = head * res_row + mm_wide(w_in, row_part)
     col_sums = head * res_col + mm_wide(w_in, col_part)
     left_low, right_low = left_ref[...], right.astype(BF)
     in_term = (
-        mm_wide(left_low, row_part) + mm_wide(right_low, col_part, NT) + bias * jnp.sum(row_part, axis=0, keepdims=True)
+        mm_wide(left_low, row_part, NT) + mm_wide(right_low, col_part, NT) + bias * to_row(jnp.sum(row_part, axis=1, keepdims=True))
     )
     head_term = jnp.sum(left * res_row + right * res_col + w_out_t * act_sum, axis=1, keepdims=True) + bias * res_all
     bias_sum = jnp.sum(row_sums, axis=1, keepdims=True)
@@ -326,13 +363,14 @@
         smem(),
         [
             ((tile, tile), F32),
-            ((GROUP, hidden, tile), BF),
-            ((GROUP, hidden, tile), F32),
+            ((2, GROUP, hidden, tile), BF),
+            ((2, GROUP, hidden, tile), F32),
             ((tile, tile), F32),
             ((tile, tile), F32),
-            ((tile, hidden), F32),
             ((hidden, tile), F32),
-            ((2 * GROUP, hidden), F32),
+            ((2, hidden, 2 * GROUP * tile), BF),
+            ((2 * GROUP * tile, tile), BF),
+            ((tile // GROUP, hidden, tile), F32),
             ((tile, 1), F32),
             ((tile, 1), F32),
         ],

time: 73.2 us -> 65 us (0.89)
  Pallas kernels: 26.3 us -> 18.2 us
    pallas_call x5, Pallas kernels: 26.3 us -> 18.2 us  [call(): pl.pallas_call(kernel, out_shape=[pltpu.VMEM(shape, kind) if inner and fi...]
  transfers between devices with their start and end apart: 2 -> 2, of which waited for: 1 -> 1; matrix products, arithmetic and copies ran while one was open for 0% -> 0% of each run, Pallas kernels for 31% -> 22%
where the time goes in v3:
time: 65 us; the launch traced here: 64.6 us
  blocking collectives  40.2 us (62%)
  Pallas kernels  18.2 us (28%)
  starting transfers between devices  4 us (6%)
  between operations  1.3 us (2%)
  waiting for transfers between devices  0.9 us (1%)
    all_to_all x3, blocking collectives, exchange(): return lax.all_to_all(value, axes, 0, 0, tiled=True)  40.2 us
    pallas_call x5, Pallas kernels, call(): pl.pallas_call(kernel, out_shape=[pltpu.VMEM(shape, kind) if inner and fi...  18.2 us
    all_to_all x1, starting transfers between devices, exchange(): return lax.all_to_all(value, axes, 0, 0, tiled=True)  3.49 us
  transfers between devices with their start and end apart: 2, of which 1 were waited for; matrix products, arithmetic and copies ran while one was open for 0% of the time, Pallas kernels for 22%

profile of v3, /device:TPU:0, one launch (start us, length us, event | category | flops | bytes accessed | tf_op | source)
XLA Modules:
  0.0 64.6 jit_solution(4125160869955828712)
XLA Ops:
  0.6 1.8 %shard_map.161 = (bf16[32,128]{1,0:T(8,128)(2,1)S(1)}, bf16[8,40,128]{2,1,0:T(8,128)(2,1)S(1)}, bf16[8,128,256]{2,1,0:T(8,128)(2,1)}) custom-call(bf16[128,512]{1,0:T(8,128)(2,1)} %emb_ref.1, bf16[32,512]{1,0:T(8,128)(2,1)} %bitcast.13, bf16[32,512]{1,0:T(8,128)(2,1)} %bitcast.15, s32[1,128]{1,0:T(1,128)} %bitcast.20), custom_call_target="tpu_custom_call" | custom-call | tf_op jit(solution)/shard_map/pallas_call | solution.py:324
  2.4 14.1 %all_to_all.20.recv_ref = bf16[8,40,128]{2,1,0:T(8,128)(2,1)S(1)} all-to-all(bf16[8,40,128]{2,1,0:T(8,128)(2,1)S(1)} %get-tuple-element.27), channel_id=1, replica_groups=mesh['rows'=8,'band'=4] {'rows'}, dimensions={0} | all-to-all | bytes 163840 | tf_op jit(solution)/shard_map/all_to_all | solution.py:336
  16.5 3.5 %all-to-all-start.1 = ((bf16[8,128,256]{2,1,0:T(8,128)(2,1)}), bf16[8,128,256]{2,1,0:T(8,128)(2,1)S(1)}, u32[]{:S(2)}, u32[]{:S(2)}) async-start(bf16[8,128,256]{2,1,0:T(8,128)(2,1)} %get-tuple-element.31), calls=%async_computation.1 | async-start | bytes 1048576 | tf_op jit(solution)/shard_map/all_to_all | solution.py:336
  20.7 14.0 %shard_map.162 = (bf16[128,128]{1,0:T(8,128)(2,1)}, bf16[32,24,128]{2,1,0:T(8,128)(2,1)S(1)}) custom-call(s32[1,1]{1,0:T(1,128)S(6)} %copy.18.offset_ref, bf16[32,128]{1,0:T(8,128)(2,1)S(1)} %get-tuple-element.25.left_ref, bf16[8,40,128]{2,1,0:T(8,128)(2,1)S(1)} %all_to_all.20.recv_ref, s32[1,128]{1,0:T(1,128)} %bitcast.21, bf16[128,128]{1,0:T(8,128)(2,1)} %bitcast.17, ...), custom_call_target="tpu_custom_call" | custom-call | tf_op jit(solution)/shard_map/pallas_call | solution.py:324
  34.7 0.0 all-to-all-done.1.emb_ref
  34.7 14.7 %all_to_all.21.recv_ref = bf16[32,24,128]{2,1,0:T(8,128)(2,1)S(1)} all-to-all(bf16[32,24,128]{2,1,0:T(8,128)(2,1)S(1)} %get-tuple-element.32), channel_id=1, replica_groups=mesh['rows'=8,'band'=4] {'rows','band'}, dimensions={0} | all-to-all | bytes 393216 | tf_op jit(solution)/shard_map/all_to_all | solution.py:336
  49.5 11.4 %all_to_all.22.recv_ref = bf16[32,24,128]{2,1,0:T(8,128)(2,1)S(1)} all-to-all(bf16[32,24,128]{2,1,0:T(8,128)(2,1)S(1)} %shard_map.163), channel_id=1, replica_groups=mesh['rows'=8,'band'=4] {'rows','band'}, dimensions={0} | all-to-all | bytes 393216 | tf_op jit(solution)/shard_map/all_to_all | solution.py:336
  60.8 1.6 %shard_map.164 = (f32[64,256]{1,0:T(8,128)S(1)}, bf16[128,128]{1,0:T(8,128)(2,1)}, f32[32,128]{1,0:T(8,128)}, f32[32,128]{1,0:T(8,128)}, f32[1,32]{1,0:T(1,128)}, /*index=5*/f32[4,32]{1,0:T(4,128)}) custom-call(bf16[32,24,128]{2,1,0:T(8,128)(2,1)S(1)} %all_to_all.22.recv_ref, bf16[8,128,256]{2,1,0:T(8,128)(2,1)S(1)} %all-to-all-done.1.emb_ref, ...), custom_call_target="tpu_custom_call" | custom-call | tf_op jit(solution)/shard_map/pallas_call | solution.py:324
  62.5 0.5 collective-permute-start
  63.0 0.9 %collective-permute-done.other_ref = f32[64,256]{1,0:T(8,128)S(1)} collective-permute-done((f32[64,256]{1,0:T(8,128)S(1)}, f32[64,256]{1,0:T(8,128)S(1)}, u32[]{:S(2)}, u32[]{:S(2)}) %collective-permute-start) | collective-permute-done | bytes 65568 | tf_op jit(solution)/shard_map/ppermute | solution.py:394
  63.9 0.7 %shard_map.165 = (f32[32,512]{1,0:T(8,128)}, f32[32,512]{1,0:T(8,128)}) custom-call(f32[64,256]{1,0:T(8,128)S(1)} %get-tuple-element.35.own_ref, f32[64,256]{1,0:T(8,128)S(1)} %collective-permute-done.other_ref), custom_call_target="tpu_custom_call" | custom-call | tf_op jit(solution)/shard_map/pallas_call | solution.py:324
  (1 shorter events, 0.0 us)
Async XLA Ops:
  16.5 18.2 %all-to-all-start.1 = ((bf16[8,128,256]{2,1,0:T(8,128)(2,1)}), bf16[8,128,256]{2,1,0:T(8,128)(2,1)S(1)}, u32[]{:S(2)}, u32[]{:S(2)}) async-start(bf16[8,128,256]{2,1,0:T(8,128)(2,1)} %get-tuple-element.31), calls=%async_computation.1 | async-start | bytes 1048576 | tf_op jit(solution)/shard_map/all_to_all | solution.py:336
  62.5 1.4 %collective-permute-start = (f32[64,256]{1,0:T(8,128)S(1)}, f32[64,256]{1,0:T(8,128)S(1)}, u32[]{:S(2)}, u32[]{:S(2)}) collective-permute-start(f32[64,256]{1,0:T(8,128)S(1)} %get-tuple-element.35.own_ref), channel_id=1, source_target_pairs={{0,1},{1,0},{2,3},{3,2},{4,5},{5,4},{6,7},{7,6},{8,9},{9,8},{10,11... | collective-permute-start | bytes 196616 | tf_op jit(solution)/shard_map/ppermute | solution.py:394

commit v4 on v3

--- a/solution.py
+++ b/solution.py
@@ -56,23 +56,22 @@
     bins = emb.shape[0]
     left_ref[...] = mm(wl_ref[...], emb, NT).astype(BF)
     flags = jnp.broadcast_to(flags_ref[...].astype(F32), (GROUP, bins))
-    piece = jnp.concatenate([mm(wr_ref[...], emb, NT), flags], axis=0).astype(BF)
+    send_ref[...] = jnp.concatenate([mm(wr_ref[...], emb, NT), flags], axis=0).astype(BF)
     width = share_ref.shape[2]
     start = pl.multiple_of(lax.rem(lax.axis_index("band"), HALVES) * width, width)
     share = emb_ref[:, pl.ds(start, width)]
 
     def body(row, carry):
-        send_ref[row] = piece
         share_ref[row] = share
         return carry
 
-    lax.fori_loop(0, send_ref.shape[0], body, 0, unroll=send_ref.shape[0] <= 8)
+    lax.fori_loop(0, share_ref.shape[0], body, 0, unroll=share_ref.shape[0] <= 8)
 
 
 def tile_kernel(
     offset_ref,
     left_ref,
-    recv_ref,
+    ahead_refs,
     flags_ref,
     target_ref,
     w_in_ref,
@@ -87,8 +86,7 @@
     logit_ref,
     res_ref,
     col_ref,
-    product_ref,
-    pick_ref,
+    act_sum_ref,
     sums_ref,
     logit_col_ref,
     flag_col_ref,
@@ -96,13 +94,13 @@
     channels, hidden = w_in_ref.shape
     tile = target_ref.shape[0]
     noff = bias_ref.shape[0]
-    rows = recv_ref.shape[0]
-    bands = send_ref.shape[0] // rows
+    rows, bands = lax.axis_size("rows"), lax.axis_size("band")
     part = 2 * channels // bands
     here, offset = lax.axis_index("rows"), offset_ref[0, 0]
     there = here + offset
-    inside = (there < rows).astype(F32)
-    piece = recv_ref[jnp.minimum(there, rows - 1)].astype(F32) * inside
+    piece = ahead_refs[0][...].astype(F32)
+    for step in range(1, noff):
+        piece = jnp.where(offset == step, ahead_refs[step][...].astype(F32), piece)
     right = piece[:channels]
     col_flags = piece[channels : channels + 1] * (1.0 / (noff * tile))
     left = left_ref[...].astype(F32)
@@ -130,9 +128,7 @@
         for step in range(GROUP)
     ]
     col_ref[...] = jnp.zeros_like(col_ref)
-    chosen = lax.broadcasted_iota(jnp.int32, pick_ref.shape, 0) // tile
-    lane_of = lax.broadcasted_iota(jnp.int32, pick_ref.shape, 1)
-    pick_ref[...] = jnp.where(jnp.minimum(chosen, GROUP) == lane_of, 1.0, 0.0).astype(BF)
+    act_sum_ref[...] = jnp.zeros_like(act_sum_ref)
     groups = tile // GROUP
 
     def start_of(group):
@@ -161,13 +157,11 @@
         logit_ref[at, :] = logits
         res_ref[at, :] = flag_col_ref[at, :] * col_flags * (logits - target_wide[at, :])
 
-    def backward(res, res_low, step, slot, total):
+    def backward(res, res_low, step, slot, group, total, acts):
         product = slope_ref[slot, step] * res[step : step + 1]
-        product_ref[slot, :, step * tile : (step + 1) * tile] = product.astype(BF)
-        product_ref[slot, :, (GROUP + step) * tile : (GROUP + step + 1) * tile] = (
-            act_ref[slot, step] * res_low[step : step + 1]
-        )
-        return total + product
+        sums_ref[group, :, step : step + 1] = jnp.sum(product, axis=1, keepdims=True)
+        weighted = act_ref[slot, step] * res_low[step : step + 1]
+        return total + product, acts + weighted.astype(F32)
 
     def none():
         return jnp.zeros((2 * GROUP, tile), F32)
@@ -185,14 +179,14 @@
             at = pl.ds(start_of(group), GROUP)
             res = res_ref[at, :]
             res_low = res.astype(BF)
-            total = col_ref[...]
+            total, acts = col_ref[...], act_sum_ref[...]
             turned = turn(following)
             logits = none()
             for step in range(GROUP):
                 logits = forward(turned, step, 1 - slot, logits)
-                total = backward(res, res_low, step, slot, total)
+                total, acts = backward(res, res_low, step, slot, group, total, acts)
             col_ref[...] = total
-            sums_ref[group] = mm(product_ref[slot], pick_ref[...])
+            act_sum_ref[...] = acts
             settle(following, logits)
         return carry
 
@@ -204,16 +198,12 @@
     res_row = to_row(jnp.sum(res, axis=1, keepdims=True))
     res_all = jnp.sum(res_row, axis=1, keepdims=True)
     row_sum = jnp.zeros((hidden, tile), F32)
-    act_sum = jnp.zeros((hidden, tile), F32)
     lane = lax.broadcasted_iota(jnp.int32, (hidden, tile), 1)
     for group in range(groups):
         sums = sums_ref[group]
-        act_sum = act_sum + sums
-        moved = pltpu.roll(sums, group * GROUP, 1) if group else sums
-        row_sum = jnp.where(lane // GROUP == group, moved, row_sum)
+        row_sum = jnp.where(lane // GROUP == group, pltpu.roll(sums, group * GROUP, 1) if group else sums, row_sum)
     row_part = row_sum * gain
-    act_sum = jnp.sum(jnp.where(lane == GROUP, act_sum, 0.0), axis=1, keepdims=True) * (0.5 / STRETCH)
-    act_sum = to_row(act_sum)
+    act_sum = to_row(jnp.sum(act_sum_ref[...], axis=1, keepdims=True) * (0.5 / STRETCH))
     col_part = col_ref[...] * gain
     row_sums = head * res_row + mm_wide(w_in, row_part)
     col_sums = head * res_col + mm_wide(w_in, col_part)
@@ -326,7 +316,7 @@
         out_shape=[
             pltpu.VMEM(shape, kind) if inner and fits(shape, kind) else jax.ShapeDtypeStruct(shape, kind) for shape, kind, inner in outs
         ],
-        in_specs=[first or vmem()] + [vmem()] * (len(args) - 1),
+        in_specs=[first or vmem()] + [jax.tree.map(lambda _: vmem(), arg) for arg in args[1:]],
         out_specs=[vmem()] * len(outs),
         scratch_shapes=[pltpu.VMEM(shape, kind) for shape, kind in scratch],
     )(*args)
@@ -344,22 +334,24 @@
     tile = target.shape[-1]
     part = 2 * channels // bands
     owners = channels // GROUP + 1
+    noff = dist_bias.shape[1]
     half = features // HALVES
     flags = valid_bins.reshape(1, bins)
     head_row = w_head.reshape(1, channels)
 
     left, send, share = call(
         project_kernel,
-        [((channels, bins), BF, True), ((rows, channels + GROUP, bins), BF, True), ((rows, bins, half), BF, True)],
+        [((channels, bins), BF, True), ((channels + GROUP, bins), BF, True), ((rows, bins, half), BF, True)],
         (embedding, w_left.T, w_right.T, flags),
     )
-    received = exchange(send, "rows")
-    share, received = lax.optimization_barrier((share, received))
+    ahead = [send]
+    for step in range(1, noff):
+        ahead.append(lax.ppermute(send, "rows", [(source, source - step) for source in range(step, rows)]))
     emb_all = exchange(share, "rows")
     predicted, send = call(
         tile_kernel,
         [((tile, tile), BF, False), ((devices, part + GROUP, tile), BF, True)],
-        (offsets, near(left), near(received), flags, target.reshape(tile, tile), w_in, w_out.T, head_row, dist_bias.T),
+        (offsets, near(left), [near(piece) for piece in ahead], flags, target.reshape(tile, tile), w_in, w_out.T, head_row, dist_bias.T),
         smem(),
         [
             ((tile, tile), F32),
@@ -368,8 +360,7 @@
             ((tile, tile), F32),
             ((tile, tile), F32),
             ((hidden, tile), F32),
-            ((2, hidden, 2 * GROUP * tile), BF),
-            ((2 * GROUP * tile, tile), BF),
+            ((hidden, tile), F32),
             ((tile // GROUP, hidden, tile), F32),
             ((tile, 1), F32),
             ((tile, 1), F32),

time: 65 us -> 64.1 us (0.986)
  blocking collectives: 40.2 us -> 29.6 us
  starting transfers between devices: 4 us -> 11.7 us
  waiting for transfers between devices: 0.9 us -> 4.99 us
  Pallas kernels: 18.2 us -> 16 us
    all_to_all x3 -> x2, blocking collectives: 40.2 us -> 29.6 us  [exchange(): return lax.all_to_all(value, axes, 0, 0, tiled=True)]
    ppermute x0 -> x3, waiting for transfers between devices: none -> 4.09 us  [on_device(): lax.ppermute(send, 'rows', [(source, source - step) for source in range(s...]
    ppermute x0 -> x3, starting transfers between devices: none -> 3.86 us  [on_device(): lax.ppermute(send, 'rows', [(source, source - step) for source in range(s...]
    all_to_all x1, starting transfers between devices: 3.49 us -> 7.31 us  [exchange(): return lax.all_to_all(value, axes, 0, 0, tiled=True)]
    pallas_call x5, Pallas kernels: 18.2 us -> 16 us  [call(): pl.pallas_call(kernel, out_shape=[pltpu.VMEM(shape, kind) if inner and fi...]
  transfers between devices with their start and end apart: 2 -> 5, of which waited for: 1 -> 3; matrix products, arithmetic and copies ran while one was open for 0% -> 0% of each run, Pallas kernels for 22% -> 19%
where the time goes in v4:
time: 64.1 us; the launch traced here: 63.6 us
  blocking collectives  29.6 us (46%)
  Pallas kernels  16 us (25%)
  starting transfers between devices  11.7 us (18%)
  waiting for transfers between devices  4.99 us (8%)
  between operations  1.31 us (2%)
    all_to_all x2, blocking collectives, exchange(): return lax.all_to_all(value, axes, 0, 0, tiled=True)  29.6 us
    pallas_call x5, Pallas kernels, call(): pl.pallas_call(kernel, out_shape=[pltpu.VMEM(shape, kind) if inner and fi...  16 us
    all_to_all x1, starting transfers between devices, exchange(): return lax.all_to_all(value, axes, 0, 0, tiled=True)  7.31 us
    ppermute x3, waiting for transfers between devices, on_device(): lax.ppermute(send, 'rows', [(source, source - step) for source in range(s...  4.09 us
    ppermute x3, starting transfers between devices, on_device(): lax.ppermute(send, 'rows', [(source, source - step) for source in range(s...  3.86 us
  transfers between devices with their start and end apart: 5, of which 3 were waited for; matrix products, arithmetic and copies ran while one was open for 0% of the time, Pallas kernels for 19%

profile of v4, /device:TPU:0, one launch (start us, length us, event | category | flops | bytes accessed | tf_op | source)
XLA Modules:
  0.0 63.6 jit_solution(8393025498011947802)
XLA Ops:
  0.6 1.8 %shard_map.161 = (bf16[32,128]{1,0:T(8,128)(2,1)S(1)}, bf16[40,128]{1,0:T(8,128)(2,1)S(1)}, bf16[8,128,256]{2,1,0:T(8,128)(2,1)}) custom-call(bf16[128,512]{1,0:T(8,128)(2,1)} %emb_ref.1, bf16[32,512]{1,0:T(8,128)(2,1)} %bitcast.13, bf16[32,512]{1,0:T(8,128)(2,1)} %bitcast.15, s32[1,128]{1,0:T(1,128)} %bitcast.19), custom_call_target="tpu_custom_call" | custom-call | tf_op jit(solution)/shard_map/pallas_call | solution.py:314
  2.4 7.3 %all-to-all-start = ((bf16[8,128,256]{2,1,0:T(8,128)(2,1)}), bf16[8,128,256]{2,1,0:T(8,128)(2,1)S(1)}, u32[]{:S(2)}, u32[]{:S(2)}) async-start(bf16[8,128,256]{2,1,0:T(8,128)(2,1)} %get-tuple-element.27), calls=%async_computation | async-start | bytes 1048576 | tf_op jit(solution)/shard_map/all_to_all | solution.py:326
  9.7 1.3 %collective-permute-start.2 = (bf16[40,128]{1,0:T(8,128)(2,1)S(1)}, bf16[40,128]{1,0:T(8,128)(2,1)S(1)}, u32[]{:S(2)}, u32[]{:S(2)}) collective-permute-start(bf16[40,128]{1,0:T(8,128)(2,1)S(1)} %get-tuple-element.24.ahead_refs_0_), channel_id=1, source_target_pairs={{12,0},{16,4},{20,8},{24,12},{28,16},{13,1},{17,5},{21,9},{25,13},... | collective-permute-start | bytes 30728 | tf_op jit(solution)/shard_map/ppermute | solution.py:349
  11.0 1.3 %collective-permute-start.1 = (bf16[40,128]{1,0:T(8,128)(2,1)S(1)}, bf16[40,128]{1,0:T(8,128)(2,1)S(1)}, u32[]{:S(2)}, u32[]{:S(2)}) collective-permute-start(bf16[40,128]{1,0:T(8,128)(2,1)S(1)} %get-tuple-element.24.ahead_refs_0_), channel_id=1, source_target_pairs={{8,0},{12,4},{16,8},{20,12},{24,16},{28,20},{9,1},{13,5},{17,9},{2... | collective-permute-start | bytes 30728 | tf_op jit(solution)/shard_map/ppermute | solution.py:349
  12.3 1.3 %collective-permute-start = (bf16[40,128]{1,0:T(8,128)(2,1)S(1)}, bf16[40,128]{1,0:T(8,128)(2,1)S(1)}, u32[]{:S(2)}, u32[]{:S(2)}) collective-permute-start(bf16[40,128]{1,0:T(8,128)(2,1)S(1)} %get-tuple-element.24.ahead_refs_0_), channel_id=1, source_target_pairs={{4,0},{8,4},{12,8},{16,12},{20,16},{24,20},{28,24},{5,1},{9,5},{13... | collective-permute-start | bytes 30728 | tf_op jit(solution)/shard_map/ppermute | solution.py:349
  14.3 3.9 %collective-permute-done.2.ahead_refs_3_ = bf16[40,128]{1,0:T(8,128)(2,1)S(1)} collective-permute-done((bf16[40,128]{1,0:T(8,128)(2,1)S(1)}, bf16[40,128]{1,0:T(8,128)(2,1)S(1)}, u32[]{:S(2)}, u32[]{:S(2)}) %collective-permute-start.2) | collective-permute-done | bytes 10272 | tf_op jit(solution)/shard_map/ppermute | solution.py:349
  18.1 0.0 collective-permute-done.1.ahead_refs_2_
  18.1 0.2 collective-permute-done.ahead_refs_1_
  18.4 11.9 %shard_map.162 = (bf16[128,128]{1,0:T(8,128)(2,1)}, bf16[32,24,128]{2,1,0:T(8,128)(2,1)S(1)}) custom-call(s32[1,1]{1,0:T(1,128)S(6)} %copy.18.offset_ref, bf16[32,128]{1,0:T(8,128)(2,1)S(1)} %get-tuple-element.23.left_ref, bf16[40,128]{1,0:T(8,128)(2,1)S(1)} %get-tuple-element.24.ahead_refs_0_, bf16[40,128]{1,0:T(8,128)(2,1)S(1)} %collective-permute-done.ahead_refs_1_, ...), custom_call_target="tpu_custom_call" | custom-call | tf_op jit(solution)/shard_map/pallas_call | solution.py:314
  30.2 0.0 all-to-all-done.emb_ref
  30.2 18.2 %all_to_all.15.recv_ref = bf16[32,24,128]{2,1,0:T(8,128)(2,1)S(1)} all-to-all(bf16[32,24,128]{2,1,0:T(8,128)(2,1)S(1)} %get-tuple-element.28), channel_id=1, replica_groups=mesh['rows'=8,'band'=4] {'rows','band'}, dimensions={0} | all-to-all | bytes 393216 | tf_op jit(solution)/shard_map/all_to_all | solution.py:326
  48.5 11.4 %all_to_all.16.recv_ref = bf16[32,24,128]{2,1,0:T(8,128)(2,1)S(1)} all-to-all(bf16[32,24,128]{2,1,0:T(8,128)(2,1)S(1)} %shard_map.163), channel_id=1, replica_groups=mesh['rows'=8,'band'=4] {'rows','band'}, dimensions={0} | all-to-all | bytes 393216 | tf_op jit(solution)/shard_map/all_to_all | solution.py:326
  59.9 1.6 %shard_map.164 = (f32[64,256]{1,0:T(8,128)S(1)}, bf16[128,128]{1,0:T(8,128)(2,1)}, f32[32,128]{1,0:T(8,128)}, f32[32,128]{1,0:T(8,128)}, f32[1,32]{1,0:T(1,128)}, /*index=5*/f32[4,32]{1,0:T(4,128)}) custom-call(bf16[32,24,128]{2,1,0:T(8,128)(2,1)S(1)} %all_to_all.16.recv_ref, bf16[8,128,256]{2,1,0:T(8,128)(2,1)S(1)} %all-to-all-done.emb_ref, ...), custom_call_target="tpu_custom_call" | custom-call | tf_op jit(solution)/shard_map/pallas_call | solution.py:314
  61.5 0.5 collective-permute-start.3
  62.0 0.9 %collective-permute-done.3.other_ref = f32[64,256]{1,0:T(8,128)S(1)} collective-permute-done((f32[64,256]{1,0:T(8,128)S(1)}, f32[64,256]{1,0:T(8,128)S(1)}, u32[]{:S(2)}, u32[]{:S(2)}) %collective-permute-start.3) | collective-permute-done | bytes 65568 | tf_op jit(solution)/shard_map/ppermute | solution.py:385
  63.0 0.7 %shard_map.165 = (f32[32,512]{1,0:T(8,128)}, f32[32,512]{1,0:T(8,128)}) custom-call(f32[64,256]{1,0:T(8,128)S(1)} %get-tuple-element.31.own_ref, f32[64,256]{1,0:T(8,128)S(1)} %collective-permute-done.3.other_ref), custom_call_target="tpu_custom_call" | custom-call | tf_op jit(solution)/shard_map/pallas_call | solution.py:314
  (1 shorter events, 0.0 us)
Async XLA Ops:
  2.4 27.8 %all-to-all-start = ((bf16[8,128,256]{2,1,0:T(8,128)(2,1)}), bf16[8,128,256]{2,1,0:T(8,128)(2,1)S(1)}, u32[]{:S(2)}, u32[]{:S(2)}) async-start(bf16[8,128,256]{2,1,0:T(8,128)(2,1)} %get-tuple-element.27), calls=%async_computation | async-start | bytes 1048576 | tf_op jit(solution)/shard_map/all_to_all | solution.py:326
  9.7 8.4 %collective-permute-start.2 = (bf16[40,128]{1,0:T(8,128)(2,1)S(1)}, bf16[40,128]{1,0:T(8,128)(2,1)S(1)}, u32[]{:S(2)}, u32[]{:S(2)}) collective-permute-start(bf16[40,128]{1,0:T(8,128)(2,1)S(1)} %get-tuple-element.24.ahead_refs_0_), channel_id=1, source_target_pairs={{12,0},{16,4},{20,8},{24,12},{28,16},{13,1},{17,5},{21,9},{25,13},... | collective-permute-start | bytes 30728 | tf_op jit(solution)/shard_map/ppermute | solution.py:349
  11.0 7.1 %collective-permute-start.1 = (bf16[40,128]{1,0:T(8,128)(2,1)S(1)}, bf16[40,128]{1,0:T(8,128)(2,1)S(1)}, u32[]{:S(2)}, u32[]{:S(2)}) collective-permute-start(bf16[40,128]{1,0:T(8,128)(2,1)S(1)} %get-tuple-element.24.ahead_refs_0_), channel_id=1, source_target_pairs={{8,0},{12,4},{16,8},{20,12},{24,16},{28,20},{9,1},{13,5},{17,9},{2... | collective-permute-start | bytes 30728 | tf_op jit(solution)/shard_map/ppermute | solution.py:349
  12.3 6.0 %collective-permute-start = (bf16[40,128]{1,0:T(8,128)(2,1)S(1)}, bf16[40,128]{1,0:T(8,128)(2,1)S(1)}, u32[]{:S(2)}, u32[]{:S(2)}) collective-permute-start(bf16[40,128]{1,0:T(8,128)(2,1)S(1)} %get-tuple-element.24.ahead_refs_0_), channel_id=1, source_target_pairs={{4,0},{8,4},{12,8},{16,12},{20,16},{24,20},{28,24},{5,1},{9,5},{13... | collective-permute-start | bytes 30728 | tf_op jit(solution)/shard_map/ppermute | solution.py:349
  61.5 1.4 %collective-permute-start.3 = (f32[64,256]{1,0:T(8,128)S(1)}, f32[64,256]{1,0:T(8,128)S(1)}, u32[]{:S(2)}, u32[]{:S(2)}) collective-permute-start(f32[64,256]{1,0:T(8,128)S(1)} %get-tuple-element.31.own_ref), channel_id=1, source_target_pairs={{0,1},{1,0},{2,3},{3,2},{4,5},{5,4},{6,7},{7,6},{8,9},{9,8},{10,11... | collective-permute-start | bytes 196616 | tf_op jit(solution)/shard_map/ppermute | solution.py:385

commit v5 on v4

--- a/solution.py
+++ b/solution.py
@@ -15,6 +15,7 @@
 STRETCH = (0.044715 * CURVE) ** (1.0 / 3.0)
 LINEAR = CURVE / STRETCH
 GROUP = 8
+UNROLL = 4
 HALVES = 2
 SMALL = 1 << 20
 NT = (((1,), (1,)), ((), ()))
@@ -58,7 +59,8 @@
     flags = jnp.broadcast_to(flags_ref[...].astype(F32), (GROUP, bins))
     send_ref[...] = jnp.concatenate([mm(wr_ref[...], emb, NT), flags], axis=0).astype(BF)
     width = share_ref.shape[2]
-    start = pl.multiple_of(lax.rem(lax.axis_index("band"), HALVES) * width, width)
+    band, sides = lax.axis_index("band"), lax.axis_size("band") // HALVES
+    start = pl.multiple_of((lax.rem(band, HALVES) * sides + band // HALVES) * width, width)
     share = emb_ref[:, pl.ds(start, width)]
 
     def body(row, carry):
@@ -83,6 +85,7 @@
     target_wide,
     act_ref,
     slope_ref,
+    pair_ref,
     logit_ref,
     res_ref,
     col_ref,
@@ -134,11 +137,13 @@
     def start_of(group):
         return pl.multiple_of(group * GROUP, GROUP)
 
-    def turn(group):
-        return pltpu.roll(left, lax.rem(tile - start_of(group), tile), 1)
-
-    def forward(turned, step, slot, logits):
-        pair_in = (turned[:, step : step + 1] + shifted).astype(BF)
+    def prepare(group, slot):
+        turned = pltpu.roll(left, lax.rem(tile - start_of(group), tile), 1)
+        for step in range(GROUP):
+            pair_ref[slot, step] = (turned[:, step : step + 1] + shifted).astype(BF)
+
+    def forward(step, slot, logits):
+        pair_in = pair_ref[slot, step]
         x = mm(w_both, jnp.concatenate([pair_in, pair_in], axis=0))
         square = x * x
         inner = square + LINEAR
@@ -146,9 +151,8 @@
         lift = 1.0 + bend
         act = x * lift
         slope_ref[slot, step] = lift + (act * (1.0 - bend)) * (inner + (square + square))
-        act = act.astype(BF)
         act_ref[slot, step] = act
-        return logits + mm(gain_parts[step], act)
+        return logits + mm(gain_parts[step], act.astype(BF))
 
     def settle(group, logits):
         at = pl.ds(start_of(group), GROUP)
@@ -157,40 +161,39 @@
         logit_ref[at, :] = logits
         res_ref[at, :] = flag_col_ref[at, :] * col_flags * (logits - target_wide[at, :])
 
-    def backward(res, res_low, step, slot, group, total, acts):
+    def backward(res, step, slot, group, total, acts):
         product = slope_ref[slot, step] * res[step : step + 1]
         sums_ref[group, :, step : step + 1] = jnp.sum(product, axis=1, keepdims=True)
-        weighted = act_ref[slot, step] * res_low[step : step + 1]
-        return total + product, acts + weighted.astype(F32)
+        return total + product, acts + act_ref[slot, step] * res[step : step + 1]
 
     def none():
         return jnp.zeros((2 * GROUP, tile), F32)
 
+    prepare(0, 0)
+    prepare(1, 1)
     logits = none()
-    turned = turn(0)
     for step in range(GROUP):
-        logits = forward(turned, step, 0, logits)
+        logits = forward(step, 0, logits)
     settle(0, logits)
 
     def body(index, carry):
-        for slot in range(2):
-            group = 2 * index + slot
+        for block in range(UNROLL):
+            slot = block % 2
+            group = UNROLL * index + block
             following = lax.rem(group + 1, groups)
-            at = pl.ds(start_of(group), GROUP)
-            res = res_ref[at, :]
-            res_low = res.astype(BF)
+            res = res_ref[pl.ds(start_of(group), GROUP), :]
             total, acts = col_ref[...], act_sum_ref[...]
-            turned = turn(following)
+            prepare(lax.rem(group + 2, groups), slot)
             logits = none()
             for step in range(GROUP):
-                logits = forward(turned, step, 1 - slot, logits)
-                total, acts = backward(res, res_low, step, slot, group, total, acts)
+                logits = forward(step, 1 - slot, logits)
+                total, acts = backward(res, step, slot, group, total, acts)
             col_ref[...] = total
             act_sum_ref[...] = acts
             settle(following, logits)
         return carry
 
-    lax.fori_loop(0, groups // 2, body, 0)
+    lax.fori_loop(0, groups // UNROLL, body, 0)
 
     pred_ref[...] = logit_ref[...].astype(BF)
     res = res_ref[...]
@@ -250,23 +253,31 @@
     send_ref[...] = jnp.broadcast_to(jnp.where(use_low, low, total).astype(BF)[None], send_ref.shape)
 
 
-def finish_kernel(
-    recv_ref, emb_ref, wl_ref, wr_ref, w_head_ref, share_ref, grad_emb_ref, in_ref, out_ref, head_ref, bias_ref
-):
-    rows = emb_ref.shape[0]
-    devices, height, width = recv_ref.shape
-    bands = devices // rows
+def grads_of(recv_ref, row, part):
+    bands = lax.axis_size("band")
+    return jnp.concatenate([recv_ref[row * bands + band, :part, :].astype(F32) for band in range(bands)], axis=0)
+
+
+def share_kernel(recv_ref, near_ref, far_ref, share_ref):
+    rows, width = near_ref.shape[0], near_ref.shape[2]
+    part = recv_ref.shape[1] - GROUP
+    side = lax.axis_index("band") // HALVES
+
+    def body(row, totals):
+        grads = grads_of(recv_ref, row, part).astype(BF)
+        return totals[0] + mm(grads, near_ref[row]), totals[1] + mm(grads, far_ref[row])
+
+    zero = jnp.zeros((share_ref.shape[0], width), F32)
+    totals = lax.fori_loop(0, rows, body, (zero, zero), unroll=rows <= 8)
+    for total, index in zip(totals, (side, 1 - side)):
+        share_ref[:, pl.ds(pl.multiple_of(index * width, width), width)] = total
+
+
+def finish_kernel(recv_ref, wl_ref, wr_ref, w_head_ref, grad_emb_ref, in_ref, out_ref, head_ref, bias_ref):
+    _, height, width = recv_ref.shape
     part = height - GROUP
     channels = in_ref.shape[0]
-
-    def grads(row):
-        return jnp.concatenate([recv_ref[row * bands + band, :part, :].astype(F32) for band in range(bands)], axis=0)
-
-    def body(row, total):
-        return total + mm(grads(row).astype(BF), emb_ref[row])
-
-    share_ref[...] = lax.fori_loop(0, rows, body, jnp.zeros(share_ref.shape, F32), unroll=rows <= 8)
-    own = grads(lax.axis_index("rows")).T.astype(BF)
+    own = grads_of(recv_ref, lax.axis_index("rows"), part).T.astype(BF)
     share = pl.ds(pl.multiple_of(lax.axis_index("band") * width, width), width)
     weights = jnp.concatenate([wl_ref[:, share], wr_ref[:, share]], axis=0)
     grad_emb_ref[...] = mm(own, weights).astype(BF)
@@ -335,13 +346,13 @@
     part = 2 * channels // bands
     owners = channels // GROUP + 1
     noff = dist_bias.shape[1]
-    half = features // HALVES
+    quarter = features // bands
     flags = valid_bins.reshape(1, bins)
     head_row = w_head.reshape(1, channels)
 
     left, send, share = call(
         project_kernel,
-        [((channels, bins), BF, True), ((channels + GROUP, bins), BF, True), ((rows, bins, half), BF, True)],
+        [((channels, bins), BF, True), ((channels + GROUP, bins), BF, True), ((rows, bins, quarter), BF, True)],
         (embedding, w_left.T, w_right.T, flags),
     )
     ahead = [send]
@@ -350,13 +361,14 @@
     emb_all = exchange(share, "rows")
     predicted, send = call(
         tile_kernel,
-        [((tile, tile), BF, False), ((devices, part + GROUP, tile), BF, True)],
-        (offsets, near(left), [near(piece) for piece in ahead], flags, target.reshape(tile, tile), w_in, w_out.T, head_row, dist_bias.T),
+        [((tile, tile), BF, True), ((devices, part + GROUP, tile), BF, True)],
+        (offsets, near(left), [near(piece) for piece in ahead], near(flags), near(target.reshape(tile, tile)), near(w_in), near(w_out.T), near(head_row), near(dist_bias.T)),
         smem(),
         [
             ((tile, tile), F32),
-            ((2, GROUP, hidden, tile), BF),
             ((2, GROUP, hidden, tile), F32),
+            ((2, GROUP, hidden, tile), F32),
+            ((2, GROUP, channels, tile), BF),
             ((tile, tile), F32),
             ((tile, tile), F32),
             ((hidden, tile), F32),
@@ -367,22 +379,25 @@
         ],
     )
     send, emb_all = lax.optimization_barrier((send, emb_all))
+    emb_far = lax.ppermute(emb_all, "band", [(source, source ^ HALVES) for source in range(bands)])
     partial = exchange(send, ("rows", "band"))
     (send,) = call(functools.partial(total_kernel, owners), [(partial.shape, BF, True)], (near(partial),))
     complete = exchange(send, ("rows", "band"))
-    mine, grad_embedding, grad_in, grad_out, grad_head, grad_bias = call(
+    (mine,) = call(
+        share_kernel, [((2 * channels, features // HALVES), F32, True)], (near(complete), near(emb_all), near(emb_far))
+    )
+    other = lax.ppermute(mine, "band", [(source, source ^ 1) for source in range(bands)])
+    grad_embedding, grad_in, grad_out, grad_head, grad_bias = call(
         finish_kernel,
         [
-            ((2 * channels, half), F32, True),
             ((bins, features // bands), BF, False),
             ((channels, hidden), F32, False),
             ((channels, hidden), F32, False),
             ((1, channels), F32, False),
             (dist_bias.shape[::-1], F32, False),
         ],
-        (near(complete), near(emb_all), w_left.T, w_right.T, head_row),
-    )
-    other = lax.ppermute(mine, "band", [(source, source ^ 1) for source in range(bands)])
+        (near(complete), near(w_left.T), near(w_right.T), near(head_row)),
+    )
     grad_left, grad_right = call(arrange_kernel, [((channels, features), F32, False)] * 2, (near(mine), near(other)))
     return (
         predicted.reshape(target.shape),

time: 64.1 us -> 60.8 us (0.949)
  blocking collectives: 29.6 us -> 17.1 us
  waiting for transfers between devices: 4.99 us -> 12.5 us
  starting transfers between devices: 11.7 us -> 15.8 us
  Pallas kernels: 16 us -> 12.1 us
  local copies, waits for them, and re-layouts: 0 us -> 1.43 us
    all_to_all x2 -> x1, blocking collectives: 29.6 us -> 17.1 us  [exchange(): return lax.all_to_all(value, axes, 0, 0, tiled=True)]
    ppermute x0 -> x1, waiting for transfers between devices: none -> 8.72 us  [on_device(): lax.ppermute(emb_all, 'band', [(source, source ^ HALVES) for source in ra...]
    pallas_call x5 -> x6, Pallas kernels: 16 us -> 12.1 us  [call(): pl.pallas_call(kernel, out_shape=[pltpu.VMEM(shape, kind) if inner and fi...]
    all_to_all x1 -> x2, starting transfers between devices: 7.31 us -> 10.1 us  [exchange(): return lax.all_to_all(value, axes, 0, 0, tiled=True)]
    ppermute x0 -> x1, starting transfers between devices: none -> 1.83 us  [on_device(): lax.ppermute(emb_all, 'band', [(source, source ^ HALVES) for source in ra...]
    unnamed x0 -> x17, local copies, waits for them, and re-layouts: none -> 1.43 us
    ppermute x1, waiting for transfers between devices: 0.9 us -> 0.01 us  [on_device(): lax.ppermute(mine, 'band', [(source, source ^ 1) for source in range(band...]
  transfers between devices with their start and end apart: 5 -> 7, of which waited for: 3 -> 4; matrix products, arithmetic and copies ran while one was open for 0% -> 1% of each run, Pallas kernels for 19% -> 15%
where the time goes in v5:
time: 60.8 us; the launch traced here: 60.3 us
  blocking collectives  17.1 us (28%)
  starting transfers between devices  15.8 us (26%)
  waiting for transfers between devices  12.5 us (21%)
  Pallas kernels  12.1 us (20%)
  local copies, waits for them, and re-layouts  1.43 us (2%)
  between operations  1.37 us (2%)
    all_to_all x1, blocking collectives, exchange(): return lax.all_to_all(value, axes, 0, 0, tiled=True)  17.1 us
    pallas_call x6, Pallas kernels, call(): pl.pallas_call(kernel, out_shape=[pltpu.VMEM(shape, kind) if inner and fi...  12.1 us
    all_to_all x2, starting transfers between devices, exchange(): return lax.all_to_all(value, axes, 0, 0, tiled=True)  10.1 us
    ppermute x1, waiting for transfers between devices, on_device(): lax.ppermute(emb_all, 'band', [(source, source ^ HALVES) for source in ra...  8.72 us
    ppermute x3, starting transfers between devices, on_device(): lax.ppermute(send, 'rows', [(source, source - step) for source in range(s...  3.88 us
    ppermute x3, waiting for transfers between devices, on_device(): lax.ppermute(send, 'rows', [(source, source - step) for source in range(s...  3.74 us
    ppermute x1, starting transfers between devices, on_device(): lax.ppermute(emb_all, 'band', [(source, source ^ HALVES) for source in ra...  1.83 us
    unnamed x17, local copies, waits for them, and re-layouts  1.43 us
  transfers between devices with their start and end apart: 7, of which 4 were waited for; matrix products, arithmetic and copies ran while one was open for 1% of the time, Pallas kernels for 15%

profile of v5, /device:TPU:0, one launch (start us, length us, event | category | flops | bytes accessed | tf_op | source)
XLA Modules:
  0.0 60.3 jit_solution(5114094700404347956)
XLA Ops:
  0.6 1.7 %shard_map.161 = (bf16[32,128]{1,0:T(8,128)(2,1)S(1)}, bf16[40,128]{1,0:T(8,128)(2,1)S(1)}, bf16[8,128,128]{2,1,0:T(8,128)(2,1)}) custom-call(bf16[128,512]{1,0:T(8,128)(2,1)} %emb_ref.1, bf16[32,512]{1,0:T(8,128)(2,1)} %bitcast.14, bf16[32,512]{1,0:T(8,128)(2,1)} %bitcast.16, s32[1,128]{1,0:T(1,128)} %bitcast.20), custom_call_target="tpu_custom_call" | custom-call | tf_op jit(solution)/shard_map/pallas_call | solution.py:325
  2.3 7.4 %all-to-all-start = ((bf16[8,128,128]{2,1,0:T(8,128)(2,1)}), bf16[8,128,128]{2,1,0:T(8,128)(2,1)S(1)}, u32[]{:S(2)}, u32[]{:S(2)}) async-start(bf16[8,128,128]{2,1,0:T(8,128)(2,1)} %get-tuple-element.26), calls=%async_computation | async-start | bytes 524288 | tf_op jit(solution)/shard_map/all_to_all | solution.py:337
  9.8 1.3 %collective-permute-start.2 = (bf16[40,128]{1,0:T(8,128)(2,1)S(1)}, bf16[40,128]{1,0:T(8,128)(2,1)S(1)}, u32[]{:S(2)}, u32[]{:S(2)}) collective-permute-start(bf16[40,128]{1,0:T(8,128)(2,1)S(1)} %get-tuple-element.23.ahead_refs_0_), channel_id=1, source_target_pairs={{12,0},{16,4},{20,8},{24,12},{28,16},{13,1},{17,5},{21,9},{25,13},... | collective-permute-start | bytes 30728 | tf_op jit(solution)/shard_map/ppermute | solution.py:360
  11.1 1.3 %collective-permute-start.1 = (bf16[40,128]{1,0:T(8,128)(2,1)S(1)}, bf16[40,128]{1,0:T(8,128)(2,1)S(1)}, u32[]{:S(2)}, u32[]{:S(2)}) collective-permute-start(bf16[40,128]{1,0:T(8,128)(2,1)S(1)} %get-tuple-element.23.ahead_refs_0_), channel_id=1, source_target_pairs={{8,0},{12,4},{16,8},{20,12},{24,16},{28,20},{9,1},{13,5},{17,9},{2... | collective-permute-start | bytes 30728 | tf_op jit(solution)/shard_map/ppermute | solution.py:360
  12.4 1.3 %collective-permute-start = (bf16[40,128]{1,0:T(8,128)(2,1)S(1)}, bf16[40,128]{1,0:T(8,128)(2,1)S(1)}, u32[]{:S(2)}, u32[]{:S(2)}) collective-permute-start(bf16[40,128]{1,0:T(8,128)(2,1)S(1)} %get-tuple-element.23.ahead_refs_0_), channel_id=1, source_target_pairs={{4,0},{8,4},{12,8},{16,12},{20,16},{24,20},{28,24},{5,1},{9,5},{13... | collective-permute-start | bytes 30728 | tf_op jit(solution)/shard_map/ppermute | solution.py:360
  14.3 2.1 %collective-permute-done.2.ahead_refs_3_ = bf16[40,128]{1,0:T(8,128)(2,1)S(1)} collective-permute-done((bf16[40,128]{1,0:T(8,128)(2,1)S(1)}, bf16[40,128]{1,0:T(8,128)(2,1)S(1)}, u32[]{:S(2)}, u32[]{:S(2)}) %collective-permute-start.2) | collective-permute-done | bytes 10272 | tf_op jit(solution)/shard_map/ppermute | solution.py:360
  16.5 0.3 collective-permute-done.1.ahead_refs_2_
  16.8 1.3 %collective-permute-done.ahead_refs_1_ = bf16[40,128]{1,0:T(8,128)(2,1)S(1)} collective-permute-done((bf16[40,128]{1,0:T(8,128)(2,1)S(1)}, bf16[40,128]{1,0:T(8,128)(2,1)S(1)}, u32[]{:S(2)}, u32[]{:S(2)}) %collective-permute-start) | collective-permute-done | bytes 10272 | tf_op jit(solution)/shard_map/ppermute | solution.py:360
  18.1 0.7 %copy-done.7 = f32[32,4]{0,1:T(4,128)S(1)} copy-done((f32[32,4]{0,1:T(4,128)S(1)}, f32[32,4]{0,1:T(4,128)}, u32[]{:S(2)}) %copy-start.7) | copy-done | bytes 536
  18.8 7.9 %shard_map.162 = (bf16[128,128]{1,0:T(8,128)(2,1)S(1)}, bf16[32,24,128]{2,1,0:T(8,128)(2,1)S(1)}) custom-call(s32[1,1]{1,0:T(1,128)S(6)} %copy.19.offset_ref, bf16[32,128]{1,0:T(8,128)(2,1)S(1)} %get-tuple-element.22.left_ref, bf16[40,128]{1,0:T(8,128)(2,1)S(1)} %get-tuple-element.23.ahead_refs_0_, bf16[40,128]{1,0:T(8,128)(2,1)S(1)} %collective-permute-done.ahead_refs_1_, ...), custom_call_target="tpu_custom_call" | custom-call | tf_op jit(solution)/shard_map/pallas_call | solution.py:325
  26.7 17.1 %all_to_all.15.recv_ref = bf16[32,24,128]{2,1,0:T(8,128)(2,1)S(1)} all-to-all(bf16[32,24,128]{2,1,0:T(8,128)(2,1)S(1)} %get-tuple-element.27), channel_id=1, replica_groups=mesh['rows'=8,'band'=4] {'rows','band'}, dimensions={0} | all-to-all | bytes 393216 | tf_op jit(solution)/shard_map/all_to_all | solution.py:337
  43.8 0.7 %shard_map.163 = bf16[32,24,128]{2,1,0:T(8,128)(2,1)} custom-call(bf16[32,24,128]{2,1,0:T(8,128)(2,1)S(1)} %all_to_all.15.recv_ref), custom_call_target="tpu_custom_call" | custom-call | tf_op jit(solution)/shard_map/pallas_call | solution.py:325
  44.5 2.6 %all-to-all-start.2 = ((bf16[32,24,128]{2,1,0:T(8,128)(2,1)}), bf16[32,24,128]{2,1,0:T(8,128)(2,1)S(1)}, u32[]{:S(2)}, u32[]{:S(2)}) async-start(bf16[32,24,128]{2,1,0:T(8,128)(2,1)} %shard_map.163), calls=%async_computation.2 | async-start | bytes 393216 | tf_op jit(solution)/shard_map/all_to_all | solution.py:337
  47.1 1.8 %collective-permute-start.3 = (bf16[8,128,128]{2,1,0:T(8,128)(2,1)S(1)}, bf16[8,128,128]{2,1,0:T(8,128)(2,1)S(1)}, u32[]{:S(2)}, u32[]{:S(2)}) collective-permute-start(bf16[8,128,128]{2,1,0:T(8,128)(2,1)S(1)} %all-to-all-done.near_ref), channel_id=1, source_target_pairs={{0,2},{1,3},{2,0},{3,1},{4,6},{5,7},{6,4},{7,5},{8,10},{9,11},{10,... | collective-permute-start | bytes 786440 | tf_op jit(solution)/shard_map/ppermute | solution.py:382
  49.0 8.7 %collective-permute-done.3.far_ref = bf16[8,128,128]{2,1,0:T(8,128)(2,1)S(1)} collective-permute-done((bf16[8,128,128]{2,1,0:T(8,128)(2,1)S(1)}, bf16[8,128,128]{2,1,0:T(8,128)(2,1)S(1)}, u32[]{:S(2)}, u32[]{:S(2)}) %collective-permute-start.3) | collective-permute-done | bytes 262176 | tf_op jit(solution)/shard_map/ppermute | solution.py:382
  57.7 0.3 shard_map.165.own_ref
  58.0 0.0 collective-permute-start.4
  58.0 0.0 copy-start
  58.0 0.0 copy-start.1
  58.0 0.6 %copy.18 = bf16[1,1,128,128]{3,2,1,0:T(8,128)(2,1)} copy(bf16[1,1,128,128]{3,2,1,0:T(8,128)(2,1)S(1)} %bitcast.13) | data formatting | bytes 65536
  58.6 0.1 copy-done
  58.7 0.0 copy-done.1
  58.8 0.8 %shard_map.164 = (bf16[128,128]{1,0:T(8,128)(2,1)}, f32[32,128]{1,0:T(8,128)}, f32[32,128]{1,0:T(8,128)}, f32[1,32]{1,0:T(1,128)}, f32[4,32]{1,0:T(4,128)}) custom-call(bf16[32,24,128]{2,1,0:T(8,128)(2,1)S(1)} %all-to-all-done.2.recv_ref, bf16[32,512]{1,0:T(8,128)(2,1)S(1)} %bitcast.15, bf16[32,512]{1,0:T(8,128)(2,1)S(1)} %bitcast.17, f32[1,32]{1,0:T(1,128)S(1)} %bitcast.23), custom_call_target="tpu_custom_call" | custom-call | tf_op jit(solution)/shard_map/pallas_call | solution.py:325
  59.6 0.7 %shard_map.166 = (f32[32,512]{1,0:T(8,128)}, f32[32,512]{1,0:T(8,128)}) custom-call(f32[64,256]{1,0:T(8,128)S(1)} %shard_map.165.own_ref, f32[64,256]{1,0:T(8,128)S(1)} %collective-permute-done.4.other_ref), custom_call_target="tpu_custom_call" | custom-call | tf_op jit(solution)/shard_map/pallas_call | solution.py:325
  (14 shorter events, 0.0 us)
Async XLA Ops:
  2.3 15.8 %copy-start.2 = (bf16[1,1,128,128]{3,2,1,0:T(8,128)(2,1)S(1)}, bf16[1,1,128,128]{3,2,1,0:T(8,128)(2,1)}, u32[]{:S(2)}) copy-start(bf16[1,1,128,128]{3,2,1,0:T(8,128)(2,1)} %param.19) | copy-start | bytes 98308
  2.3 15.8 %copy-start.4 = (bf16[128,32]{0,1:T(8,128)(2,1)S(1)}, bf16[128,32]{0,1:T(8,128)(2,1)}, u32[]{:S(2)}) copy-start(bf16[128,32]{0,1:T(8,128)(2,1)} %param.14) | copy-start | bytes 24580
  2.3 24.3 %all-to-all-start = ((bf16[8,128,128]{2,1,0:T(8,128)(2,1)}), bf16[8,128,128]{2,1,0:T(8,128)(2,1)S(1)}, u32[]{:S(2)}, u32[]{:S(2)}) async-start(bf16[8,128,128]{2,1,0:T(8,128)(2,1)} %get-tuple-element.26), calls=%async_computation | async-start | bytes 524288 | tf_op jit(solution)/shard_map/all_to_all | solution.py:337
  9.8 8.3 %copy-start.3 = (bf16[32,128]{1,0:T(8,128)(2,1)S(1)}, bf16[32,128]{1,0:T(8,128)(2,1)}, u32[]{:S(2)}) copy-start(bf16[32,128]{1,0:T(8,128)(2,1)} %w_in_ref.1) | copy-start | bytes 24580
  9.8 6.7 %collective-permute-start.2 = (bf16[40,128]{1,0:T(8,128)(2,1)S(1)}, bf16[40,128]{1,0:T(8,128)(2,1)S(1)}, u32[]{:S(2)}, u32[]{:S(2)}) collective-permute-start(bf16[40,128]{1,0:T(8,128)(2,1)S(1)} %get-tuple-element.23.ahead_refs_0_), channel_id=1, source_target_pairs={{12,0},{16,4},{20,8},{24,12},{28,16},{13,1},{17,5},{21,9},{25,13},... | collective-permute-start | bytes 30728 | tf_op jit(solution)/shard_map/ppermute | solution.py:360
  11.1 5.7 %collective-permute-start.1 = (bf16[40,128]{1,0:T(8,128)(2,1)S(1)}, bf16[40,128]{1,0:T(8,128)(2,1)S(1)}, u32[]{:S(2)}, u32[]{:S(2)}) collective-permute-start(bf16[40,128]{1,0:T(8,128)(2,1)S(1)} %get-tuple-element.23.ahead_refs_0_), channel_id=1, source_target_pairs={{8,0},{12,4},{16,8},{20,12},{24,16},{28,20},{9,1},{13,5},{17,9},{2... | collective-permute-start | bytes 30728 | tf_op jit(solution)/shard_map/ppermute | solution.py:360
  12.4 5.7 %collective-permute-start = (bf16[40,128]{1,0:T(8,128)(2,1)S(1)}, bf16[40,128]{1,0:T(8,128)(2,1)S(1)}, u32[]{:S(2)}, u32[]{:S(2)}) collective-permute-start(bf16[40,128]{1,0:T(8,128)(2,1)S(1)} %get-tuple-element.23.ahead_refs_0_), channel_id=1, source_target_pairs={{4,0},{8,4},{12,8},{16,12},{20,16},{24,20},{28,24},{5,1},{9,5},{13... | collective-permute-start | bytes 30728 | tf_op jit(solution)/shard_map/ppermute | solution.py:360
  18.1 0.7 %copy-start.7 = (f32[32,4]{0,1:T(4,128)S(1)}, f32[32,4]{0,1:T(4,128)}, u32[]{:S(2)}) copy-start(f32[32,4]{0,1:T(4,128)} %param.16) | copy-start | bytes 1540
  18.1 0.7 %copy-start.5 = (s32[128]{0:T(128)S(1)}, s32[128]{0:T(128)}, u32[]{:S(2)}) copy-start(s32[128]{0:T(128)} %param.18) | copy-start | bytes 1540
  18.1 0.7 %copy-start.6 = (f32[32]{0:T(128)S(1)}, f32[32]{0:T(128)}, u32[]{:S(2)}) copy-start(f32[32]{0:T(128)} %param.15) | copy-start | bytes 388
  44.5 13.2 %all-to-all-start.2 = ((bf16[32,24,128]{2,1,0:T(8,128)(2,1)}), bf16[32,24,128]{2,1,0:T(8,128)(2,1)S(1)}, u32[]{:S(2)}, u32[]{:S(2)}) async-start(bf16[32,24,128]{2,1,0:T(8,128)(2,1)} %shard_map.163), calls=%async_computation.2 | async-start | bytes 393216 | tf_op jit(solution)/shard_map/all_to_all | solution.py:337
  47.1 10.6 %collective-permute-start.3 = (bf16[8,128,128]{2,1,0:T(8,128)(2,1)S(1)}, bf16[8,128,128]{2,1,0:T(8,128)(2,1)S(1)}, u32[]{:S(2)}, u32[]{:S(2)}) collective-permute-start(bf16[8,128,128]{2,1,0:T(8,128)(2,1)S(1)} %all-to-all-done.near_ref), channel_id=1, source_target_pairs={{0,2},{1,3},{2,0},{3,1},{4,6},{5,7},{6,4},{7,5},{8,10},{9,11},{10,... | collective-permute-start | bytes 786440 | tf_op jit(solution)/shard_map/ppermute | solution.py:382
  58.0 1.6 %collective-permute-start.4 = (f32[64,256]{1,0:T(8,128)S(1)}, f32[64,256]{1,0:T(8,128)S(1)}, u32[]{:S(2)}, u32[]{:S(2)}) collective-permute-start(f32[64,256]{1,0:T(8,128)S(1)} %shard_map.165.own_ref), channel_id=1, source_target_pairs={{0,1},{1,0},{2,3},{3,2},{4,5},{5,4},{6,7},{7,6},{8,9},{9,8},{10,11... | collective-permute-start | bytes 196616 | tf_op jit(solution)/shard_map/ppermute | solution.py:389
  58.0 0.8 %copy-start = (bf16[512,32]{0,1:T(8,128)(2,1)S(1)}, bf16[512,32]{0,1:T(8,128)(2,1)}, u32[]{:S(2)}) copy-start(bf16[512,32]{0,1:T(8,128)(2,1)} %param.11) | copy-start | bytes 98308
  58.0 0.8 %copy-start.1 = (bf16[512,32]{0,1:T(8,128)(2,1)S(1)}, bf16[512,32]{0,1:T(8,128)(2,1)}, u32[]{:S(2)}) copy-start(bf16[512,32]{0,1:T(8,128)(2,1)} %param.12) | copy-start | bytes 98308

commit v6 on v5

--- a/solution.py
+++ b/solution.py
@@ -52,37 +52,91 @@
     return jnp.sum(jnp.where(eye(count), jnp.broadcast_to(col, (count, count)), 0.0), axis=0, keepdims=True)
 
 
-def project_kernel(emb_ref, wl_ref, wr_ref, flags_ref, left_ref, send_ref, share_ref):
-    emb = emb_ref[...]
-    bins = emb.shape[0]
-    left_ref[...] = mm(wl_ref[...], emb, NT).astype(BF)
-    flags = jnp.broadcast_to(flags_ref[...].astype(F32), (GROUP, bins))
-    send_ref[...] = jnp.concatenate([mm(wr_ref[...], emb, NT), flags], axis=0).astype(BF)
-    width = share_ref.shape[2]
-    band, sides = lax.axis_index("band"), lax.axis_size("band") // HALVES
-    start = pl.multiple_of((lax.rem(band, HALVES) * sides + band // HALVES) * width, width)
-    share = emb_ref[:, pl.ds(start, width)]
-
-    def body(row, carry):
-        share_ref[row] = share
-        return carry
-
-    lax.fori_loop(0, share_ref.shape[0], body, 0, unroll=share_ref.shape[0] <= 8)
-
-
-def tile_kernel(
+def project_kernel(
     offset_ref,
-    left_ref,
-    ahead_refs,
+    emb_ref,
+    wl_ref,
+    wr_ref,
     flags_ref,
     target_ref,
     w_in_ref,
     w_out_ref,
     w_head_ref,
     bias_ref,
+    left_ref,
+    send_ref,
+    share_ref,
+    target_wide,
+    w_both_ref,
+    parts_ref,
+    gain_ref,
+    logit_col_ref,
+    flag_col_ref,
+    head_ref,
+    own_bias_ref,
+    weights_ref,
+    w_in_near,
+    w_out_near,
+):
+    emb = emb_ref[...]
+    bins = emb.shape[0]
+    left = mm(wl_ref[...], emb, NT).astype(BF)
+    left_ref[...] = left
+    flags_row = flags_ref[...].astype(F32)
+    flags = jnp.broadcast_to(flags_row, (GROUP, bins))
+    send_ref[...] = jnp.concatenate([mm(wr_ref[...], emb, NT), flags], axis=0).astype(BF)
+    width = share_ref.shape[2]
+    band, sides = lax.axis_index("band"), lax.axis_size("band") // HALVES
+    start = pl.multiple_of((lax.rem(band, HALVES) * sides + band // HALVES) * width, width)
+    share = emb_ref[:, pl.ds(start, width)]
+
+    def body(row, carry):
+        share_ref[row] = share
+        return carry
+
+    lax.fori_loop(0, share_ref.shape[0], body, 0, unroll=share_ref.shape[0] <= 8)
+    target_wide[...] = target_ref[...].astype(F32)
+    w_in = w_in_ref[...]
+    w_in_near[...] = w_in
+    w_out_near[...] = w_out_ref[...]
+    w_high, w_low = split(w_in.astype(F32).T * STRETCH)
+    w_both_ref[...] = jnp.concatenate([w_high, w_low], axis=1)
+    head = to_col(w_head_ref[...])
+    head_ref[...] = head
+    off_row = lax.broadcasted_iota(jnp.int32, bias_ref.shape, 0)
+    bias = to_col(jnp.sum(jnp.where(off_row == offset_ref[0, 0], bias_ref[...], 0.0), axis=0, keepdims=True))
+    own_bias_ref[...] = bias
+    gain_row = jnp.sum(w_out_ref[...].astype(F32) * head, axis=0, keepdims=True)
+    gain_ref[...] = to_col(gain_row) * 0.5
+    gain_row = gain_row * (0.5 / STRETCH)
+    gain_high = gain_row.astype(BF).astype(F32)
+    group_row = lax.broadcasted_iota(jnp.int32, (GROUP, 1), 0)
+    for step in range(GROUP):
+        parts_ref[step] = jnp.concatenate(
+            [jnp.where(group_row == step, piece, 0.0) for piece in (gain_high, gain_row - gain_high)], axis=0
+        ).astype(BF)
+    logit_col_ref[...] = to_col(jnp.sum((left.astype(F32) + bias) * head, axis=0, keepdims=True))
+    flag_col_ref[...] = to_col(flags_row)
+    lanes = pl.ds(pl.multiple_of(band * width, width), width)
+    weights_ref[...] = jnp.concatenate([wl_ref[:, lanes], wr_ref[:, lanes]], axis=0)
+
+
+def tile_kernel(
+    offset_ref,
+    left_ref,
+    ahead_refs,
+    target_wide,
+    w_both_ref,
+    parts_ref,
+    gain_ref,
+    logit_col_ref,
+    flag_col_ref,
+    head_ref,
+    own_bias_ref,
+    w_in_ref,
+    w_out_ref,
     pred_ref,
     send_ref,
-    target_wide,
     act_ref,
     slope_ref,
     pair_ref,
@@ -91,12 +145,10 @@
     col_ref,
     act_sum_ref,
     sums_ref,
-    logit_col_ref,
-    flag_col_ref,
 ):
     channels, hidden = w_in_ref.shape
-    tile = target_ref.shape[0]
-    noff = bias_ref.shape[0]
+    tile = target_wide.shape[0]
+    noff = len(ahead_refs)
     rows, bands = lax.axis_size("rows"), lax.axis_size("band")
     part = 2 * channels // bands
     here, offset = lax.axis_index("rows"), offset_ref[0, 0]
@@ -107,29 +159,10 @@
     right = piece[:channels]
     col_flags = piece[channels : channels + 1] * (1.0 / (noff * tile))
     left = left_ref[...].astype(F32)
-    off_row = lax.broadcasted_iota(jnp.int32, (noff, channels), 0)
-    bias = to_col(jnp.sum(jnp.where(off_row == offset, bias_ref[...], 0.0), axis=0, keepdims=True))
-    head_row = w_head_ref[...]
-    head = to_col(head_row)
-    w_out_t = w_out_ref[...].astype(F32)
-    gain_row = jnp.sum(w_out_t * head, axis=0, keepdims=True)
-    gain = to_col(gain_row) * 0.5
-    gain_row = gain_row * (0.5 / STRETCH)
-    logit_col_ref[...] = to_col(jnp.sum((left + bias) * head, axis=0, keepdims=True))
+    bias, head, gain = own_bias_ref[...], head_ref[...], gain_ref[...]
     logit_row = jnp.sum(right * head, axis=0, keepdims=True)
-    flag_col_ref[...] = to_col(flags_ref[...].astype(F32))
-    target_wide[...] = target_ref[...].astype(F32)
     shifted = right + bias
-    w_in = w_in_ref[...]
-    w_high, w_low = split(w_in.astype(F32).T * STRETCH)
-    w_both = jnp.concatenate([w_high, w_low], axis=1)
-    gain_high = gain_row.astype(BF).astype(F32)
-    gain_low = gain_row - gain_high
-    group_row = lax.broadcasted_iota(jnp.int32, (GROUP, 1), 0)
-    gain_parts = [
-        jnp.concatenate([jnp.where(group_row == step, piece, 0.0) for piece in (gain_high, gain_low)], axis=0).astype(BF)
-        for step in range(GROUP)
-    ]
+    w_both = w_both_ref[...]
     col_ref[...] = jnp.zeros_like(col_ref)
     act_sum_ref[...] = jnp.zeros_like(act_sum_ref)
     groups = tile // GROUP
@@ -152,7 +185,7 @@
         act = x * lift
         slope_ref[slot, step] = lift + (act * (1.0 - bend)) * (inner + (square + square))
         act_ref[slot, step] = act
-        return logits + mm(gain_parts[step], act.astype(BF))
+        return logits + mm(parts_ref[step], act.astype(BF))
 
     def settle(group, logits):
         at = pl.ds(start_of(group), GROUP)
@@ -208,6 +241,7 @@
     row_part = row_sum * gain
     act_sum = to_row(jnp.sum(act_sum_ref[...], axis=1, keepdims=True) * (0.5 / STRETCH))
     col_part = col_ref[...] * gain
+    w_in, w_out_t = w_in_ref[...], w_out_ref[...].astype(F32)
     row_sums = head * res_row + mm_wide(w_in, row_part)
     col_sums = head * res_col + mm_wide(w_in, col_part)
     left_low, right_low = left_ref[...], right.astype(BF)
@@ -273,14 +307,13 @@
         share_ref[:, pl.ds(pl.multiple_of(index * width, width), width)] = total
 
 
-def finish_kernel(recv_ref, wl_ref, wr_ref, w_head_ref, grad_emb_ref, in_ref, out_ref, head_ref, bias_ref):
-    _, height, width = recv_ref.shape
+def finish_kernel(recv_ref, weights_ref, head_ref_in, pred_near, pred_ref, grad_emb_ref, in_ref, out_ref, head_ref, bias_ref):
+    _, height, _ = recv_ref.shape
     part = height - GROUP
     channels = in_ref.shape[0]
     own = grads_of(recv_ref, lax.axis_index("rows"), part).T.astype(BF)
-    share = pl.ds(pl.multiple_of(lax.axis_index("band") * width, width), width)
-    weights = jnp.concatenate([wl_ref[:, share], wr_ref[:, share]], axis=0)
-    grad_emb_ref[...] = mm(own, weights).astype(BF)
+    grad_emb_ref[...] = mm(own, weights_ref[...]).astype(BF)
+    pred_ref[...] = pred_near[...]
     owners = channels // GROUP + 1
     small = [
         recv_ref[block, part:, :].astype(F32)
@@ -290,7 +323,7 @@
     ]
     in_ref[...] = jnp.concatenate(small[:-1], axis=0)
     last = small[-1]
-    out_ref[...] = last[:1] * to_col(w_head_ref[...])
+    out_ref[...] = last[:1] * head_ref_in[...]
     head_ref[...] = last[1:2, :channels]
     bias_ref[...] = last[2 : 2 + bias_ref.shape[0], :channels]
 
@@ -348,12 +381,53 @@
     noff = dist_bias.shape[1]
     quarter = features // bands
     flags = valid_bins.reshape(1, bins)
-    head_row = w_head.reshape(1, channels)
-
-    left, send, share = call(
+
+    (
+        left,
+        send,
+        share,
+        target_wide,
+        w_both,
+        parts,
+        gain,
+        logit_col,
+        flag_col,
+        head,
+        bias,
+        weights,
+        w_in_near,
+        w_out_near,
+    ) = call(
         project_kernel,
-        [((channels, bins), BF, True), ((channels + GROUP, bins), BF, True), ((rows, bins, quarter), BF, True)],
-        (embedding, w_left.T, w_right.T, flags),
+        [
+            ((channels, bins), BF, True),
+            ((channels + GROUP, bins), BF, True),
+            ((rows, bins, quarter), BF, True),
+            ((tile, tile), F32, True),
+            ((hidden, 2 * channels), BF, True),
+            ((GROUP, 2 * GROUP, hidden), BF, True),
+            ((hidden, 1), F32, True),
+            ((tile, 1), F32, True),
+            ((tile, 1), F32, True),
+            ((channels, 1), F32, True),
+            ((channels, 1), F32, True),
+            ((2 * channels, quarter), BF, True),
+            ((channels, hidden), BF, True),
+            ((channels, hidden), BF, True),
+        ],
+        (
+            offsets,
+            embedding,
+            w_left.T,
+            w_right.T,
+            flags,
+            target.reshape(tile, tile),
+            w_in,
+            w_out.T,
+            w_head.reshape(1, channels),
+            dist_bias.T,
+        ),
+        smem(),
     )
     ahead = [send]
     for step in range(1, noff):
@@ -362,10 +436,23 @@
     predicted, send = call(
         tile_kernel,
         [((tile, tile), BF, True), ((devices, part + GROUP, tile), BF, True)],
-        (offsets, near(left), [near(piece) for piece in ahead], near(flags), near(target.reshape(tile, tile)), near(w_in), near(w_out.T), near(head_row), near(dist_bias.T)),
+        (
+            offsets,
+            near(left),
+            [near(piece) for piece in ahead],
+            near(target_wide),
+            near(w_both),
+            near(parts),
+            near(gain),
+            near(logit_col),
+            near(flag_col),
+            near(head),
+            near(bias),
+            near(w_in_near),
+            near(w_out_near),
+        ),
         smem(),
         [
-            ((tile, tile), F32),
             ((2, GROUP, hidden, tile), F32),
             ((2, GROUP, hidden, tile), F32),
             ((2, GROUP, channels, tile), BF),
@@ -374,29 +461,29 @@
             ((hidden, tile), F32),
             ((hidden, tile), F32),
             ((tile // GROUP, hidden, tile), F32),
-            ((tile, 1), F32),
-            ((tile, 1), F32),
         ],
     )
     send, emb_all = lax.optimization_barrier((send, emb_all))
     emb_far = lax.ppermute(emb_all, "band", [(source, source ^ HALVES) for source in range(bands)])
     partial = exchange(send, ("rows", "band"))
     (send,) = call(functools.partial(total_kernel, owners), [(partial.shape, BF, True)], (near(partial),))
+    send, emb_far = lax.optimization_barrier((send, emb_far))
     complete = exchange(send, ("rows", "band"))
     (mine,) = call(
         share_kernel, [((2 * channels, features // HALVES), F32, True)], (near(complete), near(emb_all), near(emb_far))
     )
     other = lax.ppermute(mine, "band", [(source, source ^ 1) for source in range(bands)])
-    grad_embedding, grad_in, grad_out, grad_head, grad_bias = call(
+    predicted, grad_embedding, grad_in, grad_out, grad_head, grad_bias = call(
         finish_kernel,
         [
+            ((tile, tile), BF, False),
             ((bins, features // bands), BF, False),
             ((channels, hidden), F32, False),
             ((channels, hidden), F32, False),
             ((1, channels), F32, False),
             (dist_bias.shape[::-1], F32, False),
         ],
-        (near(complete), near(w_left.T), near(w_right.T), near(head_row)),
+        (near(complete), near(weights), near(head), near(predicted)),
     )
     grad_left, grad_right = call(arrange_kernel, [((channels, features), F32, False)] * 2, (near(mine), near(other)))
     return (

time: 60.8 us -> 62.3 us (1.025)
  starting transfers between devices: 15.8 us -> 21.9 us
  blocking collectives: 17.1 us -> 13.4 us
  local copies, waits for them, and re-layouts: 1.43 us -> 0 us
    ppermute x1, waiting for transfers between devices: 8.72 us -> 1.55 us  [on_device(): lax.ppermute(emb_all, 'band', [(source, source ^ HALVES) for source in ra...]
    all_to_all x2, waiting for transfers between devices: 0.01 us -> 7.12 us  [exchange(): return lax.all_to_all(value, axes, 0, 0, tiled=True)]
    all_to_all x2, starting transfers between devices: 10.1 us -> 15.7 us  [exchange(): return lax.all_to_all(value, axes, 0, 0, tiled=True)]
    all_to_all x1, blocking collectives: 17.1 us -> 13.4 us  [exchange(): return lax.all_to_all(value, axes, 0, 0, tiled=True)]
    unnamed x17 -> x0, local copies, waits for them, and re-layouts: 1.43 us -> none
  transfers between devices with their start and end apart: 7 -> 7, of which waited for: 4 -> 6; matrix products, arithmetic and copies ran while one was open for 1% -> 0% of each run, Pallas kernels for 15% -> 15%
where the time goes in v6:
time: 62.3 us; the launch traced here: 62 us
  starting transfers between devices  21.9 us (35%)
  blocking collectives  13.4 us (22%)
  waiting for transfers between devices  13 us (21%)
  Pallas kernels  12.4 us (20%)
  between operations  1.33 us (2%)
    all_to_all x2, starting transfers between devices, exchange(): return lax.all_to_all(value, axes, 0, 0, tiled=True)  15.7 us
    all_to_all x1, blocking collectives, exchange(): return lax.all_to_all(value, axes, 0, 0, tiled=True)  13.4 us
    pallas_call x6, Pallas kernels, call(): pl.pallas_call(kernel, out_shape=[pltpu.VMEM(shape, kind) if inner and fi...  12.4 us
    all_to_all x2, waiting for transfers between devices, exchange(): return lax.all_to_all(value, axes, 0, 0, tiled=True)  7.12 us
    ppermute x3, waiting for transfers between devices, on_device(): lax.ppermute(send, 'rows', [(source, source - step) for source in range(s...  4.27 us
    ppermute x3, starting transfers between devices, on_device(): lax.ppermute(send, 'rows', [(source, source - step) for source in range(s...  3.86 us
    ppermute x1, starting transfers between devices, on_device(): lax.ppermute(emb_all, 'band', [(source, source ^ HALVES) for source in ra...  1.83 us
    ppermute x1, waiting for transfers between devices, on_device(): lax.ppermute(emb_all, 'band', [(source, source ^ HALVES) for source in ra...  1.55 us
  transfers between devices with their start and end apart: 7, of which 6 were waited for; matrix products, arithmetic and copies ran while one was open for 0% of the time, Pallas kernels for 15%

profile of v6, /device:TPU:0, one launch (start us, length us, event | category | flops | bytes accessed | tf_op | source)
XLA Modules:
  0.0 62.0 jit_solution(9731677501565812663)
XLA Ops:
  1.3 2.0 %shard_map.161 = (bf16[32,128]{1,0:T(8,128)(2,1)S(1)}, bf16[40,128]{1,0:T(8,128)(2,1)S(1)}, bf16[8,128,128]{2,1,0:T(8,128)(2,1)}, f32[128,128]{1,0:T(8,128)S(1)}...) custom-call(s32[1,1]{1,0:T(1,128)S(6)} %copy.18.offset_ref, ...), custom_call_target="tpu_custom_call" | custom-call | tf_op jit(solution)/shard_map/pallas_call | solution.py:358
  3.2 7.3 %all-to-all-start = ((bf16[8,128,128]{2,1,0:T(8,128)(2,1)}), bf16[8,128,128]{2,1,0:T(8,128)(2,1)S(1)}, u32[]{:S(2)}, u32[]{:S(2)}) async-start(bf16[8,128,128]{2,1,0:T(8,128)(2,1)} %get-tuple-element.49), calls=%async_computation | async-start | bytes 524288 | tf_op jit(solution)/shard_map/all_to_all | solution.py:370
  10.6 1.3 %collective-permute-start.2 = (bf16[40,128]{1,0:T(8,128)(2,1)S(1)}, bf16[40,128]{1,0:T(8,128)(2,1)S(1)}, u32[]{:S(2)}, u32[]{:S(2)}) collective-permute-start(bf16[40,128]{1,0:T(8,128)(2,1)S(1)} %get-tuple-element.37.ahead_refs_0_), channel_id=1, source_target_pairs={{12,0},{16,4},{20,8},{24,12},{28,16},{13,1},{17,5},{21,9},{25,13},... | collective-permute-start | bytes 30728 | tf_op jit(solution)/shard_map/ppermute | solution.py:434
  11.8 1.3 %collective-permute-start.1 = (bf16[40,128]{1,0:T(8,128)(2,1)S(1)}, bf16[40,128]{1,0:T(8,128)(2,1)S(1)}, u32[]{:S(2)}, u32[]{:S(2)}) collective-permute-start(bf16[40,128]{1,0:T(8,128)(2,1)S(1)} %get-tuple-element.37.ahead_refs_0_), channel_id=1, source_target_pairs={{8,0},{12,4},{16,8},{20,12},{24,16},{28,20},{9,1},{13,5},{17,9},{2... | collective-permute-start | bytes 30728 | tf_op jit(solution)/shard_map/ppermute | solution.py:434
  13.1 1.3 %collective-permute-start = (bf16[40,128]{1,0:T(8,128)(2,1)S(1)}, bf16[40,128]{1,0:T(8,128)(2,1)S(1)}, u32[]{:S(2)}, u32[]{:S(2)}) collective-permute-start(bf16[40,128]{1,0:T(8,128)(2,1)S(1)} %get-tuple-element.37.ahead_refs_0_), channel_id=1, source_target_pairs={{4,0},{8,4},{12,8},{16,12},{20,16},{24,20},{28,24},{5,1},{9,5},{13... | collective-permute-start | bytes 30728 | tf_op jit(solution)/shard_map/ppermute | solution.py:434
  14.4 2.8 %collective-permute-done.2.ahead_refs_3_ = bf16[40,128]{1,0:T(8,128)(2,1)S(1)} collective-permute-done((bf16[40,128]{1,0:T(8,128)(2,1)S(1)}, bf16[40,128]{1,0:T(8,128)(2,1)S(1)}, u32[]{:S(2)}, u32[]{:S(2)}) %collective-permute-start.2) | collective-permute-done | bytes 10272 | tf_op jit(solution)/shard_map/ppermute | solution.py:434
  17.2 0.3 collective-permute-done.1.ahead_refs_2_
  17.5 1.2 %collective-permute-done.ahead_refs_1_ = bf16[40,128]{1,0:T(8,128)(2,1)S(1)} collective-permute-done((bf16[40,128]{1,0:T(8,128)(2,1)S(1)}, bf16[40,128]{1,0:T(8,128)(2,1)S(1)}, u32[]{:S(2)}, u32[]{:S(2)}) %collective-permute-start) | collective-permute-done | bytes 10272 | tf_op jit(solution)/shard_map/ppermute | solution.py:434
  18.7 8.6 %shard_map.162 = (bf16[128,128]{1,0:T(8,128)(2,1)S(1)}, bf16[32,24,128]{2,1,0:T(8,128)(2,1)}) custom-call(s32[1,1]{1,0:T(1,128)S(6)} %copy.18.offset_ref, bf16[32,128]{1,0:T(8,128)(2,1)S(1)} %get-tuple-element.36.left_ref, bf16[40,128]{1,0:T(8,128)(2,1)S(1)} %get-tuple-element.37.ahead_refs_0_, bf16[40,128]{1,0:T(8,128)(2,1)S(1)} %collective-permute-done.ahead_refs_1_, ...), custom_call_target="tpu_custom_call" | custom-call | tf_op jit(solution)/shard_map/pallas_call | solution.py:358
  27.3 0.0 all-to-all-done.near_ref
  27.3 8.4 %all-to-all-start.1 = ((bf16[32,24,128]{2,1,0:T(8,128)(2,1)}), bf16[32,24,128]{2,1,0:T(8,128)(2,1)S(1)}, u32[]{:S(2)}, u32[]{:S(2)}) async-start(bf16[32,24,128]{2,1,0:T(8,128)(2,1)} %get-tuple-element.50), calls=%async_computation.1 | async-start | bytes 393216 | tf_op jit(solution)/shard_map/all_to_all | solution.py:370
  35.7 1.8 %collective-permute-start.3 = (bf16[8,128,128]{2,1,0:T(8,128)(2,1)S(1)}, bf16[8,128,128]{2,1,0:T(8,128)(2,1)S(1)}, u32[]{:S(2)}, u32[]{:S(2)}) collective-permute-start(bf16[8,128,128]{2,1,0:T(8,128)(2,1)S(1)} %all-to-all-done.near_ref), channel_id=1, source_target_pairs={{0,2},{1,3},{2,0},{3,1},{4,6},{5,7},{6,4},{7,5},{8,10},{9,11},{10,... | collective-permute-start | bytes 786440 | tf_op jit(solution)/shard_map/ppermute | solution.py:467
  37.5 7.1 %all-to-all-done.1.recv_ref = bf16[32,24,128]{2,1,0:T(8,128)(2,1)S(1)} async-done(((bf16[32,24,128]{2,1,0:T(8,128)(2,1)}), bf16[32,24,128]{2,1,0:T(8,128)(2,1)S(1)}, u32[]{:S(2)}, u32[]{:S(2)}) %all-to-all-start.1) | async-done | bytes 196640 | tf_op jit(solution)/shard_map/all_to_all | solution.py:370
  44.7 1.5 %collective-permute-done.3.far_ref = bf16[8,128,128]{2,1,0:T(8,128)(2,1)S(1)} collective-permute-done((bf16[8,128,128]{2,1,0:T(8,128)(2,1)S(1)}, bf16[8,128,128]{2,1,0:T(8,128)(2,1)S(1)}, u32[]{:S(2)}, u32[]{:S(2)}) %collective-permute-start.3) | collective-permute-done | bytes 262176 | tf_op jit(solution)/shard_map/ppermute | solution.py:467
  46.2 13.4 %all_to_all.15.recv_ref = bf16[32,24,128]{2,1,0:T(8,128)(2,1)S(1)} all-to-all(bf16[32,24,128]{2,1,0:T(8,128)(2,1)S(1)} %shard_map.163), channel_id=1, replica_groups=mesh['rows'=8,'band'=4] {'rows','band'}, dimensions={0} | all-to-all | bytes 393216 | tf_op jit(solution)/shard_map/all_to_all | solution.py:370
  59.6 0.3 shard_map.165.own_ref
  59.9 0.5 collective-permute-start.4
  60.4 0.8 %shard_map.164 = (bf16[128,128]{1,0:T(8,128)(2,1)}, bf16[128,128]{1,0:T(8,128)(2,1)}, f32[32,128]{1,0:T(8,128)}, f32[32,128]{1,0:T(8,128)}, f32[1,32]{1,0:T(1,128)}, /*index=5*/f32[4,32]{1,0:T(4,128)}) custom-call(bf16[32,24,128]{2,1,0:T(8,128)(2,1)S(1)} %all_to_all.15.recv_ref, bf16[64,128]{1,0:T(8,128)(2,1)S(1)} %get-tuple-element.53.weights_ref, ...), custom_call_target="tpu_custom_call" | custom-call | tf_op jit(solution)/shard_map/pallas_call | solution.py:358
  61.3 0.1 collective-permute-done.4.other_ref
  61.3 0.7 %shard_map.166 = (f32[32,512]{1,0:T(8,128)}, f32[32,512]{1,0:T(8,128)}) custom-call(f32[64,256]{1,0:T(8,128)S(1)} %shard_map.165.own_ref, f32[64,256]{1,0:T(8,128)S(1)} %collective-permute-done.4.other_ref), custom_call_target="tpu_custom_call" | custom-call | tf_op jit(solution)/shard_map/pallas_call | solution.py:358
  (1 shorter events, 0.0 us)
Async XLA Ops:
  3.2 24.1 %all-to-all-start = ((bf16[8,128,128]{2,1,0:T(8,128)(2,1)}), bf16[8,128,128]{2,1,0:T(8,128)(2,1)S(1)}, u32[]{:S(2)}, u32[]{:S(2)}) async-start(bf16[8,128,128]{2,1,0:T(8,128)(2,1)} %get-tuple-element.49), calls=%async_computation | async-start | bytes 524288 | tf_op jit(solution)/shard_map/all_to_all | solution.py:370
  10.6 6.7 %collective-permute-start.2 = (bf16[40,128]{1,0:T(8,128)(2,1)S(1)}, bf16[40,128]{1,0:T(8,128)(2,1)S(1)}, u32[]{:S(2)}, u32[]{:S(2)}) collective-permute-start(bf16[40,128]{1,0:T(8,128)(2,1)S(1)} %get-tuple-element.37.ahead_refs_0_), channel_id=1, source_target_pairs={{12,0},{16,4},{20,8},{24,12},{28,16},{13,1},{17,5},{21,9},{25,13},... | collective-permute-start | bytes 30728 | tf_op jit(solution)/shard_map/ppermute | solution.py:434
  11.8 5.7 %collective-permute-start.1 = (bf16[40,128]{1,0:T(8,128)(2,1)S(1)}, bf16[40,128]{1,0:T(8,128)(2,1)S(1)}, u32[]{:S(2)}, u32[]{:S(2)}) collective-permute-start(bf16[40,128]{1,0:T(8,128)(2,1)S(1)} %get-tuple-element.37.ahead_refs_0_), channel_id=1, source_target_pairs={{8,0},{12,4},{16,8},{20,12},{24,16},{28,20},{9,1},{13,5},{17,9},{2... | collective-permute-start | bytes 30728 | tf_op jit(solution)/shard_map/ppermute | solution.py:434
  13.1 5.6 %collective-permute-start = (bf16[40,128]{1,0:T(8,128)(2,1)S(1)}, bf16[40,128]{1,0:T(8,128)(2,1)S(1)}, u32[]{:S(2)}, u32[]{:S(2)}) collective-permute-start(bf16[40,128]{1,0:T(8,128)(2,1)S(1)} %get-tuple-element.37.ahead_refs_0_), channel_id=1, source_target_pairs={{4,0},{8,4},{12,8},{16,12},{20,16},{24,20},{28,24},{5,1},{9,5},{13... | collective-permute-start | bytes 30728 | tf_op jit(solution)/shard_map/ppermute | solution.py:434
  27.3 17.3 %all-to-all-start.1 = ((bf16[32,24,128]{2,1,0:T(8,128)(2,1)}), bf16[32,24,128]{2,1,0:T(8,128)(2,1)S(1)}, u32[]{:S(2)}, u32[]{:S(2)}) async-start(bf16[32,24,128]{2,1,0:T(8,128)(2,1)} %get-tuple-element.50), calls=%async_computation.1 | async-start | bytes 393216 | tf_op jit(solution)/shard_map/all_to_all | solution.py:370
  35.7 10.6 %collective-permute-start.3 = (bf16[8,128,128]{2,1,0:T(8,128)(2,1)S(1)}, bf16[8,128,128]{2,1,0:T(8,128)(2,1)S(1)}, u32[]{:S(2)}, u32[]{:S(2)}) collective-permute-start(bf16[8,128,128]{2,1,0:T(8,128)(2,1)S(1)} %all-to-all-done.near_ref), channel_id=1, source_target_pairs={{0,2},{1,3},{2,0},{3,1},{4,6},{5,7},{6,4},{7,5},{8,10},{9,11},{10,... | collective-permute-start | bytes 786440 | tf_op jit(solution)/shard_map/ppermute | solution.py:467
  59.9 1.4 %collective-permute-start.4 = (f32[64,256]{1,0:T(8,128)S(1)}, f32[64,256]{1,0:T(8,128)S(1)}, u32[]{:S(2)}, u32[]{:S(2)}) collective-permute-start(f32[64,256]{1,0:T(8,128)S(1)} %shard_map.165.own_ref), channel_id=1, source_target_pairs={{0,1},{1,0},{2,3},{3,2},{4,5},{5,4},{6,7},{7,6},{8,9},{9,8},{10,11... | collective-permute-start | bytes 196616 | tf_op jit(solution)/shard_map/ppermute | solution.py:475

commit v7 on v6

--- a/solution.py
+++ b/solution.py
@@ -259,32 +259,47 @@
     small = jnp.concatenate([in_term, jnp.where(first, act_sum, flat[:GROUP])], axis=0)
     small_high = small.astype(BF).astype(F32)
     small_low = small - small_high
-    owners = small.shape[0] // GROUP
+    blocks = small.shape[0] // GROUP
     send_ref[...] = jnp.zeros_like(send_ref)
-    for piece_index in range(3 * owners):
-        source = small_low if piece_index // owners == 1 else small_high
-        block = piece_index % owners
-        send_ref[piece_index, part:, :] = source[block * GROUP : (block + 1) * GROUP].astype(BF)
+    for block in range(blocks):
+        lines = slice(block * GROUP, (block + 1) * GROUP)
+        piece = jnp.concatenate([small_high[lines], small_low[lines]], axis=0)
+        for band in range(2):
+            send_ref[block * bands + band] = piece.astype(BF)
+        send_ref[spare_of(block, blocks, bands)] = jnp.where(here == block, piece, 0.0).astype(BF)
     for quarter in range(bands // 2):
-        send_ref[here * bands + quarter, :part, :] = row_sums[quarter * part : (quarter + 1) * part].astype(BF)
+        send_ref[here * bands + quarter] = row_sums[quarter * part : (quarter + 1) * part].astype(BF)
 
     @pl.when(there < rows)
     def _():
         for quarter in range(bands // 2):
-            send_ref[there * bands + bands // 2 + quarter, :part, :] = col_sums[
-                quarter * part : (quarter + 1) * part
-            ].astype(BF)
-
-
-def total_kernel(owners, recv_ref, send_ref):
-    _, height, width = recv_ref.shape
-    total = jnp.sum(recv_ref[...].astype(F32), axis=0)
-    index = lax.axis_index("rows") * lax.axis_size("band") + lax.axis_index("band")
-    low = total - total.astype(BF).astype(F32)
-    row = lax.broadcasted_iota(jnp.int32, (height, width), 0)
-    third = jnp.logical_and(index >= 2 * owners, index < 3 * owners)
-    use_low = jnp.logical_and(third, row >= height - GROUP)
-    send_ref[...] = jnp.broadcast_to(jnp.where(use_low, low, total).astype(BF)[None], send_ref.shape)
+            send_ref[there * bands + bands // 2 + quarter] = col_sums[quarter * part : (quarter + 1) * part].astype(BF)
+
+
+def spare_of(block, blocks, bands):
+    return (blocks + block // 2) * bands + block % 2
+
+
+def total_kernel(blocks, recv_ref, send_ref):
+    devices, part, width = recv_ref.shape
+    bands = lax.axis_size("band")
+    here, band = lax.axis_index("rows"), lax.axis_index("band")
+
+    def body(row, totals):
+        total = recv_ref[row * bands].astype(F32)
+        for source in range(1, bands):
+            total = total + recv_ref[row * bands + source].astype(F32)
+        mine = jnp.where(row == here, total, 0.0)
+        return totals[0] + mine, totals[1] + (total - mine)
+
+    zero = jnp.zeros((part, width), F32)
+    own, rest = lax.fori_loop(0, devices // bands, body, (zero, zero), unroll=devices // bands <= 8)
+    grads = jnp.where(band < bands // 2, own, own + rest)
+    small = rest[:GROUP] + rest[GROUP:]
+    second = jnp.logical_and(band == 1, here < blocks)
+    small = jnp.where(second, small - small.astype(BF).astype(F32), small)
+    piece = jnp.concatenate([grads, small], axis=0).astype(BF)
+    send_ref[...] = jnp.broadcast_to(piece[None], send_ref.shape)
 
 
 def grads_of(recv_ref, row, part):
@@ -314,12 +329,13 @@
     own = grads_of(recv_ref, lax.axis_index("rows"), part).T.astype(BF)
     grad_emb_ref[...] = mm(own, weights_ref[...]).astype(BF)
     pred_ref[...] = pred_near[...]
-    owners = channels // GROUP + 1
+    blocks = channels // GROUP + 1
+    bands = lax.axis_size("band")
     small = [
-        recv_ref[block, part:, :].astype(F32)
-        + recv_ref[owners + block, part:, :].astype(F32)
-        + recv_ref[2 * owners + block, part:, :].astype(F32)
-        for block in range(owners)
+        recv_ref[block * bands, part:, :].astype(F32)
+        + recv_ref[block * bands + 1, part:, :].astype(F32)
+        + recv_ref[spare_of(block, blocks, bands), part:, :].astype(F32)
+        for block in range(blocks)
     ]
     in_ref[...] = jnp.concatenate(small[:-1], axis=0)
     last = small[-1]
@@ -377,7 +393,7 @@
     channels, hidden = w_in.shape
     tile = target.shape[-1]
     part = 2 * channels // bands
-    owners = channels // GROUP + 1
+    blocks = channels // GROUP + 1
     noff = dist_bias.shape[1]
     quarter = features // bands
     flags = valid_bins.reshape(1, bins)
@@ -435,7 +451,7 @@
     emb_all = exchange(share, "rows")
     predicted, send = call(
         tile_kernel,
-        [((tile, tile), BF, True), ((devices, part + GROUP, tile), BF, True)],
+        [((tile, tile), BF, True), ((devices, part, tile), BF, True)],
         (
             offsets,
             near(left),
@@ -466,7 +482,7 @@
     send, emb_all = lax.optimization_barrier((send, emb_all))
     emb_far = lax.ppermute(emb_all, "band", [(source, source ^ HALVES) for source in range(bands)])
     partial = exchange(send, ("rows", "band"))
-    (send,) = call(functools.partial(total_kernel, owners), [(partial.shape, BF, True)], (near(partial),))
+    (send,) = call(functools.partial(total_kernel, blocks), [((devices, part + GROUP, tile), BF, True)], (near(partial),))
     send, emb_far = lax.optimization_barrier((send, emb_far))
     complete = exchange(send, ("rows", "band"))
     (mine,) = call(

time: 62.3 us -> 57.1 us (0.917)
  blocking collectives: 13.4 us -> 26.1 us
  starting transfers between devices: 21.9 us -> 13.2 us
  waiting for transfers between devices: 13 us -> 4.33 us
  Pallas kernels: 12.4 us -> 11.7 us
    all_to_all x1 -> x2, blocking collectives: 13.4 us -> 26.1 us  [exchange(): return lax.all_to_all(value, axes, 0, 0, tiled=True)]
    all_to_all x2 -> x1, starting transfers between devices: 15.7 us -> 7.31 us  [exchange(): return lax.all_to_all(value, axes, 0, 0, tiled=True)]
    all_to_all x2 -> x1, waiting for transfers between devices: 7.12 us -> 0.01 us  [exchange(): return lax.all_to_all(value, axes, 0, 0, tiled=True)]
    ppermute x1, waiting for transfers between devices: 1.55 us -> 0.01 us  [on_device(): lax.ppermute(emb_all, 'band', [(source, source ^ HALVES) for source in ra...]
    pallas_call x6, Pallas kernels: 12.4 us -> 11.7 us  [call(): pl.pallas_call(kernel, out_shape=[pltpu.VMEM(shape, kind) if inner and fi...]
  transfers between devices with their start and end apart: 7 -> 6, of which waited for: 6 -> 4; matrix products, arithmetic and copies ran while one was open for 0% -> 0% of each run, Pallas kernels for 15% -> 15%
where the time goes in v7:
time: 57.1 us; the launch traced here: 56.7 us
  blocking collectives  26.1 us (46%)
  starting transfers between devices  13.2 us (23%)
  Pallas kernels  11.7 us (20%)
  waiting for transfers between devices  4.33 us (8%)
  between operations  1.33 us (2%)
    all_to_all x2, blocking collectives, exchange(): return lax.all_to_all(value, axes, 0, 0, tiled=True)  26.1 us
    pallas_call x6, Pallas kernels, call(): pl.pallas_call(kernel, out_shape=[pltpu.VMEM(shape, kind) if inner and fi...  11.7 us
    all_to_all x1, starting transfers between devices, exchange(): return lax.all_to_all(value, axes, 0, 0, tiled=True)  7.31 us
    ppermute x3, waiting for transfers between devices, on_device(): lax.ppermute(send, 'rows', [(source, source - step) for source in range(s...  4.27 us
    ppermute x3, starting transfers between devices, on_device(): lax.ppermute(send, 'rows', [(source, source - step) for source in range(s...  3.86 us
    ppermute x1, starting transfers between devices, on_device(): lax.ppermute(emb_all, 'band', [(source, source ^ HALVES) for source in ra...  1.55 us
  transfers between devices with their start and end apart: 6, of which 4 were waited for; matrix products, arithmetic and copies ran while one was open for 0% of the time, Pallas kernels for 15%

profile of v7, /device:TPU:0, one launch (start us, length us, event | category | flops | bytes accessed | tf_op | source)
XLA Modules:
  0.0 56.7 jit_solution(15858820877186790643)
XLA Ops:
  1.3 2.0 %shard_map.161 = (bf16[32,128]{1,0:T(8,128)(2,1)S(1)}, bf16[40,128]{1,0:T(8,128)(2,1)S(1)}, bf16[8,128,128]{2,1,0:T(8,128)(2,1)}, f32[128,128]{1,0:T(8,128)S(1)}...) custom-call(s32[1,1]{1,0:T(1,128)S(6)} %copy.18.offset_ref, ...), custom_call_target="tpu_custom_call" | custom-call | tf_op jit(solution)/shard_map/pallas_call | solution.py:374
  3.2 7.3 %all-to-all-start = ((bf16[8,128,128]{2,1,0:T(8,128)(2,1)}), bf16[8,128,128]{2,1,0:T(8,128)(2,1)S(1)}, u32[]{:S(2)}, u32[]{:S(2)}) async-start(bf16[8,128,128]{2,1,0:T(8,128)(2,1)} %get-tuple-element.49), calls=%async_computation | async-start | bytes 524288 | tf_op jit(solution)/shard_map/all_to_all | solution.py:386
  10.6 1.3 %collective-permute-start.2 = (bf16[40,128]{1,0:T(8,128)(2,1)S(1)}, bf16[40,128]{1,0:T(8,128)(2,1)S(1)}, u32[]{:S(2)}, u32[]{:S(2)}) collective-permute-start(bf16[40,128]{1,0:T(8,128)(2,1)S(1)} %get-tuple-element.37.ahead_refs_0_), channel_id=1, source_target_pairs={{12,0},{16,4},{20,8},{24,12},{28,16},{13,1},{17,5},{21,9},{25,13},... | collective-permute-start | bytes 30728 | tf_op jit(solution)/shard_map/ppermute | solution.py:450
  11.8 1.3 %collective-permute-start.1 = (bf16[40,128]{1,0:T(8,128)(2,1)S(1)}, bf16[40,128]{1,0:T(8,128)(2,1)S(1)}, u32[]{:S(2)}, u32[]{:S(2)}) collective-permute-start(bf16[40,128]{1,0:T(8,128)(2,1)S(1)} %get-tuple-element.37.ahead_refs_0_), channel_id=1, source_target_pairs={{8,0},{12,4},{16,8},{20,12},{24,16},{28,20},{9,1},{13,5},{17,9},{2... | collective-permute-start | bytes 30728 | tf_op jit(solution)/shard_map/ppermute | solution.py:450
  13.1 1.3 %collective-permute-start = (bf16[40,128]{1,0:T(8,128)(2,1)S(1)}, bf16[40,128]{1,0:T(8,128)(2,1)S(1)}, u32[]{:S(2)}, u32[]{:S(2)}) collective-permute-start(bf16[40,128]{1,0:T(8,128)(2,1)S(1)} %get-tuple-element.37.ahead_refs_0_), channel_id=1, source_target_pairs={{4,0},{8,4},{12,8},{16,12},{20,16},{24,20},{28,24},{5,1},{9,5},{13... | collective-permute-start | bytes 30728 | tf_op jit(solution)/shard_map/ppermute | solution.py:450
  14.4 2.8 %collective-permute-done.2.ahead_refs_3_ = bf16[40,128]{1,0:T(8,128)(2,1)S(1)} collective-permute-done((bf16[40,128]{1,0:T(8,128)(2,1)S(1)}, bf16[40,128]{1,0:T(8,128)(2,1)S(1)}, u32[]{:S(2)}, u32[]{:S(2)}) %collective-permute-start.2) | collective-permute-done | bytes 10272 | tf_op jit(solution)/shard_map/ppermute | solution.py:450
  17.2 0.3 collective-permute-done.1.ahead_refs_2_
  17.5 1.2 %collective-permute-done.ahead_refs_1_ = bf16[40,128]{1,0:T(8,128)(2,1)S(1)} collective-permute-done((bf16[40,128]{1,0:T(8,128)(2,1)S(1)}, bf16[40,128]{1,0:T(8,128)(2,1)S(1)}, u32[]{:S(2)}, u32[]{:S(2)}) %collective-permute-start) | collective-permute-done | bytes 10272 | tf_op jit(solution)/shard_map/ppermute | solution.py:450
  18.7 7.9 %shard_map.162 = (bf16[128,128]{1,0:T(8,128)(2,1)S(1)}, bf16[32,16,128]{2,1,0:T(8,128)(2,1)S(1)}) custom-call(s32[1,1]{1,0:T(1,128)S(6)} %copy.18.offset_ref, bf16[32,128]{1,0:T(8,128)(2,1)S(1)} %get-tuple-element.36.left_ref, bf16[40,128]{1,0:T(8,128)(2,1)S(1)} %get-tuple-element.37.ahead_refs_0_, bf16[40,128]{1,0:T(8,128)(2,1)S(1)} %collective-permute-done.ahead_refs_1_, ...), custom_call_target="tpu_custom_call" | custom-call | tf_op jit(solution)/shard_map/pallas_call | solution.py:374
  26.6 0.0 all-to-all-done.near_ref
  26.6 1.6 %collective-permute-start.3 = (bf16[8,128,128]{2,1,0:T(8,128)(2,1)S(1)}, bf16[8,128,128]{2,1,0:T(8,128)(2,1)S(1)}, u32[]{:S(2)}, u32[]{:S(2)}) collective-permute-start(bf16[8,128,128]{2,1,0:T(8,128)(2,1)S(1)} %all-to-all-done.near_ref), channel_id=1, source_target_pairs={{0,2},{1,3},{2,0},{3,1},{4,6},{5,7},{6,4},{7,5},{8,10},{9,11},{10,... | collective-permute-start | bytes 786440 | tf_op jit(solution)/shard_map/ppermute | solution.py:483
  28.2 15.4 %all_to_all.15.recv_ref = bf16[32,16,128]{2,1,0:T(8,128)(2,1)S(1)} all-to-all(bf16[32,16,128]{2,1,0:T(8,128)(2,1)S(1)} %get-tuple-element.50), channel_id=1, replica_groups=mesh['rows'=8,'band'=4] {'rows','band'}, dimensions={0} | all-to-all | bytes 262144 | tf_op jit(solution)/shard_map/all_to_all | solution.py:386
  43.6 0.0 collective-permute-done.3.far_ref
  43.7 10.7 %all_to_all.16.recv_ref = bf16[32,24,128]{2,1,0:T(8,128)(2,1)S(1)} all-to-all(bf16[32,24,128]{2,1,0:T(8,128)(2,1)S(1)} %shard_map.163), channel_id=1, replica_groups=mesh['rows'=8,'band'=4] {'rows','band'}, dimensions={0} | all-to-all | bytes 393216 | tf_op jit(solution)/shard_map/all_to_all | solution.py:386
  54.4 0.3 shard_map.165.own_ref
  54.6 0.5 collective-permute-start.4
  55.2 0.8 %shard_map.164 = (bf16[128,128]{1,0:T(8,128)(2,1)}, bf16[128,128]{1,0:T(8,128)(2,1)}, f32[32,128]{1,0:T(8,128)}, f32[32,128]{1,0:T(8,128)}, f32[1,32]{1,0:T(1,128)}, /*index=5*/f32[4,32]{1,0:T(4,128)}) custom-call(bf16[32,24,128]{2,1,0:T(8,128)(2,1)S(1)} %all_to_all.16.recv_ref, bf16[64,128]{1,0:T(8,128)(2,1)S(1)} %get-tuple-element.53.weights_ref, ...), custom_call_target="tpu_custom_call" | custom-call | tf_op jit(solution)/shard_map/pallas_call | solution.py:374
  56.0 0.1 collective-permute-done.4.other_ref
  56.1 0.7 %shard_map.166 = (f32[32,512]{1,0:T(8,128)}, f32[32,512]{1,0:T(8,128)}) custom-call(f32[64,256]{1,0:T(8,128)S(1)} %shard_map.165.own_ref, f32[64,256]{1,0:T(8,128)S(1)} %collective-permute-done.4.other_ref), custom_call_target="tpu_custom_call" | custom-call | tf_op jit(solution)/shard_map/pallas_call | solution.py:374
  (1 shorter events, 0.0 us)
Async XLA Ops:
  3.2 23.4 %all-to-all-start = ((bf16[8,128,128]{2,1,0:T(8,128)(2,1)}), bf16[8,128,128]{2,1,0:T(8,128)(2,1)S(1)}, u32[]{:S(2)}, u32[]{:S(2)}) async-start(bf16[8,128,128]{2,1,0:T(8,128)(2,1)} %get-tuple-element.49), calls=%async_computation | async-start | bytes 524288 | tf_op jit(solution)/shard_map/all_to_all | solution.py:386
  10.6 6.7 %collective-permute-start.2 = (bf16[40,128]{1,0:T(8,128)(2,1)S(1)}, bf16[40,128]{1,0:T(8,128)(2,1)S(1)}, u32[]{:S(2)}, u32[]{:S(2)}) collective-permute-start(bf16[40,128]{1,0:T(8,128)(2,1)S(1)} %get-tuple-element.37.ahead_refs_0_), channel_id=1, source_target_pairs={{12,0},{16,4},{20,8},{24,12},{28,16},{13,1},{17,5},{21,9},{25,13},... | collective-permute-start | bytes 30728 | tf_op jit(solution)/shard_map/ppermute | solution.py:450
  11.8 5.7 %collective-permute-start.1 = (bf16[40,128]{1,0:T(8,128)(2,1)S(1)}, bf16[40,128]{1,0:T(8,128)(2,1)S(1)}, u32[]{:S(2)}, u32[]{:S(2)}) collective-permute-start(bf16[40,128]{1,0:T(8,128)(2,1)S(1)} %get-tuple-element.37.ahead_refs_0_), channel_id=1, source_target_pairs={{8,0},{12,4},{16,8},{20,12},{24,16},{28,20},{9,1},{13,5},{17,9},{2... | collective-permute-start | bytes 30728 | tf_op jit(solution)/shard_map/ppermute | solution.py:450
  13.1 5.6 %collective-permute-start = (bf16[40,128]{1,0:T(8,128)(2,1)S(1)}, bf16[40,128]{1,0:T(8,128)(2,1)S(1)}, u32[]{:S(2)}, u32[]{:S(2)}) collective-permute-start(bf16[40,128]{1,0:T(8,128)(2,1)S(1)} %get-tuple-element.37.ahead_refs_0_), channel_id=1, source_target_pairs={{4,0},{8,4},{12,8},{16,12},{20,16},{24,20},{28,24},{5,1},{9,5},{13... | collective-permute-start | bytes 30728 | tf_op jit(solution)/shard_map/ppermute | solution.py:450
  26.6 17.0 %collective-permute-start.3 = (bf16[8,128,128]{2,1,0:T(8,128)(2,1)S(1)}, bf16[8,128,128]{2,1,0:T(8,128)(2,1)S(1)}, u32[]{:S(2)}, u32[]{:S(2)}) collective-permute-start(bf16[8,128,128]{2,1,0:T(8,128)(2,1)S(1)} %all-to-all-done.near_ref), channel_id=1, source_target_pairs={{0,2},{1,3},{2,0},{3,1},{4,6},{5,7},{6,4},{7,5},{8,10},{9,11},{10,... | collective-permute-start | bytes 786440 | tf_op jit(solution)/shard_map/ppermute | solution.py:483
  54.6 1.4 %collective-permute-start.4 = (f32[64,256]{1,0:T(8,128)S(1)}, f32[64,256]{1,0:T(8,128)S(1)}, u32[]{:S(2)}, u32[]{:S(2)}) collective-permute-start(f32[64,256]{1,0:T(8,128)S(1)} %shard_map.165.own_ref), channel_id=1, source_target_pairs={{0,1},{1,0},{2,3},{3,2},{4,5},{5,4},{6,7},{7,6},{8,9},{9,8},{10,11... | collective-permute-start | bytes 196616 | tf_op jit(solution)/shard_map/ppermute | solution.py:491
